TPU v7x, 32 devices: a whole 2x2x4 slice. The times are simulated.
32 devices in a mesh: dp: 16 (over z, y, x), tensor: 2 (over core).
Axes of the slice: x: 2, y: 2, z: 4, core: 2. Of those that a mesh axis runs over, the one named last changes fastest.
Arguments:
- tokens_in: bfloat16 [16384, 768], P('dp'), may hold values from -6 to 6
- cotangent: bfloat16 [16384, 768], P('dp'), may hold values from -6 to 6
- seq_lengths: int32 [16, 4], P('dp'), may hold values from 1 to 512, 1024 in all within a row
- q_weight: bfloat16 [768, 768], P(None, 'tensor'), may hold values from -0.4375 to 0.4375
- k_weight: bfloat16 [768, 768], P(None, 'tensor'), may hold values from -0.21875 to 0.21875
- v_weight: bfloat16 [768, 768], P(None, 'tensor'), may hold values from -0.21875 to 0.21875
- q_bias: float32 [768], P('tensor'), may hold values from -3 to 3
- v_bias: float32 [768], P('tensor'), may hold values from -3 to 3
- out_weight: bfloat16 [768, 768], P('tensor'), may hold values from -1 to 1
- out_bias: float32 [768], replicated, may hold values from -3 to 3
- first_gain: float32 [768], replicated, may hold values from 0.5 to 1.5
- first_shift: float32 [768], replicated, may hold values from -2 to 2
- up_weight: bfloat16 [768, 3072], P(None, 'tensor'), may hold values from -0.21875 to 0.21875
- up_bias: float32 [3072], P('tensor'), may hold values from -3 to 3
- down_weight: bfloat16 [3072, 768], P('tensor'), may hold values from -0.15625 to 0.15625
- down_bias: float32 [768], replicated, may hold values from -3 to 3
- second_gain: float32 [768], replicated, may hold values from 0.5 to 1.5
- second_shift: float32 [768], replicated, may hold values from -2 to 2
Outputs:
- layer_out: bfloat16 [16384, 768], P('dp')
- grad_input: bfloat16 [16384, 768], P('dp')
- grad_q_weight: float32 [768, 768], P(None, 'tensor')
- grad_k_weight: float32 [768, 768], P(None, 'tensor')
- grad_v_weight: float32 [768, 768], P(None, 'tensor')
- grad_q_bias: float32 [768], P('tensor')
- grad_v_bias: float32 [768], P('tensor')
- grad_out_weight: float32 [768, 768], P('tensor')
- grad_out_bias: float32 [768], replicated
- grad_first_gain: float32 [768], replicated
- grad_first_shift: float32 [768], replicated
- grad_up_weight: float32 [768, 3072], P(None, 'tensor')
- grad_up_bias: float32 [3072], P('tensor')
- grad_down_weight: float32 [3072, 768], P('tensor')
- grad_down_bias: float32 [768], replicated
- grad_second_gain: float32 [768], replicated
- grad_second_shift: float32 [768], replicated
Inputs may be any that keep to these rules, and one draw needn't show every extreme that they name: Each row of seq_lengths sums to 1024; in every row the longest sequence has exactly 512 tokens.
All inputs are finite; a program needn't handle non-finite values.
Results may differ from a plain program's by a relative error of at most 0.014.
The roundings to bfloat16 on the way count: a program that leaves them out, or rounds other values in their place, can miss the bound.
Values sent between devices are 32-bit elements; how exact they have to be, the bound alone decides.
No kernel may reach another device: no remote copies, remote signals or barrier semaphores. Data moves between devices by JAX's collectives and lax.ppermute only.
A program may use at most 192 MiB of HBM per device.

v0:
```python
import jax
import jax.numpy as jnp
from jax import lax
from jax.sharding import PartitionSpec as P

DH = 64


score_scale = 0.125
norm_eps = 1e-05
far_negative = -1e30


def normalize(values, norm_gain, norm_shift):
    centre = values - jnp.mean(values, axis=-1, keepdims=True)
    spread = jnp.mean(centre * centre, axis=-1, keepdims=True)
    return centre * lax.rsqrt(spread + norm_eps) * norm_gain + norm_shift


def gelu_exact(values):
    return jax.nn.gelu(values, approximate=False)


def contract_rows(left_side, right_side):
    return lax.dot_general(
        left_side, right_side, (((0,), (0,)), ((), ())), preferred_element_type=jnp.float32
    )


def times_transposed(left_side, right_side):
    return lax.dot_general(
        left_side, right_side, (((1,), (1,)), ((), ())), preferred_element_type=jnp.float32
    )


def same_sequence(lengths_row, row_count):
    seq_ends = jnp.cumsum(lengths_row)
    positions = jnp.arange(row_count, dtype=jnp.int32)
    seq_labels = jnp.sum((positions[:, None] >= seq_ends[None, :]).astype(jnp.int32), axis=1)
    return seq_labels[:, None] == seq_labels[None, :]


def masked_scores(queries, key_rows, same_seq):
    scores = (
        jnp.einsum("qhd,khd->hqk", queries, key_rows, preferred_element_type=jnp.float32)
        * score_scale
    )
    return jnp.where(same_seq[None], scores, far_negative)


def local(
    tokens_in,
    cotangent,
    seq_lengths,
    q_weight,
    k_weight,
    v_weight,
    q_bias,
    v_bias,
    out_weight,
    out_bias,
    first_gain,
    first_shift,
    up_weight,
    up_bias,
    down_weight,
    down_bias,
    second_gain,
    second_shift,
):
    row_count = tokens_in.shape[0]
    heads_here = q_weight.shape[1] // DH
    same_seq = same_sequence(seq_lengths[0], row_count)
    queries = (jnp.dot(tokens_in, q_weight, preferred_element_type=jnp.float32) + q_bias).astype(
        jnp.bfloat16
    )
    key_rows = jnp.dot(tokens_in, k_weight, preferred_element_type=jnp.float32).astype(jnp.bfloat16)
    value_rows = (jnp.dot(tokens_in, v_weight, preferred_element_type=jnp.float32) + v_bias).astype(
        jnp.bfloat16
    )
    queries = queries.reshape(row_count, heads_here, DH)
    key_rows = key_rows.reshape(row_count, heads_here, DH)
    value_rows = value_rows.reshape(row_count, heads_here, DH)
    scores = masked_scores(queries, key_rows, same_seq)
    row_peak = jnp.max(scores, axis=-1, keepdims=True)
    exponents = jnp.exp(scores - row_peak)
    row_total = jnp.sum(exponents, axis=-1, keepdims=True)
    log_total = row_peak + jnp.log(row_total)
    probs_low = (exponents / row_total).astype(jnp.bfloat16)
    context = jnp.einsum("hqk,khd->qhd", probs_low, value_rows, preferred_element_type=jnp.float32)
    context = context.astype(jnp.bfloat16).reshape(row_count, heads_here * DH)
    attn_out = lax.psum(jnp.dot(context, out_weight, preferred_element_type=jnp.float32), "tensor")
    first_sum = tokens_in.astype(jnp.float32) + attn_out + out_bias
    first_norm = normalize(first_sum, first_gain, first_shift)
    first_low = first_norm.astype(jnp.bfloat16)
    ffn_inner = jnp.dot(first_low, up_weight, preferred_element_type=jnp.float32) + up_bias
    ffn_active = gelu_exact(ffn_inner).astype(jnp.bfloat16)
    down_out = lax.psum(
        jnp.dot(ffn_active, down_weight, preferred_element_type=jnp.float32), "tensor"
    )
    second_sum = first_norm + down_out + down_bias
    layer_out = normalize(second_sum, second_gain, second_shift).astype(jnp.bfloat16)
    unused, pull_second = jax.vjp(normalize, second_sum, second_gain, second_shift)
    back_second, grad_second_gain, grad_second_shift = pull_second(cotangent.astype(jnp.float32))
    back_down = back_second.astype(jnp.bfloat16)
    grad_down_bias = jnp.sum(back_second, axis=0)
    grad_down_weight = contract_rows(ffn_active, back_down)
    back_active = times_transposed(back_down, down_weight)
    unused_inner, pull_gelu = jax.vjp(gelu_exact, ffn_inner)
    back_inner = pull_gelu(back_active)[0].astype(jnp.bfloat16)
    grad_up_bias = jnp.sum(back_inner.astype(jnp.float32), axis=0)
    grad_up_weight = contract_rows(first_low, back_inner)
    ffn_members = (
        grad_up_weight,
        grad_up_bias,
        grad_down_weight,
        grad_down_bias,
        grad_second_gain,
        grad_second_shift,
    )
    back_first = lax.psum(times_transposed(back_inner, up_weight), "tensor") + back_second
    unused_first, pull_first = jax.vjp(normalize, first_sum, first_gain, first_shift)
    back_first_sum, grad_first_gain, grad_first_shift = pull_first(back_first)
    back_attn = back_first_sum.astype(jnp.bfloat16)
    grad_out_bias = jnp.sum(back_first_sum, axis=0)
    grad_out_weight = contract_rows(context, back_attn)
    back_context = (
        times_transposed(back_attn, out_weight)
        .astype(jnp.bfloat16)
        .reshape(row_count, heads_here, DH)
    )
    probs_exact = jnp.exp(masked_scores(queries, key_rows, same_seq) - log_total)
    probs_again = probs_exact.astype(jnp.bfloat16)
    back_values = jnp.einsum(
        "hqk,qhd->khd", probs_again, back_context, preferred_element_type=jnp.float32
    )
    back_probs = jnp.einsum(
        "qhd,khd->hqk", back_context, value_rows, preferred_element_type=jnp.float32
    )
    row_inner = jnp.sum(back_probs * probs_exact, axis=-1, keepdims=True)
    back_scores = (probs_exact * (back_probs - row_inner) * score_scale).astype(jnp.bfloat16)
    back_queries = jnp.einsum(
        "hqk,khd->qhd", back_scores, key_rows, preferred_element_type=jnp.float32
    )
    back_keys = jnp.einsum("hqk,qhd->khd", back_scores, queries, preferred_element_type=jnp.float32)
    back_queries = back_queries.astype(jnp.bfloat16).reshape(row_count, heads_here * DH)
    back_keys = back_keys.astype(jnp.bfloat16).reshape(row_count, heads_here * DH)
    back_values = back_values.astype(jnp.bfloat16).reshape(row_count, heads_here * DH)
    grad_q_bias = jnp.sum(back_queries.astype(jnp.float32), axis=0)
    grad_v_bias = jnp.sum(back_values.astype(jnp.float32), axis=0)
    grad_q_weight = contract_rows(tokens_in, back_queries)
    grad_k_weight = contract_rows(tokens_in, back_keys)
    grad_v_weight = contract_rows(tokens_in, back_values)
    partial_input = (
        times_transposed(back_queries, q_weight)
        + times_transposed(back_keys, k_weight)
        + times_transposed(back_values, v_weight)
    )
    summed = lax.psum(
        (
            grad_q_weight,
            grad_k_weight,
            grad_v_weight,
            grad_q_bias,
            grad_v_bias,
            grad_out_weight,
            grad_out_bias,
            grad_first_gain,
            grad_first_shift,
            grad_up_weight,
            grad_up_bias,
            grad_down_weight,
            grad_down_bias,
            grad_second_gain,
            grad_second_shift,
        ),
        "dp",
    )
    attn_members = summed[:9]
    ffn_members = summed[9:]
    grad_input = (lax.psum(partial_input, "tensor") + back_first_sum).astype(jnp.bfloat16)
    return (
        layer_out,
        grad_input,
        attn_members[0],
        attn_members[1],
        attn_members[2],
        attn_members[3],
        attn_members[4],
        attn_members[5],
        attn_members[6],
        attn_members[7],
        attn_members[8],
        ffn_members[0],
        ffn_members[1],
        ffn_members[2],
        ffn_members[3],
        ffn_members[4],
        ffn_members[5],
    )


def solution(mesh):
    placed = (
        P("dp", None),
        P("dp", None),
        P("dp", None),
        P(None, "tensor"),
        P(None, "tensor"),
        P(None, "tensor"),
        P("tensor"),
        P("tensor"),
        P("tensor", None),
        P(),
        P(),
        P(),
        P(None, "tensor"),
        P("tensor"),
        P("tensor", None),
        P(),
        P(),
        P(),
    )
    return jax.shard_map(
        local,
        mesh=mesh,
        in_specs=placed,
        out_specs=(
            P("dp", None),
            P("dp", None),
            P(None, "tensor"),
            P(None, "tensor"),
            P(None, "tensor"),
            P("tensor"),
            P("tensor"),
            P("tensor", None),
            P(),
            P(),
            P(),
            P(None, "tensor"),
            P("tensor"),
            P("tensor", None),
            P(),
            P(),
            P(),
        ),
        check_vma=False,
    )
```

profile of v0, /device:TPU:0, one launch (start us, length us, event | category | flops | bytes accessed | tf_op | source)
XLA Modules:
  0.0 739.1 jit_solution(1990451481380839616)
XLA Ops:
  13.6 10.6 %fusion.3 = (f32[6,1024]{1,0:T(8,128)S(1)}, f32[6,1024,1024]{1,2,0:T(8,128)}) fusion(pred[1024,1024]{0,1:T(8,128)(4,1)S(1)} %broadcast_compare_fusion, bf16[1024,6,64]{0,2,1:T(8,128)(2,1)S(1)} %bitcast.68, bf16[1024,6,64]{0,2,1:T(8,128)(2,1)S(1)} %bitcast.66), kind=kOutput, calls=%fused_computation.9 | convolution fusion | flops 824174592 | bytes 27811840 | tf_op jit(solution)/shard_map/qhd,khd->hqk/dot_general | solution.py:45
  24.2 11.3 %fusion.2 = f32[6,1024]{1,0:T(8,128)S(1)} fusion(f32[6,1024,1024]{1,2,0:T(8,128)} %get-tuple-element.88, f32[6,1024]{1,0:T(8,128)S(1)} %get-tuple-element.87, pred[1024,1024]{0,1:T(8,128)(4,1)S(1)} %broadcast_compare_fusion), kind=kLoop, calls=%fused_computation.8 | loop fusion | flops 25159680 | bytes 26263552 | tf_op jit(solution)/shard_map/reduce_sum | solution.py:87
  35.5 12.0 %fusion.53 = bf16[6,64,1024]{2,1,0:T(8,128)(2,1)S(1)} fusion(bf16[1024,6,64]{0,2,1:T(8,128)(2,1)S(1)} %bitcast.70, f32[6,1024,1024]{1,2,0:T(8,128)} %get-tuple-element.88, f32[6,1024]{1,0:T(8,128)S(1)} %fusion.2, f32[6,1024]{1,0:T(8,128)S(1)} %get-tuple-element.87, pred[1024,1024]{0,1:T(8,128)(4,1)S(1)} %broadcast_compare_fusion), kind=kOutput, calls=%fused_computation.80 | convolution fusion | flops 837156864 | bytes 27836416 | tf_op jit(solution)/shard_map/hqk,khd->qhd/dot_general | solution.py:90
  51.6 25.5 %all-reduce.8.cloned.1.call-done = f32[1024,768]{1,0:T(8,128)} async-done(((f32[1024,768]{1,0:T(8,128)}), f32[1024,768]{1,0:T(8,128)}) %all-reduce.8.cloned.1.call-update) | async-done | bytes 3145744 | tf_op jit(solution)/shard_map/psum | solution.py:92
  77.2 2.8 fusion.81
  80.8 17.6 %multiply_convert_fusion.1 = (bf16[1024,1536]{1,0:T(8,128)(2,1)S(1)}, f32[1024,1536]{1,0:T(8,128)}, f32[1024,1536]{1,0:T(8,128)}) fusion(f32[1536]{0:T(1024)S(1)} %copy-done.41, bf16[768,1536]{1,0:T(8,128)(2,1)S(1)} %copy-done, f32[1024,768]{1,0:T(8,128)S(1)} %get-tuple-element.82, f32[768]{0:T(1024)S(1)} %copy-done.38, f32[768]{0:T(1024)S(1)} %copy-done.33, ...), kind=kOutput, calls=%fused_computation.28 | convolution fusion | flops 2523660288 | bytes 21254144 | tf_op jit(solution)/shard_map/dot_general | solution.py:96
  100.1 4.3 fusion.85
  104.5 24.5 %all-reduce.10.cloned.1.call-done = f32[1024,768]{1,0:T(8,128)} async-done(((f32[1024,768]{1,0:T(8,128)}), f32[1024,768]{1,0:T(8,128)}) %all-reduce.10.cloned.1.call-update) | async-done | bytes 3145744 | tf_op jit(solution)/shard_map/psum | solution.py:98
  128.9 4.0 fusion.79
  138.3 8.0 %convert_reduce_fusion = (f32[1536]{0:T(1024)S(1)}, bf16[1024,1536]{1,0:T(8,128)(2,1)S(1)}) fusion(f32[1024,1536]{1,0:T(8,128)S(1)} %bitcast.85, bf16[1536,768]{1,0:T(8,128)(2,1)S(1)} %copy-done.40, f32[1024,768]{1,0:T(8,128)S(1)} %get-tuple-element.76, f32[1024]{0:T(1024)S(1)} %negate_multiply_fusion.2, f32[1024,1536]{1,0:T(8,128)} %get-tuple-element.89, ...), kind=kOutput, calls=%fused_computation.26 | convolution fusion | flops 2444229120 | bytes 21250048 | tf_op jit(solution)/shard_map/dot_general | solution.py:31
  148.0 4.3 fusion.86
  152.6 24.3 %all-reduce.12.cloned.1.call-done = f32[1024,768]{1,0:T(8,128)} async-done(((f32[1024,768]{1,0:T(8,128)}), f32[1024,768]{1,0:T(8,128)}) %all-reduce.12.cloned.1.call-update) | async-done | bytes 3145744 | tf_op jit(solution)/shard_map/psum | solution.py:121
  176.9 4.8 multiply_reduce_fusion.1
  185.8 10.1 %fusion.87 = f32[6,1024,1024]{1,2,0:T(8,128)} fusion(bf16[1024,6,64]{0,2,1:T(8,128)(2,1)S(1)} %bitcast.72, bf16[1024,6,64]{0,2,1:T(8,128)(2,1)S(1)} %bitcast.71), kind=kOutput, calls=%fused_computation.116 | convolution fusion | flops 805306368 | bytes 26738688 | tf_op jit(solution)/shard_map/qhd,khd->hqk/dot_general | solution.py:137
  195.9 12.6 %convert_reduce_fusion.2 = (f32[6,64]{1,0:T(8,128)S(1)}, bf16[6,64,1024]{2,1,0:T(8,128)(2,1)}) fusion(bf16[1024,6,64]{0,2,1:T(8,128)(2,1)S(1)} %bitcast.73, f32[6,1024,1024]{1,2,0:T(8,128)} %get-tuple-element.88, f32[6,1024]{1,0:T(8,128)S(1)} %log_add_fusion, pred[1024,1024]{0,1:T(8,128)(4,1)S(1)} %broadcast_compare_fusion), kind=kOutput, calls=%fused_computation.68 | convolution fusion | flops 831651456 | bytes 27813376 | tf_op jit(solution)/shard_map/hqk,qhd->khd/dot_general | solution.py:134
  208.4 34.5 %fusion.50 = bf16[6,64,1024]{2,1,0:T(8,128)(2,1)S(1)} fusion(bf16[1024,6,64]{0,2,1:T(8,128)(2,1)S(1)} %bitcast.69, f32[6,1024,1024]{1,2,0:T(8,128)} %fusion.87, f32[6,1024,1024]{1,2,0:T(8,128)} %get-tuple-element.88, f32[6,1024]{1,0:T(8,128)S(1)} %log_add_fusion, pred[1024,1024]{0,1:T(8,128)(4,1)S(1)} %broadcast_compare_fusion), kind=kOutput, calls=%fused_computation.76 | convolution fusion | flops 874912768 | bytes 52977664 | tf_op jit(solution)/shard_map/hqk,qhd->khd/dot_general | solution.py:145
  242.9 34.5 %convert_reduce_fusion.3 = (f32[6,64]{1,0:T(8,128)S(1)}, bf16[6,64,1024]{2,1,0:T(8,128)(2,1)S(1)}) fusion(bf16[1024,6,64]{0,2,1:T(8,128)(2,1)S(1)} %bitcast.67, f32[6,1024,1024]{1,2,0:T(8,128)} %fusion.87, f32[6,1024,1024]{1,2,0:T(8,128)} %get-tuple-element.88, f32[6,1024]{1,0:T(8,128)S(1)} %log_add_fusion, pred[1024,1024]{0,1:T(8,128)(4,1)S(1)} %broadcast_compare_fusion), kind=kOutput, calls=%fused_computation.69 | convolution fusion | flops 875698816 | bytes 52979200 | tf_op jit(solution)/shard_map/hqk,khd->qhd/dot_general | solution.py:142
  284.0 8.4 %fusion.70 = f32[1536,768]{1,0:T(8,128)} fusion(bf16[1024,1536]{1,0:T(8,128)(2,1)} %copy-done.44, f32[1024,768]{1,0:T(8,128)} %copy-done.7, f32[1024]{0:T(1024)S(1)} %negate_multiply_fusion.2), kind=kOutput, calls=%fused_computation.104 | convolution fusion | flops 2417491968 | bytes 11014144 | tf_op jit(solution)/shard_map/dot_general | solution.py:25
  292.4 4.9 fusion.73
  305.6 2.9 all-reduce.14.cloned.1.call-done
  308.5 4.4 add_reduce_fusion
  312.9 81.8 %all-reduce = (f32[384]{0:T(512)}, f32[384]{0:T(512)}, f32[768]{0:T(1024)}, f32[768]{0:T(1024)}, f32[768]{0:T(1024)}, /*index=5*/f32[1536]{0:T(1024)}, f32[768]{0:T(1024)}, f32[768]{0:T(1024)}, f32[768]{0:T(1024)}) all-reduce(f32[384]{0:T(512)S(1)} %reduce_sum.203, ...), channel_id=1, replica_groups=mesh['dp'=16,'tensor'=2] {'dp'}, use_global_device_ids=true, to_apply=%region_21.22 | all-reduce | flops 6912 | bytes 55296 | tf_op jit(solution)/shard_map/psum | solution.py:159
  394.6 323.1 %all-reduce.16.cloned.1.call-done = (f32[768,384]{0,1:T(8,128)}, f32[768,384]{0,1:T(8,128)}, f32[768,384]{0,1:T(8,128)}, f32[384,768]{1,0:T(8,128)}, f32[768,1536]{1,0:T(8,128)}, /*index=5*/f32[1536,768]{1,0:T(8,128)}) async-done(((f32[768,384]{0,1:T(8,128)}, f32[768,384]{0,1:T(8,128)}, f32[768,384]{0,1:T(8,128)}, f32[384,768]{1,0:T(8,128)}, f32[768,1536]{1,0:T(8,128)}, /*index=5*/f32[1536,768]{1,0:T(8,128)}), ...) | async-done | bytes 14155792 | tf_op jit(solution)/shard_map/psum | solution.py:159
  724.4 5.5 copy.64
  (150 shorter events, 47.7 us)
Async XLA Ops:
  7.2 73.4 %copy-start = (bf16[768,1536]{1,0:T(8,128)(2,1)S(1)}, bf16[768,1536]{1,0:T(8,128)(2,1)}, u32[]{:S(2)}) copy-start(bf16[768,1536]{1,0:T(8,128)(2,1)} %param.30) | copy-start | bytes 7077892
  7.2 70.0 %all-reduce.8.cloned.1.call-start = ((), (), s32[]{:S(2)}) async-start(), calls=%async_computation | async-start | bytes 6291456 | tf_op jit(solution)/shard_map/psum | solution.py:92
  12.8 11.4 %copy-start.11 = (bf16[1024,384]{0,1:T(8,128)(2,1)}, bf16[1024,384]{0,1:T(8,128)(2,1)S(1)}, u32[]{:S(2)}) copy-start(bf16[1024,384]{0,1:T(8,128)(2,1)S(1)} %add_convert_fusion.5) | copy-start | bytes 2359300
  13.6 21.9 %copy-start.15 = (bf16[1024,384]{0,1:T(8,128)(2,1)}, bf16[1024,384]{0,1:T(8,128)(2,1)S(1)}, u32[]{:S(2)}) copy-start(bf16[1024,384]{0,1:T(8,128)(2,1)S(1)} %add_convert_fusion.6) | copy-start | bytes 2359300
  35.5 12.9 %copy-start.27 = (bf16[384,768]{1,0:T(8,128)(2,1)S(1)}, bf16[384,768]{1,0:T(8,128)(2,1)}, u32[]{:S(2)}) copy-start(bf16[384,768]{1,0:T(8,128)(2,1)} %param.26) | copy-start | bytes 1769476
  48.4 28.8 %copy-start.35 = (f32[768]{0:T(1024)S(1)}, f32[768]{0:T(1024)}, u32[]{:S(2)}) copy-start(f32[768]{0:T(1024)} %param.27) | copy-start | bytes 9220
  51.1 77.8 %all-reduce.10.cloned.1.call-start = ((), (), s32[]{:S(2)}) async-start(), calls=%async_computation.1 | async-start | bytes 6291456 | tf_op jit(solution)/shard_map/psum | solution.py:98
  80.0 18.4 %copy-start.2 = (f32[1024,768]{1,0:T(8,128)}, f32[1024,768]{1,0:T(8,128)S(1)}, u32[]{:S(2)}) copy-start(f32[1024,768]{1,0:T(8,128)S(1)} %get-tuple-element.82) | copy-start | bytes 9437188
  80.8 19.3 %copy-start.39 = (bf16[1536,768]{1,0:T(8,128)(2,1)S(1)}, bf16[1536,768]{1,0:T(8,128)(2,1)}, u32[]{:S(2)}) copy-start(bf16[1536,768]{1,0:T(8,128)(2,1)} %param.32) | copy-start | bytes 7077892
  104.4 24.6 %copy-start.36 = (f32[768]{0:T(1024)S(1)}, f32[768]{0:T(1024)}, u32[]{:S(2)}) copy-start(f32[768]{0:T(1024)} %param.33) | copy-start | bytes 9220
  104.4 72.5 %all-reduce.12.cloned.1.call-start = ((), (), s32[]{:S(2)}) async-start(), calls=%async_computation.2 | async-start | bytes 6291456 | tf_op jit(solution)/shard_map/psum | solution.py:121
  128.9 9.4 %slice-start.2 = ((s8[6291456]{0:T(1024)(128)(4,1)}), s8[4194304]{0:T(1024)(128)(4,1)S(1)}, s32[]{:S(2)}) async-start(s8[6291456]{0:T(1024)(128)(4,1)} %bitcast.84), calls=%async_computation.7 | async-start | bytes 8388608
  138.3 8.0 %copy-start.7 = (f32[1024,768]{1,0:T(8,128)}, f32[1024,768]{1,0:T(8,128)S(1)}, u32[]{:S(2)}) copy-start(f32[1024,768]{1,0:T(8,128)S(1)} %get-tuple-element.76) | copy-start | bytes 9437188
  152.3 156.1 %all-reduce.14.cloned.1.call-start = ((), (), s32[]{:S(2)}) async-start(), calls=%async_computation.3 | async-start | bytes 6291456 | tf_op jit(solution)/shard_map/psum | solution.py:181
  195.8 12.6 %copy-start.12 = (bf16[1024,384]{0,1:T(8,128)(2,1)S(1)}, bf16[1024,384]{0,1:T(8,128)(2,1)}, u32[]{:S(2)}) copy-start(bf16[1024,384]{0,1:T(8,128)(2,1)} %copy-done.11) | copy-start | bytes 2359300
  208.4 34.5 %copy-start.10 = (bf16[1024,384]{0,1:T(8,128)(2,1)S(1)}, bf16[1024,384]{0,1:T(8,128)(2,1)}, u32[]{:S(2)}) copy-start(bf16[1024,384]{0,1:T(8,128)(2,1)} %copy-done.9) | copy-start | bytes 2359300
  242.9 34.6 %copy-start.22 = (bf16[6,64,1024]{2,1,0:T(8,128)(2,1)}, bf16[6,64,1024]{2,1,0:T(8,128)(2,1)S(1)}, u32[]{:S(2)}) copy-start(bf16[6,64,1024]{2,1,0:T(8,128)(2,1)S(1)} %fusion.50) | copy-start | bytes 2359300
  283.9 433.9 %all-reduce.16.cloned.1.call-start = ((), (), s32[]{:S(2)}) async-start(), calls=%async_computation.4 | async-start | bytes 28311552 | tf_op jit(solution)/shard_map/psum | solution.py:159
  284.0 8.4 %copy-start.4 = (f32[1024,768]{1,0:T(8,128)S(1)}, f32[1024,768]{1,0:T(8,128)}, u32[]{:S(2)}) copy-start(f32[1024,768]{1,0:T(8,128)} %copy-done.2) | copy-start | bytes 9437188
  284.0 8.4 %copy-start.46 = (bf16[1024,1536]{1,0:T(8,128)(2,1)S(1)}, bf16[1024,1536]{1,0:T(8,128)(2,1)}, u32[]{:S(2)}) copy-start(bf16[1024,1536]{1,0:T(8,128)(2,1)} %copy-done.45) | copy-start | bytes 9437188
  717.8 5.6 copy-start.17
  723.4 6.5 slice-start
  724.4 5.5 slice-start.1
  724.4 7.7 %copy-start.1 = (bf16[768,1536]{1,0:T(8,128)(2,1)S(1)}, bf16[768,1536]{1,0:T(8,128)(2,1)}, u32[]{:S(2)}) copy-start(bf16[768,1536]{1,0:T(8,128)(2,1)} %param.30) | copy-start | bytes 7077892
  (32 other events, 74.3 us)
Sparse Core Ops, SparseCore 0:
  51.2 25.8 all-reduce.7
  104.5 24.3 all-reduce.9
  152.4 24.3 all-reduce.11
  284.0 24.3 all-reduce.13
  315.9 401.8 all-reduce.15
where the time goes:
time: 747 us; the launch traced here: 739 us
  waiting for transfers between devices  400 us (54%)
  matrix products  183 us (24%)
  blocking collectives  81.8 us (11%)
  other arithmetic  35.5 us (5%)
  local copies, waits for them, and re-layouts  23.1 us (3%)
  between operations  14.8 us (2%)
    psum x1, waiting for transfers between devices, local(): lax.psum((grad_q_weight, grad_k_weight, grad_v_weight, grad_q_bias, grad_...  323 us
    psum x1, blocking collectives, local(): lax.psum((grad_q_weight, grad_k_weight, grad_v_weight, grad_q_bias, grad_...  81.8 us
    dot_general x1, matrix products, local(): jnp.einsum('hqk,khd->qhd', back_scores, key_rows, preferred_element_type=...  34.5 us
    dot_general x1, matrix products, local(): jnp.einsum('hqk,qhd->khd', back_scores, queries, preferred_element_type=j...  34.5 us
    psum x1, waiting for transfers between devices, local(): lax.psum(jnp.dot(context, out_weight, preferred_element_type=jnp.float32)...  25.5 us
    psum x1, waiting for transfers between devices, local(): lax.psum(jnp.dot(ffn_active, down_weight, preferred_element_type=jnp.floa...  24.5 us
    psum x1, waiting for transfers between devices, local(): lax.psum(times_transposed(back_inner, up_weight), 'tensor') + back_second  24.3 us
    unnamed x108, local copies, waits for them, and re-layouts  22.9 us
  transfers between devices with their start and end apart: 5, of which 5 were waited for; matrix products, arithmetic and copies ran while one was open for 3% of the time, Pallas kernels for 0%

commit v1 on v0

--- a/solution.py
+++ b/solution.py
@@ -34,9 +34,12 @@
 
 
 def same_sequence(lengths_row, row_count):
-    seq_ends = jnp.cumsum(lengths_row)
     positions = jnp.arange(row_count, dtype=jnp.int32)
-    seq_labels = jnp.sum((positions[:, None] >= seq_ends[None, :]).astype(jnp.int32), axis=1)
+    seq_labels = jnp.zeros((row_count,), jnp.int32)
+    seq_end = jnp.int32(0)
+    for at in range(lengths_row.shape[0]):
+        seq_end = seq_end + lengths_row[at]
+        seq_labels = seq_labels + (positions >= seq_end).astype(jnp.int32)
     return seq_labels[:, None] == seq_labels[None, :]
 
 
@@ -48,7 +51,66 @@
     return jnp.where(same_seq[None], scores, far_negative)
 
 
+def pair_sum(value, tensor_count):
+    if tensor_count == 1:
+        return value
+    if tensor_count != 2:
+        return lax.psum(value, "tensor")
+    return value + lax.ppermute(value, "tensor", [(0, 1), (1, 0)])
+
+
+def swap_bit(value, bit, count):
+    return lax.ppermute(value, "dp", [(i, i ^ (1 << bit)) for i in range(count)])
+
+
+def halve(value, bit, count, place):
+    rows = value.shape[0] // 2
+    mine = (place >> bit) & 1
+    sent = lax.dynamic_slice_in_dim(value, (1 - mine) * rows, rows, 0)
+    kept = lax.dynamic_slice_in_dim(value, mine * rows, rows, 0)
+    return kept + swap_bit(sent, bit, count)
+
+
+def join(value, bit, count, place):
+    other = swap_bit(value, bit, count)
+    mine = (place >> bit) & 1
+    first = jnp.where(mine == 0, value, other)
+    second = jnp.where(mine == 0, other, value)
+    return jnp.concatenate([first, second], axis=0)
+
+
+def line_sum(value, count, place):
+    stride = count // 4
+    inward = []
+    across = []
+    outward = []
+    for low in range(stride):
+        ring = [low + stride * at for at in range(4)]
+        inward += [(ring[0], ring[1]), (ring[3], ring[2])]
+        across += [(ring[1], ring[2]), (ring[2], ring[1])]
+        outward += [(ring[1], ring[0]), (ring[2], ring[3])]
+    at_line = place // stride
+    value = value + lax.ppermute(value, "dp", inward)
+    value = value + lax.ppermute(value, "dp", across)
+    ended = lax.ppermute(value, "dp", outward)
+    return jnp.where((at_line == 1) | (at_line == 2), value, ended)
+
+
+def all_sum(value, first_bit, count, place):
+    second_bit = 1 - first_bit
+    value = halve(value, first_bit, count, place)
+    value = halve(value, second_bit, count, place)
+    low_bits = (count // 4).bit_length() - 1
+    for bit in range(2, low_bits):
+        value = value + swap_bit(value, bit, count)
+    value = line_sum(value, count, place)
+    value = join(value, second_bit, count, place)
+    return join(value, first_bit, count, place)
+
+
 def local(
+    dp_count,
+    tensor_count,
     tokens_in,
     cotangent,
     seq_lengths,
@@ -68,8 +130,12 @@
     second_gain,
     second_shift,
 ):
+    place = lax.axis_index("dp")
     row_count = tokens_in.shape[0]
-    heads_here = q_weight.shape[1] // DH
+    width = q_weight.shape[1]
+    model = q_weight.shape[0]
+    hidden = up_weight.shape[1]
+    heads_here = width // DH
     same_seq = same_sequence(seq_lengths[0], row_count)
     queries = (jnp.dot(tokens_in, q_weight, preferred_element_type=jnp.float32) + q_bias).astype(
         jnp.bfloat16
@@ -89,14 +155,16 @@
     probs_low = (exponents / row_total).astype(jnp.bfloat16)
     context = jnp.einsum("hqk,khd->qhd", probs_low, value_rows, preferred_element_type=jnp.float32)
     context = context.astype(jnp.bfloat16).reshape(row_count, heads_here * DH)
-    attn_out = lax.psum(jnp.dot(context, out_weight, preferred_element_type=jnp.float32), "tensor")
+    attn_out = pair_sum(
+        jnp.dot(context, out_weight, preferred_element_type=jnp.float32), tensor_count
+    )
     first_sum = tokens_in.astype(jnp.float32) + attn_out + out_bias
     first_norm = normalize(first_sum, first_gain, first_shift)
     first_low = first_norm.astype(jnp.bfloat16)
     ffn_inner = jnp.dot(first_low, up_weight, preferred_element_type=jnp.float32) + up_bias
     ffn_active = gelu_exact(ffn_inner).astype(jnp.bfloat16)
-    down_out = lax.psum(
-        jnp.dot(ffn_active, down_weight, preferred_element_type=jnp.float32), "tensor"
+    down_out = pair_sum(
+        jnp.dot(ffn_active, down_weight, preferred_element_type=jnp.float32), tensor_count
     )
     second_sum = first_norm + down_out + down_bias
     layer_out = normalize(second_sum, second_gain, second_shift).astype(jnp.bfloat16)
@@ -104,26 +172,25 @@
     back_second, grad_second_gain, grad_second_shift = pull_second(cotangent.astype(jnp.float32))
     back_down = back_second.astype(jnp.bfloat16)
     grad_down_bias = jnp.sum(back_second, axis=0)
-    grad_down_weight = contract_rows(ffn_active, back_down)
+    half = hidden // 2
+    down_sums = [
+        all_sum(contract_rows(ffn_active[:, at : at + half], back_down), bit, dp_count, place)
+        for bit, at in enumerate((0, half))
+    ]
     back_active = times_transposed(back_down, down_weight)
     unused_inner, pull_gelu = jax.vjp(gelu_exact, ffn_inner)
     back_inner = pull_gelu(back_active)[0].astype(jnp.bfloat16)
     grad_up_bias = jnp.sum(back_inner.astype(jnp.float32), axis=0)
-    grad_up_weight = contract_rows(first_low, back_inner)
-    ffn_members = (
-        grad_up_weight,
-        grad_up_bias,
-        grad_down_weight,
-        grad_down_bias,
-        grad_second_gain,
-        grad_second_shift,
-    )
-    back_first = lax.psum(times_transposed(back_inner, up_weight), "tensor") + back_second
+    up_sums = [
+        all_sum(contract_rows(first_low, back_inner[:, at : at + half]), bit, dp_count, place)
+        for bit, at in enumerate((0, half))
+    ]
+    back_first = pair_sum(times_transposed(back_inner, up_weight), tensor_count) + back_second
     unused_first, pull_first = jax.vjp(normalize, first_sum, first_gain, first_shift)
     back_first_sum, grad_first_gain, grad_first_shift = pull_first(back_first)
     back_attn = back_first_sum.astype(jnp.bfloat16)
     grad_out_bias = jnp.sum(back_first_sum, axis=0)
-    grad_out_weight = contract_rows(context, back_attn)
+    grad_out_turned = contract_rows(back_attn, context)
     back_context = (
         times_transposed(back_attn, out_weight)
         .astype(jnp.bfloat16)
@@ -148,55 +215,61 @@
     back_values = back_values.astype(jnp.bfloat16).reshape(row_count, heads_here * DH)
     grad_q_bias = jnp.sum(back_queries.astype(jnp.float32), axis=0)
     grad_v_bias = jnp.sum(back_values.astype(jnp.float32), axis=0)
-    grad_q_weight = contract_rows(tokens_in, back_queries)
-    grad_k_weight = contract_rows(tokens_in, back_keys)
-    grad_v_weight = contract_rows(tokens_in, back_values)
+    small = [
+        grad_q_bias,
+        grad_v_bias,
+        grad_up_bias,
+        grad_out_bias,
+        grad_first_gain,
+        grad_first_shift,
+        grad_down_bias,
+        grad_second_gain,
+        grad_second_shift,
+    ]
+    sizes = [member.shape[0] for member in small]
+    small_rows = -(-sum(sizes) // (32 * model)) * 32
+    packed = jnp.concatenate(small + [jnp.zeros((small_rows * model - sum(sizes),), jnp.float32)])
+    first_pack = jnp.concatenate(
+        [contract_rows(tokens_in, back_queries), contract_rows(tokens_in, back_keys)], axis=1
+    )
+    second_pack = jnp.concatenate(
+        [contract_rows(tokens_in, back_values), grad_out_turned], axis=1
+    )
+    second_pack = jnp.concatenate(
+        [second_pack, packed.reshape(small_rows, model)], axis=0
+    )
+    first_pack = all_sum(first_pack, 0, dp_count, place)
+    second_pack = all_sum(second_pack, 1, dp_count, place)
     partial_input = (
         times_transposed(back_queries, q_weight)
         + times_transposed(back_keys, k_weight)
         + times_transposed(back_values, v_weight)
     )
-    summed = lax.psum(
-        (
-            grad_q_weight,
-            grad_k_weight,
-            grad_v_weight,
-            grad_q_bias,
-            grad_v_bias,
-            grad_out_weight,
-            grad_out_bias,
-            grad_first_gain,
-            grad_first_shift,
-            grad_up_weight,
-            grad_up_bias,
-            grad_down_weight,
-            grad_down_bias,
-            grad_second_gain,
-            grad_second_shift,
-        ),
-        "dp",
-    )
-    attn_members = summed[:9]
-    ffn_members = summed[9:]
-    grad_input = (lax.psum(partial_input, "tensor") + back_first_sum).astype(jnp.bfloat16)
+    grad_input = (pair_sum(partial_input, tensor_count) + back_first_sum).astype(jnp.bfloat16)
+    flat = second_pack[model:].reshape(-1)
+    sums = []
+    start = 0
+    for size in sizes:
+        sums.append(flat[start : start + size])
+        start += size
     return (
         layer_out,
         grad_input,
-        attn_members[0],
-        attn_members[1],
-        attn_members[2],
-        attn_members[3],
-        attn_members[4],
-        attn_members[5],
-        attn_members[6],
-        attn_members[7],
-        attn_members[8],
-        ffn_members[0],
-        ffn_members[1],
-        ffn_members[2],
-        ffn_members[3],
-        ffn_members[4],
-        ffn_members[5],
+        first_pack[:, :width],
+        first_pack[:, width:],
+        second_pack[:model, :width],
+        sums[0],
+        sums[1],
+        second_pack[:model, width:].T,
+        sums[3],
+        sums[4],
+        sums[5],
+        jnp.concatenate(up_sums, axis=1),
+        sums[2],
+        jnp.concatenate(down_sums, axis=0),
+        sums[6],
+        sums[7],
+        sums[8],
     )
 
 
@@ -221,8 +294,13 @@
         P(),
         P(),
     )
+    counts = (mesh.shape["dp"], mesh.shape["tensor"])
+
+    def on_device(*args):
+        return local(*counts, *args)
+
     return jax.shard_map(
-        local,
+        on_device,
         mesh=mesh,
         in_specs=placed,
         out_specs=(

time: 747 us -> 571 us (0.76)
  waiting for transfers between devices: 400 us -> 161 us
  starting transfers between devices: 0.84 us -> 94.7 us
  blocking collectives: 81.8 us -> 0 us
  other arithmetic: 35.5 us -> 89.7 us
  between operations: 14.8 us -> 4.92 us
    psum x5 -> x0, waiting for transfers between devices: 400 us -> none  [the longest x1 323 us: local(): lax.psum((grad_q_weight, grad_k_weight, grad_v_weight, grad_q_bias, grad_...]
    ppermute x0 -> x46, waiting for transfers between devices: none -> 161 us  [the longest x24 110 us: swap_bit(): return lax.ppermute(value, 'dp', [(i, i ^ 1 << bit) for i in range(count)])]
    ppermute x0 -> x46, starting transfers between devices: none -> 94.7 us  [the longest x6 46.5 us: line_sum(): value = value + lax.ppermute(value, 'dp', inward)]
    psum x1 -> x0, blocking collectives: 81.8 us -> none  [local(): lax.psum((grad_q_weight, grad_k_weight, grad_v_weight, grad_q_bias, grad_...]
    add x0 -> x25, other arithmetic: none -> 24.6 us  [the longest x12 8.21 us: halve(): return kept + swap_bit(sent, bit, count)]
    select_n x0 -> x18, other arithmetic: none -> 15.6 us  [the longest x11 7.6 us: join(): first = jnp.where(mine == 0, value, other)]
    concatenate x0 -> x11, other arithmetic: none -> 14.4 us  [the longest x7 6.26 us: join(): return jnp.concatenate([first, second], axis=0)]
    dot_general x6 -> x8, matrix products: 20.6 us -> 16.5 us  [contract_rows(): lax.dot_general(left_side, right_side, (((0,), (0,)), ((), ())), preferre...]
  transfers between devices with their start and end apart: 5 -> 46, of which waited for: 5 -> 21; matrix products, arithmetic and copies ran while one was open for 3% -> 36% of each run, Pallas kernels for 0% -> 0%
where the time goes in v1:
time: 571 us; the launch traced here: 560 us
  matrix products  182 us (32%)
  waiting for transfers between devices  161 us (28%)
  starting transfers between devices  94.7 us (17%)
  other arithmetic  89.7 us (16%)
  local copies, waits for them, and re-layouts  28.7 us (5%)
    ppermute x24, waiting for transfers between devices, swap_bit(): return lax.ppermute(value, 'dp', [(i, i ^ 1 << bit) for i in range(count)])  110 us
    ppermute x6, starting transfers between devices, line_sum(): value = value + lax.ppermute(value, 'dp', inward)  46.5 us
    dot_general x1, matrix products, local(): jnp.einsum('hqk,khd->qhd', back_scores, key_rows, preferred_element_type=...  35.8 us
    dot_general x1, matrix products, local(): jnp.einsum('hqk,qhd->khd', back_scores, queries, preferred_element_type=j...  35.5 us
    ppermute x24, starting transfers between devices, swap_bit(): return lax.ppermute(value, 'dp', [(i, i ^ 1 << bit) for i in range(count)])  31.4 us
    ppermute x6, waiting for transfers between devices, line_sum(): ended = lax.ppermute(value, 'dp', outward)  27.9 us
    unnamed x130, local copies, waits for them, and re-layouts  20.7 us
    dot_general x1, matrix products, local(): jnp.dot(first_low, up_weight, preferred_element_type=jnp.float32) + up_bias  18.9 us
  transfers between devices with their start and end apart: 46, of which 21 were waited for; matrix products, arithmetic and copies ran while one was open for 36% of the time, Pallas kernels for 0%

profile of v1, /device:TPU:0, one launch (start us, length us, event | category | flops | bytes accessed | tf_op | source)
XLA Modules:
  0.0 560.4 jit_solution(11086967104568502519)
XLA Ops:
  9.5 10.6 %fusion.3 = (f32[6,1024]{1,0:T(8,128)S(1)}, f32[6,1024,1024]{1,2,0:T(8,128)}) fusion(pred[1024,1024]{0,1:T(8,128)(4,1)S(1)} %broadcast_compare_fusion, bf16[1024,6,64]{0,2,1:T(8,128)(2,1)S(1)} %bitcast.74, bf16[1024,6,64]{0,2,1:T(8,128)(2,1)S(1)} %bitcast.76), kind=kOutput, calls=%fused_computation.9 | convolution fusion | flops 824174592 | bytes 27811840 | tf_op jit(solution)/shard_map/qhd,khd->hqk/dot_general | solution.py:48
  20.1 11.3 %fusion.2 = f32[6,1024]{1,0:T(8,128)S(1)} fusion(f32[6,1024,1024]{1,2,0:T(8,128)} %get-tuple-element.154, f32[6,1024]{1,0:T(8,128)S(1)} %get-tuple-element.153, pred[1024,1024]{0,1:T(8,128)(4,1)S(1)} %broadcast_compare_fusion), kind=kLoop, calls=%fused_computation.8 | loop fusion | flops 25159680 | bytes 26263552 | tf_op jit(solution)/shard_map/reduce_sum | solution.py:153
  32.3 12.3 %fusion.61 = bf16[6,64,1024]{2,1,0:T(8,128)(2,1)S(1)} fusion(bf16[1024,6,64]{0,2,1:T(8,128)(2,1)S(1)} %bitcast.78, f32[6,1024,1024]{1,2,0:T(8,128)} %get-tuple-element.154, f32[6,1024]{1,0:T(8,128)S(1)} %fusion.2, f32[6,1024]{1,0:T(8,128)S(1)} %get-tuple-element.153, pred[1024,1024]{0,1:T(8,128)(4,1)S(1)} %broadcast_compare_fusion), kind=kOutput, calls=%fused_computation.97 | convolution fusion | flops 837156864 | bytes 27836416 | tf_op jit(solution)/shard_map/hqk,khd->qhd/dot_general | solution.py:156
  58.9 18.9 %multiply_convert_fusion.1 = (bf16[1024,1536]{1,0:T(8,128)(2,1)S(1)}, f32[1024,1536]{1,0:T(8,128)}, f32[1024,1536]{1,0:T(8,128)}) fusion(f32[1536]{0:T(1024)S(1)} %copy-done.51, bf16[1024,768]{0,1:T(8,128)(2,1)S(1)} %fusion.43, bf16[768,1536]{1,0:T(8,128)(2,1)S(1)} %copy-done), kind=kOutput, calls=%fused_computation.28 | convolution fusion | flops 2519728128 | bytes 19666944 | tf_op jit(solution)/shard_map/dot_general | solution.py:164
  104.5 8.5 %convert_reduce_fusion = (f32[1536]{0:T(1024)}, bf16[1024,1536]{1,0:T(8,128)(2,1)S(1)}) fusion(f32[1024,1536]{1,0:T(8,128)} %get-tuple-element.107, f32[1024,1536]{1,0:T(8,128)} %get-tuple-element.155, f32[1536]{0:T(1024)S(1)} %copy-done.51, bf16[1024,768]{0,1:T(8,128)(2,1)S(1)} %add_convert_fusion.4, bf16[1536,768]{1,0:T(8,128)(2,1)S(1)} %copy-done.50), kind=kOutput, calls=%fused_computation.26 | convolution fusion | flops 2442656256 | bytes 19673088 | tf_op jit(solution)/shard_map/dot_general | solution.py:31
  123.5 6.1 %collective-permute-done.32 = f32[384,768]{1,0:T(8,128)} collective-permute-done((f32[384,768]{1,0:T(8,128)S(1)}, f32[384,768]{1,0:T(8,128)}, u32[]{:S(2)}, u32[]{:S(2)}) %collective-permute-start.32) | collective-permute-done | bytes 1179680 | tf_op jit(solution)/shard_map/ppermute | solution.py:63
  135.0 19.8 %collective-permute-done.18 = f32[384,768]{1,0:T(8,128)S(1)} collective-permute-done((f32[384,768]{1,0:T(8,128)S(1)}, f32[384,768]{1,0:T(8,128)S(1)}, u32[]{:S(2)}, u32[]{:S(2)}) %collective-permute-start.18) | collective-permute-done | bytes 1179680 | tf_op jit(solution)/shard_map/ppermute | solution.py:63
  159.7 10.0 %collective-permute-done.33 = f32[192,768]{1,0:T(8,128)S(1)} collective-permute-done((f32[192,768]{1,0:T(8,128)S(1)}, f32[192,768]{1,0:T(8,128)S(1)}, u32[]{:S(2)}, u32[]{:S(2)}) %collective-permute-start.33) | collective-permute-done | bytes 589856 | tf_op jit(solution)/shard_map/ppermute | solution.py:63
  194.0 10.1 %fusion.96 = f32[6,1024,1024]{1,2,0:T(8,128)} fusion(bf16[1024,6,64]{0,2,1:T(8,128)(2,1)S(1)} %bitcast.80, bf16[1024,6,64]{0,2,1:T(8,128)(2,1)S(1)} %bitcast.79), kind=kOutput, calls=%fused_computation.216 | convolution fusion | flops 805306368 | bytes 26738688 | tf_op jit(solution)/shard_map/qhd,khd->hqk/dot_general | solution.py:204
  204.1 13.1 %convert_reduce_fusion.2 = (f32[6,64]{1,0:T(8,128)}, bf16[6,64,1024]{2,1,0:T(8,128)(2,1)}) fusion(bf16[1024,6,64]{0,2,1:T(8,128)(2,1)S(1)} %bitcast.81, f32[6,1024,1024]{1,2,0:T(8,128)} %get-tuple-element.154, f32[6,1024]{1,0:T(8,128)S(1)} %log_add_fusion, pred[1024,1024]{0,1:T(8,128)(4,1)S(1)} %broadcast_compare_fusion), kind=kOutput, calls=%fused_computation.85 | convolution fusion | flops 831651456 | bytes 27813376 | tf_op jit(solution)/shard_map/hqk,qhd->khd/dot_general | solution.py:201
  217.2 35.8 %convert_reduce_fusion.3 = (f32[6,64]{1,0:T(8,128)}, bf16[6,64,1024]{2,1,0:T(8,128)(2,1)}) fusion(bf16[1024,6,64]{0,2,1:T(8,128)(2,1)} %bitcast.77, f32[6,1024,1024]{1,2,0:T(8,128)} %fusion.96, f32[6,1024,1024]{1,2,0:T(8,128)} %get-tuple-element.154, f32[6,1024]{1,0:T(8,128)S(1)} %log_add_fusion, pred[1024,1024]{0,1:T(8,128)(4,1)S(1)} %broadcast_compare_fusion), kind=kOutput, calls=%fused_computation.86 | convolution fusion | flops 875698816 | bytes 52979200 | tf_op jit(solution)/shard_map/hqk,khd->qhd/dot_general | solution.py:209
  253.0 35.5 %fusion.58 = bf16[6,64,1024]{2,1,0:T(8,128)(2,1)} fusion(bf16[1024,6,64]{0,2,1:T(8,128)(2,1)S(1)} %bitcast.75, f32[6,1024,1024]{1,2,0:T(8,128)} %fusion.96, f32[6,1024,1024]{1,2,0:T(8,128)} %get-tuple-element.154, f32[6,1024]{1,0:T(8,128)S(1)} %log_add_fusion, pred[1024,1024]{0,1:T(8,128)(4,1)S(1)} %broadcast_compare_fusion), kind=kOutput, calls=%fused_computation.93 | convolution fusion | flops 874912768 | bytes 52977664 | tf_op jit(solution)/shard_map/hqk,qhd->khd/dot_general | solution.py:212
  305.7 5.0 collective-permute-done.27
  354.2 6.5 %collective-permute-done.22 = f32[192,768]{1,0:T(8,128)} collective-permute-done((f32[192,768]{1,0:T(8,128)}, f32[192,768]{1,0:T(8,128)}, u32[]{:S(2)}, u32[]{:S(2)}) %collective-permute-start.22) | collective-permute-done | bytes 589856 | tf_op jit(solution)/shard_map/ppermute | solution.py:95
  363.1 9.2 %collective-permute-done.29 = f32[192,768]{1,0:T(8,128)} collective-permute-done((f32[192,768]{1,0:T(8,128)}, f32[192,768]{1,0:T(8,128)}, u32[]{:S(2)}, u32[]{:S(2)}) %collective-permute-start.29) | collective-permute-done | bytes 589856 | tf_op jit(solution)/shard_map/ppermute | solution.py:95
  381.5 10.9 %collective-permute-done.37 = f32[192,768]{1,0:T(8,128)S(1)} collective-permute-done((f32[192,768]{1,0:T(8,128)S(1)}, f32[192,768]{1,0:T(8,128)S(1)}, u32[]{:S(2)}, u32[]{:S(2)}) %collective-permute-start.37) | collective-permute-done | bytes 589856 | tf_op jit(solution)/shard_map/ppermute | solution.py:63
  395.0 21.2 %collective-permute-done.5 = f32[192,768]{1,0:T(8,128)S(1)} collective-permute-done((f32[192,768]{1,0:T(8,128)S(1)}, f32[192,768]{1,0:T(8,128)S(1)}, u32[]{:S(2)}, u32[]{:S(2)}) %collective-permute-start.5) | collective-permute-done | bytes 589856 | tf_op jit(solution)/shard_map/ppermute | solution.py:63
  417.9 32.3 %collective-permute-start.6 = (f32[192,768]{1,0:T(8,128)S(1)}, f32[192,768]{1,0:T(8,128)S(1)}, u32[]{:S(2)}, u32[]{:S(2)}) collective-permute-start(f32[192,768]{1,0:T(8,128)S(1)} %dynamic-slice_add_fusion.10), channel_id=1, source_target_pairs={{0,8},{24,16},{2,10},{26,18},{4,12},{28,20},{6,14},{30,22},{1,9},{... | collective-permute-start | bytes 1769480 | tf_op jit(solution)/shard_map/ppermute | solution.py:93
  455.2 8.7 %collective-permute-done.6 = f32[192,768]{1,0:T(8,128)S(1)} collective-permute-done((f32[192,768]{1,0:T(8,128)S(1)}, f32[192,768]{1,0:T(8,128)S(1)}, u32[]{:S(2)}, u32[]{:S(2)}) %collective-permute-start.6) | collective-permute-done | bytes 589856 | tf_op jit(solution)/shard_map/ppermute | solution.py:93
  484.6 9.3 %collective-permute-done.45 = f32[384,768]{1,0:T(8,128)} collective-permute-done((f32[384,768]{1,0:T(8,128)}, f32[384,768]{1,0:T(8,128)}, u32[]{:S(2)}, u32[]{:S(2)}) %collective-permute-start.45) | collective-permute-done | bytes 1179680 | tf_op jit(solution)/shard_map/ppermute | solution.py:63
  499.7 10.1 %collective-permute-done.15 = f32[200,768]{1,0:T(8,128)S(1)} collective-permute-done((f32[200,768]{1,0:T(8,128)S(1)}, f32[200,768]{1,0:T(8,128)S(1)}, u32[]{:S(2)}, u32[]{:S(2)}) %collective-permute-start.15) | collective-permute-done | bytes 614432 | tf_op jit(solution)/shard_map/ppermute | solution.py:95
  511.5 7.4 %collective-permute-done.31 = f32[384,768]{1,0:T(8,128)S(1)} collective-permute-done((f32[384,768]{1,0:T(8,128)S(1)}, f32[384,768]{1,0:T(8,128)S(1)}, u32[]{:S(2)}, u32[]{:S(2)}) %collective-permute-start.31) | collective-permute-done | bytes 1179680 | tf_op jit(solution)/shard_map/ppermute | solution.py:63
  519.1 6.3 %collective-permute-done.9 = f32[192,768]{1,0:T(8,128)S(1)} collective-permute-done((f32[192,768]{1,0:T(8,128)S(1)}, f32[192,768]{1,0:T(8,128)S(1)}, u32[]{:S(2)}, u32[]{:S(2)}) %collective-permute-start.9) | collective-permute-done | bytes 589856 | tf_op jit(solution)/shard_map/ppermute | solution.py:63
  536.9 12.3 %collective-permute-done.10 = f32[384,768]{1,0:T(8,128)} collective-permute-done((f32[384,768]{1,0:T(8,128)}, f32[384,768]{1,0:T(8,128)}, u32[]{:S(2)}, u32[]{:S(2)}) %collective-permute-start.10) | collective-permute-done | bytes 1179680 | tf_op jit(solution)/shard_map/ppermute | solution.py:63
  (322 shorter events, 224.2 us)
Async XLA Ops:
  102.9 30.4 %collective-permute-start.39 = (f32[384,768]{1,0:T(8,128)S(1)}, f32[384,768]{1,0:T(8,128)S(1)}, u32[]{:S(2)}, u32[]{:S(2)}) collective-permute-start(f32[384,768]{1,0:T(8,128)S(1)} %constant_dynamic-slice_fusion.1), channel_id=1, source_target_pairs={{0,4},{2,6},{4,0},{6,2},{8,12},{10,14},{12,8},{14,10},{16,20},{18,... | collective-permute-start | bytes 3538952 | tf_op jit(solution)/shard_map/ppermute | solution.py:63
  117.3 69.2 %collective-permute-start.2 = (f32[1024,768]{0,1:T(8,128)S(1)}, f32[1024,768]{0,1:T(8,128)S(1)}, u32[]{:S(2)}, u32[]{:S(2)}) collective-permute-start(f32[1024,768]{0,1:T(8,128)S(1)} %fusion.95), channel_id=1, source_target_pairs={{0,1},{1,0},{2,3},{3,2},{4,5},{5,4},{6,7},{7,6},{8,9},{9,8},{10,11... | collective-permute-start | bytes 9437192 | tf_op jit(solution)/shard_map/ppermute | solution.py:59
  120.4 34.4 %collective-permute-start.18 = (f32[384,768]{1,0:T(8,128)S(1)}, f32[384,768]{1,0:T(8,128)S(1)}, u32[]{:S(2)}, u32[]{:S(2)}) collective-permute-start(f32[384,768]{1,0:T(8,128)S(1)} %constant_dynamic-slice_fusion.7), channel_id=1, source_target_pairs={{0,2},{2,0},{4,6},{6,4},{8,10},{10,8},{12,14},{14,12},{16,18},{18,... | collective-permute-start | bytes 3538952 | tf_op jit(solution)/shard_map/ppermute | solution.py:63
  122.5 34.7 %collective-permute-start.25 = (f32[384,768]{1,0:T(8,128)S(1)}, f32[384,768]{1,0:T(8,128)S(1)}, u32[]{:S(2)}, u32[]{:S(2)}) collective-permute-start(f32[384,768]{1,0:T(8,128)S(1)} %constant_dynamic-slice_fusion.5), channel_id=1, source_target_pairs={{0,4},{2,6},{4,0},{6,2},{8,12},{10,14},{12,8},{14,10},{16,20},{18,... | collective-permute-start | bytes 3538952 | tf_op jit(solution)/shard_map/ppermute | solution.py:63
  131.1 38.6 %collective-permute-start.33 = (f32[192,768]{1,0:T(8,128)S(1)}, f32[192,768]{1,0:T(8,128)S(1)}, u32[]{:S(2)}, u32[]{:S(2)}) collective-permute-start(f32[192,768]{1,0:T(8,128)S(1)} %constant_dynamic-slice_fusion.2), channel_id=1, source_target_pairs={{0,4},{2,6},{4,0},{6,2},{8,12},{10,14},{12,8},{14,10},{16,20},{18,... | collective-permute-start | bytes 1769480 | tf_op jit(solution)/shard_map/ppermute | solution.py:63
  133.5 41.4 %collective-permute-start.40 = (f32[192,768]{1,0:T(8,128)S(1)}, f32[192,768]{1,0:T(8,128)S(1)}, u32[]{:S(2)}, u32[]{:S(2)}) collective-permute-start(f32[192,768]{1,0:T(8,128)S(1)} %constant_dynamic-slice_fusion), channel_id=1, source_target_pairs={{0,2},{2,0},{4,6},{6,4},{8,10},{10,8},{12,14},{14,12},{16,18},{18,... | collective-permute-start | bytes 1769480 | tf_op jit(solution)/shard_map/ppermute | solution.py:63
  158.2 136.5 %collective-permute-start.26 = (f32[192,768]{1,0:T(8,128)}, f32[192,768]{1,0:T(8,128)}, u32[]{:S(2)}, u32[]{:S(2)}) collective-permute-start(f32[192,768]{1,0:T(8,128)} %constant_dynamic-slice_fusion.4), channel_id=1, source_target_pairs={{0,2},{2,0},{4,6},{6,4},{8,10},{10,8},{12,14},{14,12},{16,18},{18,... | collective-permute-start | bytes 1769480 | tf_op jit(solution)/shard_map/ppermute | solution.py:63
  170.6 126.7 %collective-permute-start.34 = (f32[192,768]{1,0:T(8,128)}, f32[192,768]{1,0:T(8,128)}, u32[]{:S(2)}, u32[]{:S(2)}) collective-permute-start(f32[192,768]{1,0:T(8,128)} %dynamic-slice_add_fusion.7), channel_id=1, source_target_pairs={{0,8},{24,16},{2,10},{26,18},{4,12},{28,20},{6,14},{30,22},{1,9},{... | collective-permute-start | bytes 1769480 | tf_op jit(solution)/shard_map/ppermute | solution.py:93
  175.8 124.3 %collective-permute-start.41 = (f32[192,768]{1,0:T(8,128)}, f32[192,768]{1,0:T(8,128)}, u32[]{:S(2)}, u32[]{:S(2)}) collective-permute-start(f32[192,768]{1,0:T(8,128)} %dynamic-slice_add_fusion.6), channel_id=1, source_target_pairs={{0,8},{24,16},{2,10},{26,18},{4,12},{28,20},{6,14},{30,22},{1,9},{... | collective-permute-start | bytes 1769480 | tf_op jit(solution)/shard_map/ppermute | solution.py:93
  182.1 120.7 %collective-permute-start.20 = (f32[192,768]{1,0:T(8,128)}, f32[192,768]{1,0:T(8,128)}, u32[]{:S(2)}, u32[]{:S(2)}) collective-permute-start(f32[192,768]{1,0:T(8,128)} %dynamic-slice_add_fusion.9), channel_id=1, source_target_pairs={{0,8},{24,16},{2,10},{26,18},{4,12},{28,20},{6,14},{30,22},{1,9},{... | collective-permute-start | bytes 1769480 | tf_op jit(solution)/shard_map/ppermute | solution.py:93
  294.8 47.9 %collective-permute-start.3 = (f32[1024,768]{0,1:T(8,128)}, f32[1024,768]{0,1:T(8,128)}, u32[]{:S(2)}, u32[]{:S(2)}) collective-permute-start(f32[1024,768]{0,1:T(8,128)} %add_add_fusion.2), channel_id=1, source_target_pairs={{0,1},{1,0},{2,3},{3,2},{4,5},{5,4},{6,7},{7,6},{8,9},{9,8},{10,11... | collective-permute-start | bytes 9437192 | tf_op jit(solution)/shard_map/ppermute | solution.py:59
  315.1 34.7 %collective-permute-start.36 = (f32[192,768]{1,0:T(8,128)}, f32[192,768]{1,0:T(8,128)}, u32[]{:S(2)}, u32[]{:S(2)}) collective-permute-start(f32[192,768]{1,0:T(8,128)} %add.343), channel_id=1, source_target_pairs={{8,0},{16,24},{10,2},{18,26},{12,4},{20,28},{14,6},{22,30},{9,1},{... | collective-permute-start | bytes 1769480 | tf_op jit(solution)/shard_map/ppermute | solution.py:95
  318.3 34.2 %collective-permute-start.43 = (f32[192,768]{1,0:T(8,128)}, f32[192,768]{1,0:T(8,128)}, u32[]{:S(2)}, u32[]{:S(2)}) collective-permute-start(f32[192,768]{1,0:T(8,128)} %add.347), channel_id=1, source_target_pairs={{8,0},{16,24},{10,2},{18,26},{12,4},{20,28},{14,6},{22,30},{9,1},{... | collective-permute-start | bytes 1769480 | tf_op jit(solution)/shard_map/ppermute | solution.py:95
  321.6 39.1 %collective-permute-start.22 = (f32[192,768]{1,0:T(8,128)}, f32[192,768]{1,0:T(8,128)}, u32[]{:S(2)}, u32[]{:S(2)}) collective-permute-start(f32[192,768]{1,0:T(8,128)} %add.331), channel_id=1, source_target_pairs={{8,0},{16,24},{10,2},{18,26},{12,4},{20,28},{14,6},{22,30},{9,1},{... | collective-permute-start | bytes 1769480 | tf_op jit(solution)/shard_map/ppermute | solution.py:95
  325.1 47.2 %collective-permute-start.29 = (f32[192,768]{1,0:T(8,128)}, f32[192,768]{1,0:T(8,128)}, u32[]{:S(2)}, u32[]{:S(2)}) collective-permute-start(f32[192,768]{1,0:T(8,128)} %add.339), channel_id=1, source_target_pairs={{8,0},{16,24},{10,2},{18,26},{12,4},{20,28},{14,6},{22,30},{9,1},{... | collective-permute-start | bytes 1769480 | tf_op jit(solution)/shard_map/ppermute | solution.py:95
  342.7 33.2 %collective-permute-start.4 = (f32[384,768]{1,0:T(8,128)}, f32[384,768]{1,0:T(8,128)}, u32[]{:S(2)}, u32[]{:S(2)}) collective-permute-start(f32[384,768]{1,0:T(8,128)} %fusion.63), channel_id=1, source_target_pairs={{0,2},{2,0},{4,6},{6,4},{8,10},{10,8},{12,14},{14,12},{16,18},{18,... | collective-permute-start | bytes 3538952 | tf_op jit(solution)/shard_map/ppermute | solution.py:63
  352.5 39.9 %collective-permute-start.37 = (f32[192,768]{1,0:T(8,128)S(1)}, f32[192,768]{1,0:T(8,128)S(1)}, u32[]{:S(2)}, u32[]{:S(2)}) collective-permute-start(f32[192,768]{1,0:T(8,128)S(1)} %broadcast_select_fusion.20), channel_id=1, source_target_pairs={{0,4},{2,6},{4,0},{6,2},{8,12},{10,14},{12,8},{14,10},{16,20},{18,... | collective-permute-start | bytes 1769480 | tf_op jit(solution)/shard_map/ppermute | solution.py:63
  360.6 90.4 %collective-permute-start.44 = (f32[192,768]{1,0:T(8,128)S(1)}, f32[192,768]{1,0:T(8,128)S(1)}, u32[]{:S(2)}, u32[]{:S(2)}) collective-permute-start(f32[192,768]{1,0:T(8,128)S(1)} %broadcast_select_fusion.19), channel_id=1, source_target_pairs={{0,2},{2,0},{4,6},{6,4},{8,10},{10,8},{12,14},{14,12},{16,18},{18,... | collective-permute-start | bytes 1769480 | tf_op jit(solution)/shard_map/ppermute | solution.py:63
  372.4 96.8 %collective-permute-start.23 = (f32[192,768]{1,0:T(8,128)}, f32[192,768]{1,0:T(8,128)}, u32[]{:S(2)}, u32[]{:S(2)}) collective-permute-start(f32[192,768]{1,0:T(8,128)} %broadcast_select_fusion.22), channel_id=1, source_target_pairs={{0,4},{2,6},{4,0},{6,2},{8,12},{10,14},{12,8},{14,10},{16,20},{18,... | collective-permute-start | bytes 1769480 | tf_op jit(solution)/shard_map/ppermute | solution.py:63
  375.8 100.4 %collective-permute-start.30 = (f32[192,768]{1,0:T(8,128)}, f32[192,768]{1,0:T(8,128)}, u32[]{:S(2)}, u32[]{:S(2)}) collective-permute-start(f32[192,768]{1,0:T(8,128)} %broadcast_select_fusion.21), channel_id=1, source_target_pairs={{0,2},{2,0},{4,6},{6,4},{8,10},{10,8},{12,14},{14,12},{16,18},{18,... | collective-permute-start | bytes 1769480 | tf_op jit(solution)/shard_map/ppermute | solution.py:63
  379.8 36.5 %collective-permute-start.5 = (f32[192,768]{1,0:T(8,128)S(1)}, f32[192,768]{1,0:T(8,128)S(1)}, u32[]{:S(2)}, u32[]{:S(2)}) collective-permute-start(f32[192,768]{1,0:T(8,128)S(1)} %constant_dynamic-slice_fusion.10), channel_id=1, source_target_pairs={{0,4},{2,6},{4,0},{6,2},{8,12},{10,14},{12,8},{14,10},{16,20},{18,... | collective-permute-start | bytes 1769480 | tf_op jit(solution)/shard_map/ppermute | solution.py:63
  416.3 63.8 %collective-permute-start.38 = (f32[384,768]{1,0:T(8,128)}, f32[384,768]{1,0:T(8,128)}, u32[]{:S(2)}, u32[]{:S(2)}) collective-permute-start(f32[384,768]{1,0:T(8,128)} %pad_maximum_fusion.9), channel_id=1, source_target_pairs={{0,2},{2,0},{4,6},{6,4},{8,10},{10,8},{12,14},{14,12},{16,18},{18,... | collective-permute-start | bytes 3538952 | tf_op jit(solution)/shard_map/ppermute | solution.py:63
  417.9 46.1 %collective-permute-start.6 = (f32[192,768]{1,0:T(8,128)S(1)}, f32[192,768]{1,0:T(8,128)S(1)}, u32[]{:S(2)}, u32[]{:S(2)}) collective-permute-start(f32[192,768]{1,0:T(8,128)S(1)} %dynamic-slice_add_fusion.10), channel_id=1, source_target_pairs={{0,8},{24,16},{2,10},{26,18},{4,12},{28,20},{6,14},{30,22},{1,9},{... | collective-permute-start | bytes 1769480 | tf_op jit(solution)/shard_map/ppermute | solution.py:93
  478.4 40.5 %collective-permute-start.31 = (f32[384,768]{1,0:T(8,128)S(1)}, f32[384,768]{1,0:T(8,128)S(1)}, u32[]{:S(2)}, u32[]{:S(2)}) collective-permute-start(f32[384,768]{1,0:T(8,128)S(1)} %pad_maximum_fusion.8), channel_id=1, source_target_pairs={{0,4},{2,6},{4,0},{6,2},{8,12},{10,14},{12,8},{14,10},{16,20},{18,... | collective-permute-start | bytes 3538952 | tf_op jit(solution)/shard_map/ppermute | solution.py:63
  (80 other events, 942.5 us)

commit v2 on v1

v2 whole, which is shorter than its diff:
```python
import functools

import jax
import jax.numpy as jnp
from jax import lax
from jax.experimental import pallas as pl
from jax.experimental.pallas import tpu as pltpu
from jax.sharding import PartitionSpec as P

DH = 64
LANES = 128
ROW_BLOCK = 256
MIB = 1 << 20

score_scale = 0.125
norm_eps = 1e-05
far_negative = -1e30
log2_e = 1.4426950408889634


def contract(left_side, right_side, left_dim, right_dim):
    return lax.dot_general(
        left_side,
        right_side,
        (((left_dim,), (right_dim,)), ((), ())),
        preferred_element_type=jnp.float32,
    )


def sequence_ends(lengths_ref, count):
    ends = []
    total = jnp.int32(0)
    for at in range(count):
        total = total + lengths_ref[0, at]
        ends.append(total)
    return ends


def key_window(ends, first_row, rows):
    last_row = first_row + LANES - 1
    start = jnp.int32(0)
    stop = jnp.int32(rows)
    for end in ends:
        start = jnp.where(end <= first_row, jnp.maximum(start, end), start)
        stop = jnp.where(end > last_row, jnp.minimum(stop, end), stop)
    start = (start // LANES) * LANES
    stop = ((stop + LANES - 1) // LANES) * LANES
    return start, stop


def window_bias(ends, first_row, key_start, width):
    query_at = lax.broadcasted_iota(jnp.int32, (1, LANES), 1) + first_row
    seq_start = jnp.zeros((1, LANES), jnp.int32)
    seq_stop = jnp.full((1, LANES), 1 << 30, jnp.int32)
    for end in ends:
        seq_start = jnp.where(query_at >= end, jnp.maximum(seq_start, end), seq_start)
        seq_stop = jnp.where(query_at < end, jnp.minimum(seq_stop, end), seq_stop)
    key_at = lax.broadcasted_iota(jnp.int32, (width, LANES), 0) + key_start
    seen = (key_at >= seq_start) & (key_at < seq_stop)
    bias = jnp.where(seen, 0.0, far_negative).astype(jnp.float32)
    return jnp.concatenate([bias, bias], axis=1)


def split_heads(block):
    lane = lax.broadcasted_iota(jnp.int32, block.shape, 1)
    wide = block.astype(jnp.float32)
    return jnp.concatenate(
        [jnp.where(lane < DH, wide, 0.0), jnp.where(lane < DH, 0.0, wide)], axis=0
    ).astype(jnp.bfloat16)


def merge_heads(turned):
    return jnp.concatenate([turned[:DH, :LANES], turned[DH:, LANES:]], axis=0).T


def over_query_blocks(ends, rows, widths, body):
    @pl.loop(0, rows // LANES)
    def _(block):
        first_row = pl.multiple_of(block * LANES, LANES)
        start, stop = key_window(ends, first_row, rows)
        span = stop - start
        lower = 0
        for width in widths:
            chosen = (span > lower) & (span <= width)
            key_start = pl.multiple_of(jnp.minimum(start, rows - width), LANES)
            pl.when(chosen)(functools.partial(body, block, first_row, key_start, width))
            lower = width


def attend_kernel(
    widths,
    seqs,
    lengths_ref,
    tokens_ref,
    q_weight_ref,
    k_weight_ref,
    v_weight_ref,
    q_bias_ref,
    v_bias_ref,
    out_weight_ref,
    queries_ref,
    keys_ref,
    values_ref,
    context_ref,
    total_ref,
    attn_out_ref,
    turned_ref,
):
    rows = tokens_ref.shape[0]
    pairs = q_weight_ref.shape[1] // LANES
    tokens = tokens_ref[...]
    queries_ref[...] = (contract(tokens, q_weight_ref[...], 1, 0) + q_bias_ref[...]).astype(
        jnp.bfloat16
    )
    keys_ref[...] = contract(tokens, k_weight_ref[...], 1, 0).astype(jnp.bfloat16)
    values = contract(tokens, v_weight_ref[...], 1, 0) + v_bias_ref[...]
    values_ref[...] = values.astype(jnp.bfloat16)
    turned_ref[...] = values.T.astype(jnp.bfloat16)
    ends = sequence_ends(lengths_ref, seqs)

    def body(block, first_row, key_start, width):
        bias = window_bias(ends, first_row, key_start, width)
        for pair in range(pairs):
            lanes = slice(pair * LANES, (pair + 1) * LANES)
            both = split_heads(queries_ref[pl.ds(first_row, LANES), lanes])
            keys = keys_ref[pl.ds(key_start, width), lanes]
            scores = contract(keys, both, 1, 1) * (score_scale * log2_e) + bias
            peak = jnp.max(scores, axis=0, keepdims=True)
            exponents = jnp.exp2(scores - peak)
            total = jnp.sum(exponents, axis=0, keepdims=True)
            total_ref[pl.ds(block * pairs + pair, 1), :] = peak + jnp.log2(total)
            probs = (exponents * (1.0 / total)).astype(jnp.bfloat16)
            turned = contract(turned_ref[lanes, pl.ds(key_start, width)], probs, 1, 0)
            context_ref[pl.ds(first_row, LANES), lanes] = merge_heads(turned).astype(jnp.bfloat16)

    over_query_blocks(ends, rows, widths, body)
    attn_out_ref[...] = contract(context_ref[...], out_weight_ref[...], 1, 0)


def attend_back_kernel(
    widths,
    seqs,
    lengths_ref,
    back_attn_ref,
    out_weight_ref,
    queries_ref,
    keys_ref,
    values_ref,
    total_ref,
    tokens_ref,
    context_ref,
    q_weight_ref,
    k_weight_ref,
    v_weight_ref,
    small_ref,
    first_pack_ref,
    second_pack_ref,
    partial_ref,
    back_context_ref,
    turned_ref,
    back_queries_ref,
    back_keys_ref,
    back_values_ref,
):
    rows = tokens_ref.shape[0]
    width_here = q_weight_ref.shape[1]
    pairs = width_here // LANES
    back_context_ref[...] = contract(back_attn_ref[...], out_weight_ref[...], 1, 1).astype(
        jnp.bfloat16
    )
    turned_ref[...] = keys_ref[...].astype(jnp.float32).T.astype(jnp.bfloat16)
    back_keys_ref[...] = jnp.zeros_like(back_keys_ref)
    back_values_ref[...] = jnp.zeros_like(back_values_ref)
    ends = sequence_ends(lengths_ref, seqs)

    def body(block, first_row, key_start, width):
        bias = window_bias(ends, first_row, key_start, width)
        for pair in range(pairs):
            lanes = slice(pair * LANES, (pair + 1) * LANES)
            both = split_heads(queries_ref[pl.ds(first_row, LANES), lanes])
            back_both = split_heads(back_context_ref[pl.ds(first_row, LANES), lanes])
            keys = keys_ref[pl.ds(key_start, width), lanes]
            values = values_ref[pl.ds(key_start, width), lanes]
            scores = contract(keys, both, 1, 1) * (score_scale * log2_e) + bias
            probs = jnp.exp2(scores - total_ref[pl.ds(block * pairs + pair, 1), :])
            back_probs = contract(values, back_both, 1, 1)
            inner = jnp.sum(back_probs * probs, axis=0, keepdims=True)
            back_scores = (probs * (back_probs - inner) * score_scale).astype(jnp.bfloat16)
            back_values_ref[pl.ds(key_start, width), lanes] += contract(
                probs.astype(jnp.bfloat16), back_both, 1, 0
            )
            back_keys_ref[pl.ds(key_start, width), lanes] += contract(back_scores, both, 1, 0)
            turned = contract(turned_ref[lanes, pl.ds(key_start, width)], back_scores, 1, 0)
            back_queries_ref[pl.ds(first_row, LANES), lanes] = merge_heads(turned).astype(
                jnp.bfloat16
            )

    over_query_blocks(ends, rows, widths, body)
    model = tokens_ref.shape[1]
    tokens = tokens_ref[...]
    back_queries = back_queries_ref[...]
    back_keys = back_keys_ref[...].astype(jnp.bfloat16)
    back_values = back_values_ref[...].astype(jnp.bfloat16)
    first_pack_ref[:, :width_here] = contract(tokens, back_queries, 0, 0)
    first_pack_ref[:, width_here:] = contract(tokens, back_keys, 0, 0)
    grad_values = contract(tokens, back_values, 0, 0)
    second_pack_ref[:width_here, :] = contract(context_ref[...], back_attn_ref[...], 0, 0)
    half = model // 2
    second_pack_ref[width_here : width_here + half, :width_here] = grad_values[:half]
    second_pack_ref[width_here : width_here + half, width_here:] = grad_values[half:]
    second_pack_ref[width_here + half :, :] = small_ref[...]
    top = width_here + half
    second_pack_ref[top : top + 1, :width_here] = jnp.sum(
        back_queries.astype(jnp.float32), axis=0, keepdims=True
    )
    second_pack_ref[top : top + 1, width_here:] = jnp.sum(
        back_values.astype(jnp.float32), axis=0, keepdims=True
    )
    partial_ref[...] = (
        contract(back_queries, q_weight_ref[...], 1, 1)
        + contract(back_keys, k_weight_ref[...], 1, 1)
        + contract(back_values, v_weight_ref[...], 1, 1)
    )


def row_mean(values):
    return jnp.mean(values, axis=-1, keepdims=True)


def standardize(values):
    centre = values - row_mean(values)
    rate = lax.rsqrt(row_mean(centre * centre) + norm_eps)
    return centre * rate, rate


def norm_back(upstream, unit, rate, gain):
    scaled = upstream * gain
    return rate * (scaled - row_mean(scaled) - unit * row_mean(scaled * unit))


def add_sums(sums_ref, members):
    @pl.when(pl.program_id(0) == 0)
    def _():
        sums_ref[...] = jnp.zeros_like(sums_ref)

    for at, member in enumerate(members):
        sums_ref[at : at + 1, :] += jnp.sum(member, axis=0, keepdims=True)


def feed_kernel(
    tokens_ref,
    own_ref,
    other_ref,
    out_bias_ref,
    gain_ref,
    shift_ref,
    up_weight_ref,
    up_bias_ref,
    down_weight_ref,
    first_sum_ref,
    first_low_ref,
    inner_ref,
    active_ref,
    partial_ref,
):
    first_sum = (
        tokens_ref[...].astype(jnp.float32) + (own_ref[...] + other_ref[...]) + out_bias_ref[...]
    )
    first_sum_ref[...] = first_sum
    unit, unused = standardize(first_sum)
    first_low = (unit * gain_ref[...] + shift_ref[...]).astype(jnp.bfloat16)
    first_low_ref[...] = first_low
    inner = contract(first_low, up_weight_ref[...], 1, 0) + up_bias_ref[...]
    inner_ref[...] = inner
    active = (inner * (0.5 * (1.0 + lax.erf(inner * 0.7071067811865476)))).astype(jnp.bfloat16)
    active_ref[...] = active
    partial_ref[...] = contract(active, down_weight_ref[...], 1, 0)


def second_norm_kernel(
    first_sum_ref,
    own_ref,
    other_ref,
    cotangent_ref,
    active_ref,
    first_gain_ref,
    first_shift_ref,
    down_bias_ref,
    gain_ref,
    shift_ref,
    layer_out_ref,
    back_second_ref,
    back_down_ref,
    grad_low_ref,
    grad_high_ref,
    sums_ref,
):
    unit, unused = standardize(first_sum_ref[...])
    first = unit * first_gain_ref[...] + first_shift_ref[...]
    second_sum = first + (own_ref[...] + other_ref[...]) + down_bias_ref[...]
    unit, rate = standardize(second_sum)
    layer_out_ref[...] = (unit * gain_ref[...] + shift_ref[...]).astype(jnp.bfloat16)
    upstream = cotangent_ref[...].astype(jnp.float32)
    back_second = norm_back(upstream, unit, rate, gain_ref[...])
    back_second_ref[...] = back_second
    back_down = back_second.astype(jnp.bfloat16)
    back_down_ref[...] = back_down
    half = grad_low_ref.shape[0]

    @pl.when(pl.program_id(0) == 0)
    def _():
        grad_low_ref[...] = jnp.zeros_like(grad_low_ref)
        grad_high_ref[...] = jnp.zeros_like(grad_high_ref)

    grad_low_ref[...] += contract(active_ref[:, :half], back_down, 0, 0)
    grad_high_ref[...] += contract(active_ref[:, half:], back_down, 0, 0)
    add_sums(sums_ref, (back_second, upstream * unit, upstream))


def feed_back_kernel(
    back_down_ref,
    inner_ref,
    first_low_ref,
    down_weight_ref,
    up_weight_ref,
    partial_ref,
    grad_low_ref,
    grad_high_ref,
    sums_ref,
):
    inner = inner_ref[...]
    slope = 0.5 * (1.0 + lax.erf(inner * 0.7071067811865476)) + inner * (
        0.3989422804014327 * jnp.exp(-0.5 * inner * inner)
    )
    back_active = contract(back_down_ref[...], down_weight_ref[...], 1, 1)
    back_inner = (back_active * slope).astype(jnp.bfloat16)
    partial_ref[...] = contract(back_inner, up_weight_ref[...], 1, 1)
    half = grad_low_ref.shape[1]

    @pl.when(pl.program_id(0) == 0)
    def _():
        grad_low_ref[...] = jnp.zeros_like(grad_low_ref)
        grad_high_ref[...] = jnp.zeros_like(grad_high_ref)

    first_low = first_low_ref[...]
    grad_low_ref[...] += contract(first_low, back_inner[:, :half], 0, 0)
    grad_high_ref[...] += contract(first_low, back_inner[:, half:], 0, 0)
    add_sums(sums_ref, (back_inner.astype(jnp.float32),))


def first_norm_kernel(
    first_sum_ref,
    own_ref,
    other_ref,
    back_second_ref,
    gain_ref,
    back_first_sum_ref,
    back_attn_ref,
    sums_ref,
):
    unit, rate = standardize(first_sum_ref[...])
    upstream = (own_ref[...] + other_ref[...]) + back_second_ref[...]
    back_first_sum = norm_back(upstream, unit, rate, gain_ref[...])
    back_first_sum_ref[...] = back_first_sum
    back_attn_ref[...] = back_first_sum.astype(jnp.bfloat16)
    add_sums(sums_ref, (back_first_sum, upstream * unit, upstream))


def struct(shape, dtype):
    return jax.ShapeDtypeStruct(shape, dtype)


def by_rows(columns):
    return pl.BlockSpec((ROW_BLOCK, columns), lambda step: (step, 0))


def whole(shape):
    return pl.BlockSpec(shape, lambda *step: (0, 0))


def held(shape):
    return pl.BlockSpec(shape, lambda *step: (0, 0), pipeline_mode=pl.Buffered(1))


def in_smem():
    return pl.BlockSpec(memory_space=pltpu.SMEM)


def in_vmem():
    return pl.BlockSpec(memory_space=pltpu.VMEM)


def params(mebibytes):
    return pltpu.CompilerParams(vmem_limit_bytes=mebibytes * MIB)


def key_widths(rows):
    return tuple(width for width in (640,) if width < rows) + (rows,)


def attend(lengths, tokens, q_weight, k_weight, v_weight, q_bias, v_bias, out_weight):
    rows, model = tokens.shape
    width = q_weight.shape[1]
    totals = rows // LANES * (width // LANES)
    low = struct((rows, width), jnp.bfloat16)
    return pl.pallas_call(
        functools.partial(attend_kernel, key_widths(rows), lengths.shape[1]),
        out_shape=(
            low,
            low,
            low,
            low,
            struct((totals, 2 * LANES), jnp.float32),
            struct((rows, model), jnp.float32),
        ),
        in_specs=[in_smem()] + [in_vmem()] * 7,
        out_specs=(in_vmem(),) * 6,
        scratch_shapes=[pltpu.VMEM((width, rows), jnp.bfloat16)],
        compiler_params=params(40),
        name="attend",
    )(lengths, tokens, q_weight, k_weight, v_weight, q_bias, v_bias, out_weight)


def attend_back(
    lengths,
    back_attn,
    out_weight,
    queries,
    keys,
    values,
    totals,
    tokens,
    context,
    q_weight,
    k_weight,
    v_weight,
    small,
):
    rows, model = tokens.shape
    width = q_weight.shape[1]
    pack_rows = width + model // 2 + small.shape[0]
    return pl.pallas_call(
        functools.partial(attend_back_kernel, key_widths(rows), lengths.shape[1]),
        out_shape=(
            struct((model, 2 * width), jnp.float32),
            struct((pack_rows, model), jnp.float32),
            struct((rows, model), jnp.float32),
        ),
        in_specs=[in_smem()] + [in_vmem()] * 12,
        out_specs=(in_vmem(),) * 3,
        scratch_shapes=[
            pltpu.VMEM((rows, width), jnp.bfloat16),
            pltpu.VMEM((width, rows), jnp.bfloat16),
            pltpu.VMEM((rows, width), jnp.bfloat16),
            pltpu.VMEM((rows, width), jnp.float32),
            pltpu.VMEM((rows, width), jnp.float32),
        ],
        compiler_params=params(44),
        name="attend_back",
    )(
        lengths,
        back_attn,
        out_weight,
        queries,
        keys,
        values,
        totals,
        tokens,
        context,
        q_weight,
        k_weight,
        v_weight,
        small,
    )


def feed(tokens, own, other, out_bias, gain, shift, up_weight, up_bias, down_weight):
    rows, model = tokens.shape
    hidden = up_weight.shape[1]
    return pl.pallas_call(
        feed_kernel,
        grid=(rows // ROW_BLOCK,),
        out_shape=(
            struct((rows, model), jnp.float32),
            struct((rows, model), jnp.bfloat16),
            struct((rows, hidden), jnp.float32),
            struct((rows, hidden), jnp.bfloat16),
            struct((rows, model), jnp.float32),
        ),
        in_specs=[by_rows(model)] * 3
        + [held((1, model))] * 3
        + [held((model, hidden)), held((1, hidden)), held((hidden, model))],
        out_specs=(
            by_rows(model),
            by_rows(model),
            by_rows(hidden),
            by_rows(hidden),
            by_rows(model),
        ),
        compiler_params=params(40),
        name="feed",
    )(tokens, own, other, out_bias, gain, shift, up_weight, up_bias, down_weight)


def second_norm(
    first_sum, own, other, cotangent, active, first_gain, first_shift, down_bias, gain, shift
):
    rows, model = first_sum.shape
    hidden = active.shape[1]
    return pl.pallas_call(
        second_norm_kernel,
        grid=(rows // ROW_BLOCK,),
        out_shape=(
            struct((rows, model), jnp.bfloat16),
            struct((rows, model), jnp.float32),
            struct((rows, model), jnp.bfloat16),
            struct((hidden // 2, model), jnp.float32),
            struct((hidden // 2, model), jnp.float32),
            struct((8, model), jnp.float32),
        ),
        in_specs=[by_rows(model)] * 4 + [by_rows(hidden)] + [held((1, model))] * 5,
        out_specs=(
            by_rows(model),
            by_rows(model),
            by_rows(model),
            whole((hidden // 2, model)),
            whole((hidden // 2, model)),
            whole((8, model)),
        ),
        compiler_params=params(40),
        name="second_norm",
    )(first_sum, own, other, cotangent, active, first_gain, first_shift, down_bias, gain, shift)


def feed_back(back_down, inner, first_low, down_weight, up_weight):
    rows, model = back_down.shape
    hidden = inner.shape[1]
    return pl.pallas_call(
        feed_back_kernel,
        grid=(rows // ROW_BLOCK,),
        out_shape=(
            struct((rows, model), jnp.float32),
            struct((model, hidden // 2), jnp.float32),
            struct((model, hidden // 2), jnp.float32),
            struct((8, hidden), jnp.float32),
        ),
        in_specs=[
            by_rows(model),
            by_rows(hidden),
            by_rows(model),
            held((hidden, model)),
            held((model, hidden)),
        ],
        out_specs=(
            by_rows(model),
            whole((model, hidden // 2)),
            whole((model, hidden // 2)),
            whole((8, hidden)),
        ),
        compiler_params=params(40),
        name="feed_back",
    )(back_down, inner, first_low, down_weight, up_weight)


def first_norm_back(first_sum, own, other, back_second, gain):
    rows, model = first_sum.shape
    return pl.pallas_call(
        first_norm_kernel,
        grid=(rows // ROW_BLOCK,),
        out_shape=(
            struct((rows, model), jnp.float32),
            struct((rows, model), jnp.bfloat16),
            struct((8, model), jnp.float32),
        ),
        in_specs=[by_rows(model)] * 4 + [held((1, model))],
        out_specs=(by_rows(model), by_rows(model), whole((8, model))),
        compiler_params=params(32),
        name="first_norm_back",
    )(first_sum, own, other, back_second, gain)


def swap_cores(value, tensor_count):
    return lax.ppermute(value, "tensor", [(i, i ^ 1) for i in range(tensor_count)])


def swap_bit(value, bit, count):
    return lax.ppermute(value, "dp", [(i, i ^ (1 << bit)) for i in range(count)])


def halve(value, bit, count, place):
    rows = value.shape[0] // 2
    mine = (place >> bit) & 1
    sent = lax.dynamic_slice_in_dim(value, (1 - mine) * rows, rows, 0)
    kept = lax.dynamic_slice_in_dim(value, mine * rows, rows, 0)
    return kept + swap_bit(sent, bit, count)


def join(value, bit, count, place):
    other = swap_bit(value, bit, count)
    mine = (place >> bit) & 1
    first = jnp.where(mine == 0, value, other)
    second = jnp.where(mine == 0, other, value)
    return jnp.concatenate([first, second], axis=0)


def line_sum(value, count, place):
    stride = count // 4
    inward = []
    across = []
    outward = []
    for low in range(stride):
        ring = [low + stride * at for at in range(4)]
        inward += [(ring[0], ring[1]), (ring[3], ring[2])]
        across += [(ring[1], ring[2]), (ring[2], ring[1])]
        outward += [(ring[1], ring[0]), (ring[2], ring[3])]
    at_line = place // stride
    value = value + lax.ppermute(value, "dp", inward)
    value = value + lax.ppermute(value, "dp", across)
    ended = lax.ppermute(value, "dp", outward)
    return jnp.where((at_line == 1) | (at_line == 2), value, ended)


def all_sum(value, first_bit, count, place):
    second_bit = 1 - first_bit
    value = halve(value, first_bit, count, place)
    value = halve(value, second_bit, count, place)
    low_bits = (count // 4).bit_length() - 1
    for bit in range(2, low_bits):
        value = value + swap_bit(value, bit, count)
    value = line_sum(value, count, place)
    value = join(value, second_bit, count, place)
    return join(value, first_bit, count, place)


def local(
    dp_count,
    tensor_count,
    tokens_in,
    cotangent,
    seq_lengths,
    q_weight,
    k_weight,
    v_weight,
    q_bias,
    v_bias,
    out_weight,
    out_bias,
    first_gain,
    first_shift,
    up_weight,
    up_bias,
    down_weight,
    down_bias,
    second_gain,
    second_shift,
):
    place = lax.axis_index("dp")
    model = q_weight.shape[0]
    width = q_weight.shape[1]
    hidden = up_weight.shape[1]
    row = lambda vector: vector.reshape(1, -1)
    queries, keys, values, context, totals, attn_part = attend(
        seq_lengths, tokens_in, q_weight, k_weight, v_weight, row(q_bias), row(v_bias), out_weight
    )
    first_sum, first_low, inner, active, down_part = feed(
        tokens_in,
        attn_part,
        swap_cores(attn_part, tensor_count),
        row(out_bias),
        row(first_gain),
        row(first_shift),
        up_weight,
        row(up_bias),
        down_weight,
    )
    layer_out, back_second, back_down, down_low, down_high, second_sums = second_norm(
        first_sum,
        down_part,
        swap_cores(down_part, tensor_count),
        cotangent,
        active,
        row(first_gain),
        row(first_shift),
        row(down_bias),
        row(second_gain),
        row(second_shift),
    )
    down_low = all_sum(down_low, 0, dp_count, place)
    down_high = all_sum(down_high, 1, dp_count, place)
    back_part, up_low, up_high, up_sums = feed_back(
        back_down, inner, first_low, down_weight, up_weight
    )
    up_low = all_sum(up_low, 0, dp_count, place)
    up_high = all_sum(up_high, 1, dp_count, place)
    back_first_sum, back_attn, first_sums = first_norm_back(
        first_sum, back_part, swap_cores(back_part, tensor_count), back_second, row(first_gain)
    )
    small = jnp.concatenate(
        [
            jnp.zeros((1, model), jnp.float32),
            up_sums[0].reshape(-1, model),
            first_sums[:3],
            second_sums[:3],
        ]
    )
    small = jnp.pad(small, ((0, -small.shape[0] % 32), (0, 0)))
    first_pack, second_pack, input_part = attend_back(
        seq_lengths,
        back_attn,
        out_weight,
        queries,
        keys,
        values,
        totals,
        tokens_in,
        context,
        q_weight,
        k_weight,
        v_weight,
        small,
    )
    first_pack = all_sum(first_pack, 0, dp_count, place)
    second_pack = all_sum(second_pack, 1, dp_count, place)
    grad_input = (
        (input_part + swap_cores(input_part, tensor_count)) + back_first_sum
    ).astype(jnp.bfloat16)
    turned = second_pack[width : width + model // 2]
    tail = second_pack[width + model // 2 :]
    up_rows = hidden // model
    return (
        layer_out,
        grad_input,
        first_pack[:, :width],
        first_pack[:, width:],
        jnp.concatenate([turned[:, :width], turned[:, width:]], axis=0),
        tail[0, :width],
        tail[0, width:],
        second_pack[:width],
        tail[up_rows + 1],
        tail[up_rows + 2],
        tail[up_rows + 3],
        jnp.concatenate([up_low, up_high], axis=1),
        tail[1 : up_rows + 1].reshape(-1),
        jnp.concatenate([down_low, down_high], axis=0),
        tail[up_rows + 4],
        tail[up_rows + 5],
        tail[up_rows + 6],
    )


def solution(mesh):
    placed = (
        P("dp", None),
        P("dp", None),
        P("dp", None),
        P(None, "tensor"),
        P(None, "tensor"),
        P(None, "tensor"),
        P("tensor"),
        P("tensor"),
        P("tensor", None),
        P(),
        P(),
        P(),
        P(None, "tensor"),
        P("tensor"),
        P("tensor", None),
        P(),
        P(),
        P(),
    )
    counts = (mesh.shape["dp"], mesh.shape["tensor"])

    def on_device(*args):
        return local(*counts, *args)

    return jax.shard_map(
        on_device,
        mesh=mesh,
        in_specs=placed,
        out_specs=(
            P("dp", None),
            P("dp", None),
            P(None, "tensor"),
            P(None, "tensor"),
            P(None, "tensor"),
            P("tensor"),
            P("tensor"),
            P("tensor", None),
            P(),
            P(),
            P(),
            P(None, "tensor"),
            P("tensor"),
            P("tensor", None),
            P(),
            P(),
            P(),
        ),
        check_vma=False,
    )
```

time: 571 us -> 450 us (0.79); the launches traced: 560 us -> 448 us
  matrix products: 182 us -> 0 us
  Pallas kernels: 0 us -> 85.3 us
  waiting for transfers between devices: 161 us -> 228 us
  other arithmetic: 89.7 us -> 28.9 us
  starting transfers between devices: 94.7 us -> 58 us
  local copies, waits for them, and re-layouts: 28.7 us -> 46.3 us
    dot_general x26 -> x0, matrix products: 182 us -> none  [the longest x1 35.8 us: local(): jnp.einsum('hqk,khd->qhd', back_scores, key_rows, preferred_element_type=...]
    pallas_call x0 -> x6, Pallas kernels: none -> 85.3 us  [the longest x1 26.7 us: attend_back(): pl.pallas_call(functools.partial(attend_back_kernel, key_widths(rows), le...]
    ppermute x24, waiting for transfers between devices: 110 us -> 145 us  [swap_bit(): return lax.ppermute(value, 'dp', [(i, i ^ 1 << bit) for i in range(count)])]
    reduce_sum x9 -> x0, other arithmetic: 31.8 us -> none  [the longest x1 11.3 us: local(): row_total = jnp.sum(exponents, axis=-1, keepdims=True)]
    ppermute x6, waiting for transfers between devices: 16.9 us -> 45.3 us  [line_sum(): value = value + lax.ppermute(value, 'dp', inward)]
    ppermute x6, starting transfers between devices: 46.5 us -> 21 us  [line_sum(): value = value + lax.ppermute(value, 'dp', inward)]
    unnamed x130 -> x106, local copies, waits for them, and re-layouts: 20.7 us -> 34 us
    ppermute x24, starting transfers between devices: 31.4 us -> 21.1 us  [swap_bit(): return lax.ppermute(value, 'dp', [(i, i ^ 1 << bit) for i in range(count)])]
  transfers between devices with their start and end apart: 46 -> 46, of which waited for: 21 -> 23; matrix products, arithmetic and copies ran while one was open for 36% -> 8% of each run, Pallas kernels for 0% -> 10%
where the time goes in v2:
time: 450 us; the launch traced here: 448 us
  waiting for transfers between devices  228 us (51%)
  Pallas kernels  85.3 us (19%)
  starting transfers between devices  58 us (13%)
  local copies, waits for them, and re-layouts  46.3 us (10%)
  other arithmetic  28.9 us (6%)
    ppermute x24, waiting for transfers between devices, swap_bit(): return lax.ppermute(value, 'dp', [(i, i ^ 1 << bit) for i in range(count)])  145 us
    ppermute x6, waiting for transfers between devices, line_sum(): value = value + lax.ppermute(value, 'dp', inward)  45.3 us
    unnamed x106, local copies, waits for them, and re-layouts  34 us
    ppermute x6, waiting for transfers between devices, line_sum(): ended = lax.ppermute(value, 'dp', outward)  27.4 us
    pallas_call x1, Pallas kernels, attend_back(): pl.pallas_call(functools.partial(attend_back_kernel, key_widths(rows), le...  26.7 us
    ppermute x24, starting transfers between devices, swap_bit(): return lax.ppermute(value, 'dp', [(i, i ^ 1 << bit) for i in range(count)])  21.1 us
    ppermute x6, starting transfers between devices, line_sum(): value = value + lax.ppermute(value, 'dp', inward)  21 us
    pallas_call x1, Pallas kernels, attend(): pl.pallas_call(functools.partial(attend_kernel, key_widths(rows), lengths...  20.5 us
  transfers between devices with their start and end apart: 46, of which 23 were waited for; matrix products, arithmetic and copies ran while one was open for 8% of the time, Pallas kernels for 10%

profile of v2, /device:TPU:0, one launch (start us, length us, event | category | flops | bytes accessed | tf_op | source)
XLA Modules:
  0.0 447.8 jit_solution(2048976611621150855)
XLA Ops:
  8.4 20.5 %attend.1 = (bf16[1024,384]{1,0:T(8,128)(2,1)S(1)}, bf16[1024,384]{1,0:T(8,128)(2,1)S(1)}, bf16[1024,384]{1,0:T(8,128)(2,1)S(1)}, bf16[1024,384]{1,0:T(8,128)(2,...) custom-call(s32[1,4]{1,0:T(1,128)S(1)} %copy-done.41, bf16[1024,768]{1,0:T(8,128)(2,1)S(1)} %copy-done, ...), custom_call_target="tpu_custom_call" | custom-call | tf_op jit(solution)/shard_map/attend/pallas_call | solution.py:406
  33.6 4.5 %collective-permute-done.other_ref = f32[1024,768]{1,0:T(8,128)S(1)} collective-permute-done((f32[1024,768]{1,0:T(8,128)S(1)}, f32[1024,768]{1,0:T(8,128)S(1)}, u32[]{:S(2)}, u32[]{:S(2)}) %collective-permute-start) | collective-permute-done | bytes 3145760 | tf_op jit(solution)/shard_map/ppermute | solution.py:583
  41.5 9.7 %feed.1 = (f32[1024,768]{1,0:T(8,128)S(1)}, bf16[1024,768]{1,0:T(8,128)(2,1)S(1)}, f32[1024,1536]{1,0:T(8,128)}, bf16[1024,1536]{1,0:T(8,128)(2,1)S(1)}, f32[1024,768]{1,0:T(8,128)}) custom-call(bf16[1024,768]{1,0:T(8,128)(2,1)S(1)} %copy-done.1, f32[1024,768]{1,0:T(8,128)} %copy-done.12, f32[1024,768]{1,0:T(8,128)} %copy-done.44, ...), custom_call_target="tpu_custom_call" | custom-call | tf_op jit(solution)/shard_map/feed/pallas_call | solution.py:480
  54.9 5.6 %collective-permute-done.1.other_ref = f32[1024,768]{1,0:T(8,128)} collective-permute-done((f32[1024,768]{1,0:T(8,128)}, f32[1024,768]{1,0:T(8,128)}, u32[]{:S(2)}, u32[]{:S(2)}) %collective-permute-start.1) | collective-permute-done | bytes 3145760 | tf_op jit(solution)/shard_map/ppermute | solution.py:583
  63.8 10.3 %second_norm.1 = (bf16[1024,768]{1,0:T(8,128)(2,1)}, f32[1024,768]{1,0:T(8,128)S(1)}, bf16[1024,768]{1,0:T(8,128)(2,1)S(1)}, f32[768,768]{1,0:T(8,128)S(1)}, f32...) custom-call(f32[1024,768]{1,0:T(8,128)S(1)} %copy-done.3, f32[1024,768]{1,0:T(8,128)} %get-tuple-element.46.own_ref, ...), custom_call_target="tpu_custom_call" | custom-call | tf_op jit(solution)/shard_map/second_norm/pallas_call | solution.py:510
  88.8 13.5 %feed_back.1 = (f32[1024,768]{1,0:T(8,128)}, f32[768,768]{1,0:T(8,128)S(1)}, f32[768,768]{1,0:T(8,128)S(1)}, f32[8,1536]{1,0:T(8,128)S(1)}) custom-call(bf16[1024,768]{1,0:T(8,128)(2,1)S(1)} %copy-done.31, f32[1024,1536]{1,0:T(8,128)} %get-tuple-element.50.inner_ref, bf16[1024,768]{1,0:T(8,128)(2,1)S(1)} %get-tuple-element.51.first_low_ref, ...), custom_call_target="tpu_custom_call" | custom-call | tf_op jit(solution)/shard_map/feed_back/pallas_call | solution.py:538
  115.8 18.9 %collective-permute-done.18 = f32[384,768]{1,0:T(8,128)} collective-permute-done((f32[384,768]{1,0:T(8,128)S(1)}, f32[384,768]{1,0:T(8,128)}, u32[]{:S(2)}, u32[]{:S(2)}) %collective-permute-start.18) | collective-permute-done | bytes 1179680 | tf_op jit(solution)/shard_map/ppermute | solution.py:587
  139.6 12.2 %collective-permute-done.33 = f32[192,768]{1,0:T(8,128)S(1)} collective-permute-done((f32[192,768]{1,0:T(8,128)S(1)}, f32[192,768]{1,0:T(8,128)S(1)}, u32[]{:S(2)}, u32[]{:S(2)}) %collective-permute-start.33) | collective-permute-done | bytes 589856 | tf_op jit(solution)/shard_map/ppermute | solution.py:587
  156.3 7.0 %collective-permute-done.19 = f32[192,768]{1,0:T(8,128)S(1)} collective-permute-done((f32[192,768]{1,0:T(8,128)S(1)}, f32[192,768]{1,0:T(8,128)S(1)}, u32[]{:S(2)}, u32[]{:S(2)}) %collective-permute-start.19) | collective-permute-done | bytes 589856 | tf_op jit(solution)/shard_map/ppermute | solution.py:587
  171.0 10.3 %collective-permute-done.41 = f32[192,768]{1,0:T(8,128)S(1)} collective-permute-done((f32[192,768]{1,0:T(8,128)S(1)}, f32[192,768]{1,0:T(8,128)S(1)}, u32[]{:S(2)}, u32[]{:S(2)}) %collective-permute-start.41) | collective-permute-done | bytes 589856 | tf_op jit(solution)/shard_map/ppermute | solution.py:617
  182.8 11.1 %collective-permute-done.20 = f32[192,768]{1,0:T(8,128)S(1)} collective-permute-done((f32[192,768]{1,0:T(8,128)S(1)}, f32[192,768]{1,0:T(8,128)S(1)}, u32[]{:S(2)}, u32[]{:S(2)}) %collective-permute-start.20) | collective-permute-done | bytes 589856 | tf_op jit(solution)/shard_map/ppermute | solution.py:617
  195.5 8.5 %collective-permute-done.27 = f32[192,768]{1,0:T(8,128)S(1)} collective-permute-done((f32[192,768]{1,0:T(8,128)S(1)}, f32[192,768]{1,0:T(8,128)S(1)}, u32[]{:S(2)}, u32[]{:S(2)}) %collective-permute-start.27) | collective-permute-done | bytes 589856 | tf_op jit(solution)/shard_map/ppermute | solution.py:617
  221.4 4.6 %first_norm_back.1 = (f32[1024,768]{1,0:T(8,128)S(1)}, bf16[1024,768]{1,0:T(8,128)(2,1)S(1)}, f32[8,768]{1,0:T(8,128)S(1)}) custom-call(f32[1024,768]{1,0:T(8,128)S(1)} %copy-done.4, f32[1024,768]{1,0:T(8,128)S(1)} %copy-done.11, f32[1024,768]{1,0:T(8,128)} %collective-permute-done.2.other_ref, f32[1024,768]{1,0:T(8,128)S(1)} %copy-done.10, ...), custom_call_target="tpu_custom_call" | custom-call | tf_op jit(solution)/shard_map/first_norm_back/pallas_call | solution.py:567
  226.2 26.7 %attend_back.1 = (f32[768,768]{1,0:T(8,128)}, f32[800,768]{1,0:T(8,128)}, f32[1024,768]{1,0:T(8,128)}) custom-call(s32[1,4]{1,0:T(1,128)S(1)} %copy-done.42, bf16[1024,768]{1,0:T(8,128)(2,1)S(1)} %get-tuple-element.54.back_attn_ref, bf16[384,768]{1,0:T(8,128)(2,1)S(1)} %copy-done.21, bf16[1024,384]{1,0:T(8,128)(2,1)S(1)} %copy-done.34, ...), custom_call_target="tpu_custom_call" | custom-call | tf_op jit(solution)/shard_map/attend_back/pallas_call | solution.py:442
  263.6 33.5 %collective-permute-done.37 = f32[192,768]{1,0:T(8,128)S(1)} collective-permute-done((f32[192,768]{1,0:T(8,128)S(1)}, f32[192,768]{1,0:T(8,128)S(1)}, u32[]{:S(2)}, u32[]{:S(2)}) %collective-permute-start.37) | collective-permute-done | bytes 589856 | tf_op jit(solution)/shard_map/ppermute | solution.py:587
  302.0 17.6 %collective-permute-done.5 = f32[192,768]{1,0:T(8,128)S(1)} collective-permute-done((f32[192,768]{1,0:T(8,128)S(1)}, f32[192,768]{1,0:T(8,128)S(1)}, u32[]{:S(2)}, u32[]{:S(2)}) %collective-permute-start.5) | collective-permute-done | bytes 589856 | tf_op jit(solution)/shard_map/ppermute | solution.py:587
  319.9 24.3 %collective-permute-done.12 = f32[200,768]{1,0:T(8,128)S(1)} collective-permute-done((f32[200,768]{1,0:T(8,128)S(1)}, f32[200,768]{1,0:T(8,128)S(1)}, u32[]{:S(2)}, u32[]{:S(2)}) %collective-permute-start.12) | collective-permute-done | bytes 614432 | tf_op jit(solution)/shard_map/ppermute | solution.py:587
  344.3 10.5 %collective-permute-start.6 = (f32[192,768]{1,0:T(8,128)S(1)}, f32[192,768]{1,0:T(8,128)S(1)}, u32[]{:S(2)}, u32[]{:S(2)}) collective-permute-start(f32[192,768]{1,0:T(8,128)S(1)} %dynamic-slice_add_fusion.11), channel_id=1, source_target_pairs={{0,8},{24,16},{2,10},{26,18},{4,12},{28,20},{6,14},{30,22},{1,9},{... | collective-permute-start | bytes 1769480 | tf_op jit(solution)/shard_map/ppermute | solution.py:617
  356.8 10.3 %collective-permute-done.6 = f32[192,768]{1,0:T(8,128)S(1)} collective-permute-done((f32[192,768]{1,0:T(8,128)S(1)}, f32[192,768]{1,0:T(8,128)S(1)}, u32[]{:S(2)}, u32[]{:S(2)}) %collective-permute-start.6) | collective-permute-done | bytes 589856 | tf_op jit(solution)/shard_map/ppermute | solution.py:617
  369.0 4.6 %collective-permute-done.13 = f32[200,768]{1,0:T(8,128)S(1)} collective-permute-done((f32[200,768]{1,0:T(8,128)S(1)}, f32[200,768]{1,0:T(8,128)S(1)}, u32[]{:S(2)}, u32[]{:S(2)}) %collective-permute-start.13) | collective-permute-done | bytes 614432 | tf_op jit(solution)/shard_map/ppermute | solution.py:617
  381.2 20.4 %collective-permute-done.8 = f32[192,768]{1,0:T(8,128)} collective-permute-done((f32[192,768]{1,0:T(8,128)S(1)}, f32[192,768]{1,0:T(8,128)}, u32[]{:S(2)}, u32[]{:S(2)}) %collective-permute-start.8) | collective-permute-done | bytes 589856 | tf_op jit(solution)/shard_map/ppermute | solution.py:619
  403.0 5.1 %collective-permute-done.15 = f32[200,768]{1,0:T(8,128)S(1)} collective-permute-done((f32[200,768]{1,0:T(8,128)S(1)}, f32[200,768]{1,0:T(8,128)S(1)}, u32[]{:S(2)}, u32[]{:S(2)}) %collective-permute-start.15) | collective-permute-done | bytes 614432 | tf_op jit(solution)/shard_map/ppermute | solution.py:619
  413.9 11.1 %collective-permute-done.16 = f32[200,768]{1,0:T(8,128)S(1)} collective-permute-done((f32[200,768]{1,0:T(8,128)S(1)}, f32[200,768]{1,0:T(8,128)S(1)}, u32[]{:S(2)}, u32[]{:S(2)}) %collective-permute-start.16) | collective-permute-done | bytes 614432 | tf_op jit(solution)/shard_map/ppermute | solution.py:587
  429.8 12.1 %collective-permute-done.10 = f32[384,768]{1,0:T(8,128)S(1)} collective-permute-done((f32[384,768]{1,0:T(8,128)S(1)}, f32[384,768]{1,0:T(8,128)S(1)}, u32[]{:S(2)}, u32[]{:S(2)}) %collective-permute-start.10) | collective-permute-done | bytes 1179680 | tf_op jit(solution)/shard_map/ppermute | solution.py:587
  (266 shorter events, 133.3 us)
Async XLA Ops:
  104.6 30.1 %collective-permute-start.18 = (f32[384,768]{1,0:T(8,128)S(1)}, f32[384,768]{1,0:T(8,128)}, u32[]{:S(2)}, u32[]{:S(2)}) collective-permute-start(f32[384,768]{1,0:T(8,128)S(1)} %constant_dynamic-slice_fusion.7), channel_id=1, source_target_pairs={{0,2},{2,0},{4,6},{6,4},{8,10},{10,8},{12,14},{14,12},{16,18},{18,... | collective-permute-start | bytes 3538952 | tf_op jit(solution)/shard_map/ppermute | solution.py:587
  106.6 32.6 %collective-permute-start.25 = (f32[384,768]{1,0:T(8,128)S(1)}, f32[384,768]{1,0:T(8,128)S(1)}, u32[]{:S(2)}, u32[]{:S(2)}) collective-permute-start(f32[384,768]{1,0:T(8,128)S(1)} %constant_dynamic-slice_fusion.5), channel_id=1, source_target_pairs={{0,4},{2,6},{4,0},{6,2},{8,12},{10,14},{12,8},{14,10},{16,20},{18,... | collective-permute-start | bytes 3538952 | tf_op jit(solution)/shard_map/ppermute | solution.py:587
  107.3 110.2 %collective-permute-start.2 = (f32[1024,768]{1,0:T(8,128)}, f32[1024,768]{1,0:T(8,128)}, u32[]{:S(2)}, u32[]{:S(2)}) collective-permute-start(f32[1024,768]{1,0:T(8,128)} %get-tuple-element.52.own_ref), channel_id=1, source_target_pairs={{0,1},{1,0},{2,3},{3,2},{4,5},{5,4},{6,7},{7,6},{8,9},{9,8},{10,11... | collective-permute-start | bytes 9437192 | tf_op jit(solution)/shard_map/ppermute | solution.py:583
  111.1 40.8 %collective-permute-start.33 = (f32[192,768]{1,0:T(8,128)S(1)}, f32[192,768]{1,0:T(8,128)S(1)}, u32[]{:S(2)}, u32[]{:S(2)}) collective-permute-start(f32[192,768]{1,0:T(8,128)S(1)} %constant_dynamic-slice_fusion.2), channel_id=1, source_target_pairs={{0,4},{2,6},{4,0},{6,2},{8,12},{10,14},{12,8},{14,10},{16,20},{18,... | collective-permute-start | bytes 1769480 | tf_op jit(solution)/shard_map/ppermute | solution.py:587
  115.7 39.2 %collective-permute-start.40 = (f32[192,768]{1,0:T(8,128)S(1)}, f32[192,768]{1,0:T(8,128)S(1)}, u32[]{:S(2)}, u32[]{:S(2)}) collective-permute-start(f32[192,768]{1,0:T(8,128)S(1)} %constant_dynamic-slice_fusion), channel_id=1, source_target_pairs={{0,2},{2,0},{4,6},{6,4},{8,10},{10,8},{12,14},{14,12},{16,18},{18,... | collective-permute-start | bytes 1769480 | tf_op jit(solution)/shard_map/ppermute | solution.py:587
  163.4 30.5 %collective-permute-start.20 = (f32[192,768]{1,0:T(8,128)S(1)}, f32[192,768]{1,0:T(8,128)S(1)}, u32[]{:S(2)}, u32[]{:S(2)}) collective-permute-start(f32[192,768]{1,0:T(8,128)S(1)} %dynamic-slice_add_fusion.10), channel_id=1, source_target_pairs={{0,8},{24,16},{2,10},{26,18},{4,12},{28,20},{6,14},{30,22},{1,9},{... | collective-permute-start | bytes 1769480 | tf_op jit(solution)/shard_map/ppermute | solution.py:617
  166.8 37.2 %collective-permute-start.27 = (f32[192,768]{1,0:T(8,128)S(1)}, f32[192,768]{1,0:T(8,128)S(1)}, u32[]{:S(2)}, u32[]{:S(2)}) collective-permute-start(f32[192,768]{1,0:T(8,128)S(1)} %dynamic-slice_add_fusion.9), channel_id=1, source_target_pairs={{0,8},{24,16},{2,10},{26,18},{4,12},{28,20},{6,14},{30,22},{1,9},{... | collective-permute-start | bytes 1769480 | tf_op jit(solution)/shard_map/ppermute | solution.py:617
  169.5 36.9 %collective-permute-start.35 = (f32[192,768]{1,0:T(8,128)}, f32[192,768]{1,0:T(8,128)}, u32[]{:S(2)}, u32[]{:S(2)}) collective-permute-start(f32[192,768]{1,0:T(8,128)} %add.161), channel_id=1, source_target_pairs={{8,16},{16,8},{10,18},{18,10},{12,20},{20,12},{14,22},{22,14},{9,1... | collective-permute-start | bytes 1769480 | tf_op jit(solution)/shard_map/ppermute | solution.py:618
  208.5 46.7 %collective-permute-start.36 = (f32[192,768]{1,0:T(8,128)}, f32[192,768]{1,0:T(8,128)}, u32[]{:S(2)}, u32[]{:S(2)}) collective-permute-start(f32[192,768]{1,0:T(8,128)} %add.162), channel_id=1, source_target_pairs={{8,0},{16,24},{10,2},{18,26},{12,4},{20,28},{14,6},{22,30},{9,1},{... | collective-permute-start | bytes 1769480 | tf_op jit(solution)/shard_map/ppermute | solution.py:619
  211.0 46.0 %collective-permute-start.43 = (f32[192,768]{1,0:T(8,128)S(1)}, f32[192,768]{1,0:T(8,128)S(1)}, u32[]{:S(2)}, u32[]{:S(2)}) collective-permute-start(f32[192,768]{1,0:T(8,128)S(1)} %add.166), channel_id=1, source_target_pairs={{8,0},{16,24},{10,2},{18,26},{12,4},{20,28},{14,6},{22,30},{9,1},{... | collective-permute-start | bytes 1769480 | tf_op jit(solution)/shard_map/ppermute | solution.py:619
  213.6 44.8 %collective-permute-start.22 = (f32[192,768]{1,0:T(8,128)S(1)}, f32[192,768]{1,0:T(8,128)S(1)}, u32[]{:S(2)}, u32[]{:S(2)}) collective-permute-start(f32[192,768]{1,0:T(8,128)S(1)} %add.150), channel_id=1, source_target_pairs={{8,0},{16,24},{10,2},{18,26},{12,4},{20,28},{14,6},{22,30},{9,1},{... | collective-permute-start | bytes 1769480 | tf_op jit(solution)/shard_map/ppermute | solution.py:619
  216.2 45.9 %collective-permute-start.29 = (f32[192,768]{1,0:T(8,128)S(1)}, f32[192,768]{1,0:T(8,128)S(1)}, u32[]{:S(2)}, u32[]{:S(2)}) collective-permute-start(f32[192,768]{1,0:T(8,128)S(1)} %add.158), channel_id=1, source_target_pairs={{8,0},{16,24},{10,2},{18,26},{12,4},{20,28},{14,6},{22,30},{9,1},{... | collective-permute-start | bytes 1769480 | tf_op jit(solution)/shard_map/ppermute | solution.py:619
  254.4 45.1 %collective-permute-start.11 = (f32[400,768]{1,0:T(8,128)S(1)}, f32[400,768]{1,0:T(8,128)S(1)}, u32[]{:S(2)}, u32[]{:S(2)}) collective-permute-start(f32[400,768]{1,0:T(8,128)S(1)} %constant_dynamic-slice_fusion.9), channel_id=1, source_target_pairs={{0,4},{2,6},{4,0},{6,2},{8,12},{10,14},{12,8},{14,10},{16,20},{18,... | collective-permute-start | bytes 3686408 | tf_op jit(solution)/shard_map/ppermute | solution.py:587
  255.2 42.5 %collective-permute-start.4 = (f32[384,768]{1,0:T(8,128)S(1)}, f32[384,768]{1,0:T(8,128)S(1)}, u32[]{:S(2)}, u32[]{:S(2)}) collective-permute-start(f32[384,768]{1,0:T(8,128)S(1)} %constant_dynamic-slice_fusion.11), channel_id=1, source_target_pairs={{0,2},{2,0},{4,6},{6,4},{8,10},{10,8},{12,14},{14,12},{16,18},{18,... | collective-permute-start | bytes 3538952 | tf_op jit(solution)/shard_map/ppermute | solution.py:587
  257.0 40.1 %collective-permute-start.37 = (f32[192,768]{1,0:T(8,128)S(1)}, f32[192,768]{1,0:T(8,128)S(1)}, u32[]{:S(2)}, u32[]{:S(2)}) collective-permute-start(f32[192,768]{1,0:T(8,128)S(1)} %broadcast_select_fusion.20), channel_id=1, source_target_pairs={{0,4},{2,6},{4,0},{6,2},{8,12},{10,14},{12,8},{14,10},{16,20},{18,... | collective-permute-start | bytes 1769480 | tf_op jit(solution)/shard_map/ppermute | solution.py:587
  258.4 42.9 %collective-permute-start.44 = (f32[192,768]{1,0:T(8,128)S(1)}, f32[192,768]{1,0:T(8,128)S(1)}, u32[]{:S(2)}, u32[]{:S(2)}) collective-permute-start(f32[192,768]{1,0:T(8,128)S(1)} %broadcast_select_fusion.19), channel_id=1, source_target_pairs={{0,2},{2,0},{4,6},{6,4},{8,10},{10,8},{12,14},{14,12},{16,18},{18,... | collective-permute-start | bytes 1769480 | tf_op jit(solution)/shard_map/ppermute | solution.py:587
  262.1 92.8 %collective-permute-start.23 = (f32[192,768]{1,0:T(8,128)S(1)}, f32[192,768]{1,0:T(8,128)S(1)}, u32[]{:S(2)}, u32[]{:S(2)}) collective-permute-start(f32[192,768]{1,0:T(8,128)S(1)} %broadcast_select_fusion.22), channel_id=1, source_target_pairs={{0,4},{2,6},{4,0},{6,2},{8,12},{10,14},{12,8},{14,10},{16,20},{18,... | collective-permute-start | bytes 1769480 | tf_op jit(solution)/shard_map/ppermute | solution.py:587
  297.1 59.5 %collective-permute-start.30 = (f32[192,768]{1,0:T(8,128)S(1)}, f32[192,768]{1,0:T(8,128)S(1)}, u32[]{:S(2)}, u32[]{:S(2)}) collective-permute-start(f32[192,768]{1,0:T(8,128)S(1)} %broadcast_select_fusion.21), channel_id=1, source_target_pairs={{0,2},{2,0},{4,6},{6,4},{8,10},{10,8},{12,14},{14,12},{16,18},{18,... | collective-permute-start | bytes 1769480 | tf_op jit(solution)/shard_map/ppermute | solution.py:587
  297.7 77.1 %collective-permute-start.38 = (f32[384,768]{1,0:T(8,128)S(1)}, f32[384,768]{1,0:T(8,128)S(1)}, u32[]{:S(2)}, u32[]{:S(2)}) collective-permute-start(f32[384,768]{1,0:T(8,128)S(1)} %pad_maximum_fusion.7), channel_id=1, source_target_pairs={{0,2},{2,0},{4,6},{6,4},{8,10},{10,8},{12,14},{14,12},{16,18},{18,... | collective-permute-start | bytes 3538952 | tf_op jit(solution)/shard_map/ppermute | solution.py:587
  301.3 43.0 %collective-permute-start.12 = (f32[200,768]{1,0:T(8,128)S(1)}, f32[200,768]{1,0:T(8,128)S(1)}, u32[]{:S(2)}, u32[]{:S(2)}) collective-permute-start(f32[200,768]{1,0:T(8,128)S(1)} %constant_dynamic-slice_fusion.8), channel_id=1, source_target_pairs={{0,2},{2,0},{4,6},{6,4},{8,10},{10,8},{12,14},{14,12},{16,18},{18,... | collective-permute-start | bytes 1843208 | tf_op jit(solution)/shard_map/ppermute | solution.py:587
  319.6 56.2 %collective-permute-start.45 = (f32[384,768]{1,0:T(8,128)S(1)}, f32[384,768]{1,0:T(8,128)S(1)}, u32[]{:S(2)}, u32[]{:S(2)}) collective-permute-start(f32[384,768]{1,0:T(8,128)S(1)} %pad_maximum_fusion.8), channel_id=1, source_target_pairs={{0,4},{2,6},{4,0},{6,2},{8,12},{10,14},{12,8},{14,10},{16,20},{18,... | collective-permute-start | bytes 3538952 | tf_op jit(solution)/shard_map/ppermute | solution.py:587
  356.7 71.5 %collective-permute-start.3 = (f32[1024,768]{1,0:T(8,128)S(1)}, f32[1024,768]{1,0:T(8,128)S(1)}, u32[]{:S(2)}, u32[]{:S(2)}) collective-permute-start(f32[1024,768]{1,0:T(8,128)S(1)} %copy-done.43), channel_id=1, source_target_pairs={{0,1},{1,0},{2,3},{3,2},{4,5},{5,4},{6,7},{7,6},{8,9},{9,8},{10,11... | collective-permute-start | bytes 9437192 | tf_op jit(solution)/shard_map/ppermute | solution.py:583
  375.7 33.6 %collective-permute-start.31 = (f32[384,768]{1,0:T(8,128)S(1)}, f32[384,768]{1,0:T(8,128)S(1)}, u32[]{:S(2)}, u32[]{:S(2)}) collective-permute-start(f32[384,768]{1,0:T(8,128)S(1)} %pad_maximum_fusion.6), channel_id=1, source_target_pairs={{0,4},{2,6},{4,0},{6,2},{8,12},{10,14},{12,8},{14,10},{16,20},{18,... | collective-permute-start | bytes 3538952 | tf_op jit(solution)/shard_map/ppermute | solution.py:587
  377.4 30.7 %collective-permute-start.15 = (f32[200,768]{1,0:T(8,128)S(1)}, f32[200,768]{1,0:T(8,128)S(1)}, u32[]{:S(2)}, u32[]{:S(2)}) collective-permute-start(f32[200,768]{1,0:T(8,128)S(1)} %add.146), channel_id=1, source_target_pairs={{8,0},{16,24},{10,2},{18,26},{12,4},{20,28},{14,6},{22,30},{9,1},{... | collective-permute-start | bytes 1843208 | tf_op jit(solution)/shard_map/ppermute | solution.py:619
  (75 other events, 740.3 us)

commit v3 on v2

--- a/solution.py
+++ b/solution.py
@@ -71,6 +71,12 @@
 
 def merge_heads(turned):
     return jnp.concatenate([turned[:DH, :LANES], turned[DH:, LANES:]], axis=0).T
+
+
+def put_halves(sent_ref, kept_ref, sums, mine):
+    rows = sent_ref.shape[0]
+    sent_ref[...] = sums[pl.ds(pl.multiple_of((1 - mine) * rows, 8), rows), :]
+    kept_ref[...] = sums[pl.ds(pl.multiple_of(mine * rows, 8), rows), :]
 
 
 def over_query_blocks(ends, rows, widths, body):
@@ -141,6 +147,7 @@
     widths,
     seqs,
     lengths_ref,
+    bits_ref,
     back_attn_ref,
     out_weight_ref,
     queries_ref,
@@ -153,9 +160,13 @@
     k_weight_ref,
     v_weight_ref,
     small_ref,
+    first_sent_ref,
+    first_kept_ref,
+    second_sent_ref,
+    second_kept_ref,
+    partial_ref,
     first_pack_ref,
     second_pack_ref,
-    partial_ref,
     back_context_ref,
     turned_ref,
     back_queries_ref,
@@ -203,19 +214,32 @@
     back_values = back_values_ref[...].astype(jnp.bfloat16)
     first_pack_ref[:, :width_here] = contract(tokens, back_queries, 0, 0)
     first_pack_ref[:, width_here:] = contract(tokens, back_keys, 0, 0)
+    put_halves(first_sent_ref, first_kept_ref, first_pack_ref, bits_ref[0, 0])
     grad_values = contract(tokens, back_values, 0, 0)
-    second_pack_ref[:width_here, :] = contract(context_ref[...], back_attn_ref[...], 0, 0)
-    half = model // 2
-    second_pack_ref[width_here : width_here + half, :width_here] = grad_values[:half]
-    second_pack_ref[width_here : width_here + half, width_here:] = grad_values[half:]
-    second_pack_ref[width_here + half :, :] = small_ref[...]
-    top = width_here + half
-    second_pack_ref[top : top + 1, :width_here] = jnp.sum(
-        back_queries.astype(jnp.float32), axis=0, keepdims=True
-    )
-    second_pack_ref[top : top + 1, width_here:] = jnp.sum(
-        back_values.astype(jnp.float32), axis=0, keepdims=True
-    )
+    grad_out = contract(context_ref[...], back_attn_ref[...], 0, 0)
+    out_half, value_half, small_half = width_here // 2, model // 4, small_ref.shape[0] // 2
+    top = 0
+    for at in range(2):
+        second_pack_ref[top : top + out_half, :] = grad_out[at * out_half : (at + 1) * out_half]
+        top += out_half
+        for side in range(2):
+            start = side * (model // 2) + at * value_half
+            second_pack_ref[
+                top : top + value_half, side * width_here : (side + 1) * width_here
+            ] = grad_values[start : start + value_half]
+        top += value_half
+        second_pack_ref[top : top + small_half, :] = small_ref[
+            at * small_half : (at + 1) * small_half
+        ]
+        if at == 0:
+            second_pack_ref[top : top + 1, :width_here] = jnp.sum(
+                back_queries.astype(jnp.float32), axis=0, keepdims=True
+            )
+            second_pack_ref[top : top + 1, width_here:] = jnp.sum(
+                back_values.astype(jnp.float32), axis=0, keepdims=True
+            )
+        top += small_half
+    put_halves(second_sent_ref, second_kept_ref, second_pack_ref, bits_ref[0, 1])
     partial_ref[...] = (
         contract(back_queries, q_weight_ref[...], 1, 1)
         + contract(back_keys, k_weight_ref[...], 1, 1)
@@ -278,6 +302,7 @@
 
 
 def second_norm_kernel(
+    bits_ref,
     first_sum_ref,
     own_ref,
     other_ref,
@@ -291,9 +316,13 @@
     layer_out_ref,
     back_second_ref,
     back_down_ref,
+    low_sent_ref,
+    low_kept_ref,
+    high_sent_ref,
+    high_kept_ref,
+    sums_ref,
     grad_low_ref,
     grad_high_ref,
-    sums_ref,
 ):
     unit, unused = standardize(first_sum_ref[...])
     first = unit * first_gain_ref[...] + first_shift_ref[...]
@@ -316,17 +345,27 @@
     grad_high_ref[...] += contract(active_ref[:, half:], back_down, 0, 0)
     add_sums(sums_ref, (back_second, upstream * unit, upstream))
 
+    @pl.when(pl.program_id(0) == pl.num_programs(0) - 1)
+    def _():
+        put_halves(low_sent_ref, low_kept_ref, grad_low_ref, bits_ref[0, 0])
+        put_halves(high_sent_ref, high_kept_ref, grad_high_ref, bits_ref[0, 1])
+
 
 def feed_back_kernel(
+    bits_ref,
     back_down_ref,
     inner_ref,
     first_low_ref,
     down_weight_ref,
     up_weight_ref,
     partial_ref,
+    low_sent_ref,
+    low_kept_ref,
+    high_sent_ref,
+    high_kept_ref,
+    sums_ref,
     grad_low_ref,
     grad_high_ref,
-    sums_ref,
 ):
     inner = inner_ref[...]
     slope = 0.5 * (1.0 + lax.erf(inner * 0.7071067811865476)) + inner * (
@@ -346,6 +385,11 @@
     grad_low_ref[...] += contract(first_low, back_inner[:, :half], 0, 0)
     grad_high_ref[...] += contract(first_low, back_inner[:, half:], 0, 0)
     add_sums(sums_ref, (back_inner.astype(jnp.float32),))
+
+    @pl.when(pl.program_id(0) == pl.num_programs(0) - 1)
+    def _():
+        put_halves(low_sent_ref, low_kept_ref, grad_low_ref, bits_ref[0, 0])
+        put_halves(high_sent_ref, high_kept_ref, grad_high_ref, bits_ref[0, 1])
 
 
 def first_norm_kernel(
@@ -374,10 +418,6 @@
     return pl.BlockSpec((ROW_BLOCK, columns), lambda step: (step, 0))
 
 
-def whole(shape):
-    return pl.BlockSpec(shape, lambda *step: (0, 0))
-
-
 def held(shape):
     return pl.BlockSpec(shape, lambda *step: (0, 0), pipeline_mode=pl.Buffered(1))
 
@@ -392,6 +432,14 @@
 
 def params(mebibytes):
     return pltpu.CompilerParams(vmem_limit_bytes=mebibytes * MIB)
+
+
+def lasting(microseconds):
+    return pl.CostEstimate(
+        flops=int(microseconds * 1.1e9),
+        transcendentals=0,
+        bytes_accessed=int(microseconds * 1e6),
+    )
 
 
 def key_widths(rows):
@@ -416,13 +464,15 @@
         in_specs=[in_smem()] + [in_vmem()] * 7,
         out_specs=(in_vmem(),) * 6,
         scratch_shapes=[pltpu.VMEM((width, rows), jnp.bfloat16)],
-        compiler_params=params(40),
+        compiler_params=params(60),
+        cost_estimate=lasting(20),
         name="attend",
     )(lengths, tokens, q_weight, k_weight, v_weight, q_bias, v_bias, out_weight)
 
 
 def attend_back(
     lengths,
+    bits,
     back_attn,
     out_weight,
     queries,
@@ -442,23 +492,29 @@
     return pl.pallas_call(
         functools.partial(attend_back_kernel, key_widths(rows), lengths.shape[1]),
         out_shape=(
-            struct((model, 2 * width), jnp.float32),
-            struct((pack_rows, model), jnp.float32),
+            struct((model // 2, 2 * width), jnp.float32),
+            struct((model // 2, 2 * width), jnp.float32),
+            struct((pack_rows // 2, model), jnp.float32),
+            struct((pack_rows // 2, model), jnp.float32),
             struct((rows, model), jnp.float32),
         ),
-        in_specs=[in_smem()] + [in_vmem()] * 12,
-        out_specs=(in_vmem(),) * 3,
+        in_specs=[in_smem()] * 2 + [in_vmem()] * 12,
+        out_specs=(in_vmem(),) * 5,
         scratch_shapes=[
+            pltpu.VMEM((model, 2 * width), jnp.float32),
+            pltpu.VMEM((pack_rows, model), jnp.float32),
             pltpu.VMEM((rows, width), jnp.bfloat16),
             pltpu.VMEM((width, rows), jnp.bfloat16),
             pltpu.VMEM((rows, width), jnp.bfloat16),
             pltpu.VMEM((rows, width), jnp.float32),
             pltpu.VMEM((rows, width), jnp.float32),
         ],
-        compiler_params=params(44),
+        compiler_params=params(60),
+        cost_estimate=lasting(27),
         name="attend_back",
     )(
         lengths,
+        bits,
         back_attn,
         out_weight,
         queries,
@@ -497,13 +553,14 @@
             by_rows(hidden),
             by_rows(model),
         ),
-        compiler_params=params(40),
+        compiler_params=params(60),
+        cost_estimate=lasting(10),
         name="feed",
     )(tokens, own, other, out_bias, gain, shift, up_weight, up_bias, down_weight)
 
 
 def second_norm(
-    first_sum, own, other, cotangent, active, first_gain, first_shift, down_bias, gain, shift
+    bits, first_sum, own, other, cotangent, active, first_gain, first_shift, down_bias, gain, shift
 ):
     rows, model = first_sum.shape
     hidden = active.shape[1]
@@ -514,25 +571,31 @@
             struct((rows, model), jnp.bfloat16),
             struct((rows, model), jnp.float32),
             struct((rows, model), jnp.bfloat16),
-            struct((hidden // 2, model), jnp.float32),
-            struct((hidden // 2, model), jnp.float32),
+            struct((hidden // 4, model), jnp.float32),
+            struct((hidden // 4, model), jnp.float32),
+            struct((hidden // 4, model), jnp.float32),
+            struct((hidden // 4, model), jnp.float32),
             struct((8, model), jnp.float32),
         ),
-        in_specs=[by_rows(model)] * 4 + [by_rows(hidden)] + [held((1, model))] * 5,
+        in_specs=[in_smem()] + [by_rows(model)] * 4 + [by_rows(hidden)] + [held((1, model))] * 5,
         out_specs=(
             by_rows(model),
             by_rows(model),
             by_rows(model),
-            whole((hidden // 2, model)),
-            whole((hidden // 2, model)),
-            whole((8, model)),
+            held((hidden // 4, model)),
+            held((hidden // 4, model)),
+            held((hidden // 4, model)),
+            held((hidden // 4, model)),
+            held((8, model)),
         ),
-        compiler_params=params(40),
+        scratch_shapes=[pltpu.VMEM((hidden // 2, model), jnp.float32)] * 2,
+        cost_estimate=lasting(10),
+        compiler_params=params(60),
         name="second_norm",
-    )(first_sum, own, other, cotangent, active, first_gain, first_shift, down_bias, gain, shift)
-
-
-def feed_back(back_down, inner, first_low, down_weight, up_weight):
+    )(bits, first_sum, own, other, cotangent, active, first_gain, first_shift, down_bias, gain, shift)
+
+
+def feed_back(bits, back_down, inner, first_low, down_weight, up_weight):
     rows, model = back_down.shape
     hidden = inner.shape[1]
     return pl.pallas_call(
@@ -540,11 +603,14 @@
         grid=(rows // ROW_BLOCK,),
         out_shape=(
             struct((rows, model), jnp.float32),
-            struct((model, hidden // 2), jnp.float32),
-            struct((model, hidden // 2), jnp.float32),
+            struct((model // 2, hidden // 2), jnp.float32),
+            struct((model // 2, hidden // 2), jnp.float32),
+            struct((model // 2, hidden // 2), jnp.float32),
+            struct((model // 2, hidden // 2), jnp.float32),
             struct((8, hidden), jnp.float32),
         ),
         in_specs=[
+            in_smem(),
             by_rows(model),
             by_rows(hidden),
             by_rows(model),
@@ -553,13 +619,17 @@
         ],
         out_specs=(
             by_rows(model),
-            whole((model, hidden // 2)),
-            whole((model, hidden // 2)),
-            whole((8, hidden)),
+            held((model // 2, hidden // 2)),
+            held((model // 2, hidden // 2)),
+            held((model // 2, hidden // 2)),
+            held((model // 2, hidden // 2)),
+            held((8, hidden)),
         ),
-        compiler_params=params(40),
+        scratch_shapes=[pltpu.VMEM((model, hidden // 2), jnp.float32)] * 2,
+        cost_estimate=lasting(13),
+        compiler_params=params(60),
         name="feed_back",
-    )(back_down, inner, first_low, down_weight, up_weight)
+    )(bits, back_down, inner, first_low, down_weight, up_weight)
 
 
 def first_norm_back(first_sum, own, other, back_second, gain):
@@ -573,63 +643,164 @@
             struct((8, model), jnp.float32),
         ),
         in_specs=[by_rows(model)] * 4 + [held((1, model))],
-        out_specs=(by_rows(model), by_rows(model), whole((8, model))),
-        compiler_params=params(32),
+        out_specs=(by_rows(model), by_rows(model), held((8, model))),
+        cost_estimate=lasting(5),
+        compiler_params=params(60),
         name="first_norm_back",
     )(first_sum, own, other, back_second, gain)
 
 
+def place_kernel(moves, starts_ref, *refs):
+    copies = []
+    inputs = 1 + max(source for source, *unused in moves)
+    for at, (source, rows, columns, target, row_start, column_start) in enumerate(moves):
+        start = row_start(starts_ref) if callable(row_start) else row_start
+        size = rows[1] - rows[0]
+        copies.append(
+            pltpu.make_async_copy(
+                refs[source].at[pl.ds(rows[0], size), pl.ds(columns[0], columns[1] - columns[0])],
+                refs[inputs + target].at[
+                    pl.ds(pl.multiple_of(start, 8), size),
+                    pl.ds(column_start, columns[1] - columns[0]),
+                ],
+                refs[-1].at[at],
+            )
+        )
+    for copy in copies:
+        copy.start()
+    for copy in copies:
+        copy.wait()
+
+
+def place_blocks(starts, operands, shapes, moves, name):
+    anywhere = pl.BlockSpec(memory_space=pl.ANY)
+    return pl.pallas_call(
+        functools.partial(place_kernel, moves),
+        out_shape=tuple(struct(shape, jnp.float32) for shape in shapes),
+        in_specs=[in_smem()] + [anywhere] * len(operands),
+        out_specs=(anywhere,) * len(shapes),
+        scratch_shapes=[pltpu.SemaphoreType.DMA((len(moves),))],
+        cost_estimate=lasting(2),
+        name=name,
+    )(starts, *operands)
+
+
+def at_bit(rows, bit, same):
+    def first(bits_ref):
+        return (bits_ref[0, bit] if same else 1 - bits_ref[0, bit]) * rows
+
+    return first
+
+
 def swap_cores(value, tensor_count):
     return lax.ppermute(value, "tensor", [(i, i ^ 1) for i in range(tensor_count)])
 
 
-def swap_bit(value, bit, count):
-    return lax.ppermute(value, "dp", [(i, i ^ (1 << bit)) for i in range(count)])
-
-
-def halve(value, bit, count, place):
-    rows = value.shape[0] // 2
-    mine = (place >> bit) & 1
-    sent = lax.dynamic_slice_in_dim(value, (1 - mine) * rows, rows, 0)
-    kept = lax.dynamic_slice_in_dim(value, mine * rows, rows, 0)
-    return kept + swap_bit(sent, bit, count)
-
-
-def join(value, bit, count, place):
-    other = swap_bit(value, bit, count)
-    mine = (place >> bit) & 1
-    first = jnp.where(mine == 0, value, other)
-    second = jnp.where(mine == 0, other, value)
-    return jnp.concatenate([first, second], axis=0)
-
-
-def line_sum(value, count, place):
-    stride = count // 4
-    inward = []
-    across = []
-    outward = []
-    for low in range(stride):
-        ring = [low + stride * at for at in range(4)]
-        inward += [(ring[0], ring[1]), (ring[3], ring[2])]
-        across += [(ring[1], ring[2]), (ring[2], ring[1])]
-        outward += [(ring[1], ring[0]), (ring[2], ring[3])]
-    at_line = place // stride
-    value = value + lax.ppermute(value, "dp", inward)
-    value = value + lax.ppermute(value, "dp", across)
-    ended = lax.ppermute(value, "dp", outward)
-    return jnp.where((at_line == 1) | (at_line == 2), value, ended)
-
-
-def all_sum(value, first_bit, count, place):
-    second_bit = 1 - first_bit
-    value = halve(value, first_bit, count, place)
-    value = halve(value, second_bit, count, place)
-    low_bits = (count // 4).bit_length() - 1
-    for bit in range(2, low_bits):
-        value = value + swap_bit(value, bit, count)
-    value = line_sum(value, count, place)
-    value = join(value, second_bit, count, place)
-    return join(value, first_bit, count, place)
+class Ring:
+    def __init__(self, count, place):
+        self.count = count
+        self.place = place
+        stride = count // 4
+        self.low_bits = stride.bit_length() - 1
+        self.inward, self.across, self.outward = [], [], []
+        for low in range(stride):
+            line = [low + stride * at for at in range(4)]
+            self.inward += [(line[0], line[1]), (line[3], line[2])]
+            self.across += [(line[1], line[2]), (line[2], line[1])]
+            self.outward += [(line[1], line[0]), (line[2], line[3])]
+        self.is_middle = (place // stride == 1) | (place // stride == 2)
+
+    def swap(self, value, bit):
+        return lax.ppermute(value, "dp", [(i, i ^ (1 << bit)) for i in range(self.count)])
+
+    def mine(self, bit):
+        return (self.place >> bit) & 1
+
+    def half(self, value, bit, same):
+        rows = value.shape[0] // 2
+        mine = self.mine(bit)
+        return lax.dynamic_slice_in_dim(value, (mine if same else 1 - mine) * rows, rows, 0)
+
+
+class Chunk:
+    def __init__(self, ring, bits, first_bit, sent, kept):
+        self.ring = ring
+        self.bits = bits
+        self.first_bit = first_bit
+        self.second_bit = 1 - first_bit
+        self.held = (kept,)
+        self.arriving = None
+        self.sent = sent
+        self.step = 0
+
+    def inputs(self):
+        return self.held + (() if self.arriving is None else (self.arriving,))
+
+    def join(self, value, arriving, bit):
+        rows, columns = value.shape
+        [joined] = place_blocks(
+            self.bits,
+            (value, arriving),
+            ((2 * rows, columns),),
+            (
+                (0, (0, rows), (0, columns), 0, at_bit(rows, bit, True), 0),
+                (1, (0, rows), (0, columns), 0, at_bit(rows, bit, False), 0),
+            ),
+            "join",
+        )
+        return joined
+
+    def advance(self, inputs):
+        ring = self.ring
+        step = self.step
+        self.step += 1
+        if step == 0:
+            self.arriving = ring.swap(self.sent, self.first_bit)
+            return None
+        if step == 1:
+            kept, arrived = inputs
+            bit = self.second_bit
+            sent = ring.half(kept, bit, False) + ring.half(arrived, bit, False)
+            self.held = (ring.half(kept, bit, True), ring.half(arrived, bit, True))
+            self.arriving = ring.swap(sent, bit)
+            return sent
+        if step == 2:
+            value = (inputs[0] + inputs[1]) + inputs[2]
+            for bit in range(2, ring.low_bits):
+                value = value + ring.swap(value, bit)
+            self.held = (value,)
+            self.arriving = lax.ppermute(value, "dp", ring.inward)
+            return value
+        value, arrived = inputs
+        if step == 3:
+            value = value + arrived
+            self.arriving = lax.ppermute(value, "dp", ring.across)
+        elif step == 4:
+            value = value + arrived
+            self.arriving = lax.ppermute(value, "dp", ring.outward)
+        elif step == 5:
+            value = jnp.where(ring.is_middle, value, arrived)
+            self.arriving = ring.swap(value, self.second_bit)
+        else:
+            value = self.join(value, arrived, self.second_bit)
+            self.arriving = ring.swap(value, self.first_bit)
+        self.held = (value,)
+        return value
+
+
+class Sequence:
+    def __init__(self):
+        self.last = None
+
+    def after(self, values):
+        if self.last is None:
+            return tuple(values)
+        held = lax.optimization_barrier((*values, self.last))
+        return held[:-1]
+
+    def ran(self, result):
+        if result is not None:
+            self.last = result
 
 
 def local(
@@ -655,6 +826,8 @@
     second_shift,
 ):
     place = lax.axis_index("dp")
+    ring = Ring(dp_count, place)
+    bits = jnp.stack([ring.mine(0), ring.mine(1)]).reshape(1, 2)
     model = q_weight.shape[0]
     width = q_weight.shape[1]
     hidden = up_weight.shape[1]
@@ -673,7 +846,8 @@
         row(up_bias),
         down_weight,
     )
-    layer_out, back_second, back_down, down_low, down_high, second_sums = second_norm(
+    layer_out, back_second, back_down, *down_halves, second_sums = second_norm(
+        bits,
         first_sum,
         down_part,
         swap_cores(down_part, tensor_count),
@@ -685,16 +859,34 @@
         row(second_gain),
         row(second_shift),
     )
-    down_low = all_sum(down_low, 0, dp_count, place)
-    down_high = all_sum(down_high, 1, dp_count, place)
-    back_part, up_low, up_high, up_sums = feed_back(
-        back_down, inner, first_low, down_weight, up_weight
-    )
-    up_low = all_sum(up_low, 0, dp_count, place)
-    up_high = all_sum(up_high, 1, dp_count, place)
+    order = Sequence()
+    order.ran(back_down)
+    chunks = {}
+
+    def begin(name, halves):
+        chunks[name + "0"] = Chunk(ring, bits, 0, *halves[:2])
+        chunks[name + "1"] = Chunk(ring, bits, 1, *halves[2:])
+
+    def run(*names):
+        for name in names:
+            chunk = chunks[name]
+            inputs = chunk.inputs()
+            order.ran(chunk.advance(order.after(inputs) if chunk.step else inputs))
+
+    begin("D", down_halves)
+    run("D1", "D0")
+    [back_down] = order.after((back_down,))
+    back_part, *up_halves, up_sums = feed_back(
+        bits, back_down, inner, first_low, down_weight, up_weight
+    )
+    order.ran(back_part)
+    begin("U", up_halves)
+    run("U1", "U0")
     back_first_sum, back_attn, first_sums = first_norm_back(
         first_sum, back_part, swap_cores(back_part, tensor_count), back_second, row(first_gain)
     )
+    order.ran(back_attn)
+    run("D1", "D0")
     small = jnp.concatenate(
         [
             jnp.zeros((1, model), jnp.float32),
@@ -704,8 +896,10 @@
         ]
     )
     small = jnp.pad(small, ((0, -small.shape[0] % 32), (0, 0)))
-    first_pack, second_pack, input_part = attend_back(
+    [back_attn] = order.after((back_attn,))
+    *attn_halves, input_part = attend_back(
         seq_lengths,
+        bits,
         back_attn,
         out_weight,
         queries,
@@ -719,29 +913,85 @@
         v_weight,
         small,
     )
-    first_pack = all_sum(first_pack, 0, dp_count, place)
-    second_pack = all_sum(second_pack, 1, dp_count, place)
-    grad_input = (
-        (input_part + swap_cores(input_part, tensor_count)) + back_first_sum
-    ).astype(jnp.bfloat16)
-    turned = second_pack[width : width + model // 2]
-    tail = second_pack[width + model // 2 :]
+    order.ran(input_part)
+    begin("A", attn_halves)
+    run("A1", "U1", "D0", "D1", "U0", "A0")
+    input_part, input_other = order.after((input_part, swap_cores(input_part, tensor_count)))
+    grad_input = ((input_part + input_other) + back_first_sum).astype(jnp.bfloat16)
+    order.ran(grad_input)
+    run("U1", "D0", "A1", "D1", "D0", "U0", "A0", "U1", "D1", "D0", "A1", "U0", "A0", "U1", "D1")
+    run("A1", "D0", "U0", "U1", "D1", "A0", "A1", "U0", "A0", "A1")
+
+    def finish(name, shapes, moves):
+        operands = ()
+        for chunk in (chunks[name + "0"], chunks[name + "1"]):
+            operands += order.after(chunk.inputs())
+        results = place_blocks(bits, operands, shapes, moves, "place")
+        order.ran(results[0])
+        return results
+
+    def halves_at(source, rows, columns, target, row_offset, column, bit, height):
+        moves = []
+        for same in (True, False):
+            first = at_bit(height, bit, same)
+            moves.append(
+                (
+                    source + (0 if same else 1),
+                    rows,
+                    columns,
+                    target,
+                    lambda ref, first=first: row_offset + first(ref),
+                    column,
+                )
+            )
+        return moves
+
+    half = hidden // 2
+    quarter = half // 2
+    [grad_down] = finish(
+        "D",
+        ((hidden, model),),
+        halves_at(0, (0, quarter), (0, model), 0, 0, 0, 0, quarter)
+        + halves_at(2, (0, quarter), (0, model), 0, half, 0, 1, quarter),
+    )
+    run("A0", "U1", "U0", "A1", "A0")
+    rows = model // 2
+    [grad_up] = finish(
+        "U",
+        ((model, hidden),),
+        halves_at(0, (0, rows), (0, half), 0, 0, 0, 0, rows)
+        + halves_at(2, (0, rows), (0, half), 0, 0, half, 1, rows),
+    )
+    out_half, value_half = width // 2, model // 4
+    tail_start = out_half + value_half
+    small_half = small.shape[0] // 2
+    square = (model, width)
+    grad_q, grad_k, grad_v, grad_out, tail = finish(
+        "A",
+        (square, square, square, (width, model), (2 * small_half, model)),
+        halves_at(0, (0, rows), (0, width), 0, 0, 0, 0, rows)
+        + halves_at(0, (0, rows), (width, 2 * width), 1, 0, 0, 0, rows)
+        + halves_at(2, (out_half, tail_start), (0, width), 2, 0, 0, 1, value_half)
+        + halves_at(2, (out_half, tail_start), (width, 2 * width), 2, rows, 0, 1, value_half)
+        + halves_at(2, (0, out_half), (0, model), 3, 0, 0, 1, out_half)
+        + halves_at(2, (tail_start, tail_start + small_half), (0, model), 4, 0, 0, 1, small_half),
+    )
     up_rows = hidden // model
     return (
         layer_out,
         grad_input,
-        first_pack[:, :width],
-        first_pack[:, width:],
-        jnp.concatenate([turned[:, :width], turned[:, width:]], axis=0),
+        grad_q,
+        grad_k,
+        grad_v,
         tail[0, :width],
         tail[0, width:],
-        second_pack[:width],
+        grad_out,
         tail[up_rows + 1],
         tail[up_rows + 2],
         tail[up_rows + 3],
-        jnp.concatenate([up_low, up_high], axis=1),
+        grad_up,
         tail[1 : up_rows + 1].reshape(-1),
-        jnp.concatenate([down_low, down_high], axis=0),
+        grad_down,
         tail[up_rows + 4],
         tail[up_rows + 5],
         tail[up_rows + 6],

time: 450 us -> 991 us (2.20)
  Pallas kernels: 85.3 us -> 768 us
  waiting for transfers between devices: 228 us -> 91.1 us
  local copies, waits for them, and re-layouts: 46.3 us -> 20.3 us
  starting transfers between devices: 58 us -> 73.5 us
    pallas_call x0 -> x9, Pallas kernels: none -> 664 us  [place_blocks(): pl.pallas_call(functools.partial(place_kernel, moves), out_shape=tuple((s...]
    ppermute x42, waiting for transfers between devices: 218 us -> 84.2 us  [the longest x24 67.1 us: swap(): lax.ppermute(value, 'dp', [(i, i ^ 1 << bit) for i in range(self.count)])]
    unnamed x106 -> x50, local copies, waits for them, and re-layouts: 34 us -> 7.28 us
    ppermute x42, starting transfers between devices: 57.2 us -> 72.2 us  [the longest x24 29.5 us: swap(): lax.ppermute(value, 'dp', [(i, i ^ 1 << bit) for i in range(self.count)])]
  transfers between devices with their start and end apart: 46 -> 46, of which waited for: 23 -> 14; matrix products, arithmetic and copies ran while one was open for 8% -> 4% of each run, Pallas kernels for 10% -> 53%
where the time goes in v3:
time: 991 us; the launch traced here: 990 us
  Pallas kernels  768 us (77%)
  waiting for transfers between devices  91.1 us (9%)
  starting transfers between devices  73.5 us (7%)
  other arithmetic  35.7 us (4%)
  local copies, waits for them, and re-layouts  20.3 us (2%)
    pallas_call x9, Pallas kernels, place_blocks(): pl.pallas_call(functools.partial(place_kernel, moves), out_shape=tuple((s...  664 us
    ppermute x24, waiting for transfers between devices, swap(): lax.ppermute(value, 'dp', [(i, i ^ 1 << bit) for i in range(self.count)])  67.1 us
    ppermute x24, starting transfers between devices, swap(): lax.ppermute(value, 'dp', [(i, i ^ 1 << bit) for i in range(self.count)])  29.5 us
    pallas_call x1, Pallas kernels, attend_back(): pl.pallas_call(functools.partial(attend_back_kernel, key_widths(rows), le...  28 us
    ppermute x6, starting transfers between devices, advance(): self.arriving = lax.ppermute(value, 'dp', ring.inward)  27.7 us
    pallas_call x1, Pallas kernels, attend(): pl.pallas_call(functools.partial(attend_kernel, key_widths(rows), lengths...  23.2 us
  transfers between devices with their start and end apart: 46, of which 14 were waited for; matrix products, arithmetic and copies ran while one was open for 4% of the time, Pallas kernels for 53%

profile of v3, /device:TPU:0, one launch (start us, length us, event | category | flops | bytes accessed | tf_op | source)
XLA Modules:
  0.0 989.6 jit_solution(17192050511149542257)
XLA Ops:
  3.2 23.2 %attend.1 = (bf16[1024,384]{1,0:T(8,128)(2,1)}, bf16[1024,384]{1,0:T(8,128)(2,1)}, bf16[1024,384]{1,0:T(8,128)(2,1)}, bf16[1024,384]{1,0:T(8,128)(2,1)}, f32[24,256]{1,0:T(8,128)}, /*index=5*/f32[1024,768]{1,0:T(8,128)}) custom-call(s32[1,4]{1,0:T(1,128)} %lengths_ref.3, bf16[1024,768]{1,0:T(8,128)(2,1)} %tokens_ref.5, bf16[768,384]{1,0:T(8,128)(2,1)} %q_weight_ref.3, ...), custom_call_target="tpu_custom_call" | custom-call | flops 22000001024 | bytes 20000000 | tf_op jit(solution)/shard_map/attend/pallas_call | solution.py:454
  34.0 12.8 %feed.1 = (f32[1024,768]{1,0:T(8,128)}, bf16[1024,768]{1,0:T(8,128)(2,1)}, f32[1024,1536]{1,0:T(8,128)}, bf16[1024,1536]{1,0:T(8,128)(2,1)}, f32[1024,768]{1,0:T(8,128)}) custom-call(bf16[1024,768]{1,0:T(8,128)(2,1)} %tokens_ref.5, f32[1024,768]{1,0:T(8,128)} %get-tuple-element.148.own_ref, f32[1024,768]{1,0:T(8,128)} %copy-done.22, ...), custom_call_target="tpu_custom_call" | custom-call | flops 11000000512 | bytes 10000000 | tf_op jit(solution)/shard_map/feed/pallas_call | solution.py:536
  54.3 13.9 %second_norm.1 = (bf16[1024,768]{1,0:T(8,128)(2,1)}, f32[1024,768]{1,0:T(8,128)}, bf16[1024,768]{1,0:T(8,128)(2,1)}, f32[384,768]{1,0:T(8,128)}, f32[384,768]{1,...) custom-call(s32[1,2]{1,0:T(1,128)} %add_bitcast_fusion.bits_ref.starts_ref, ...), custom_call_target="tpu_custom_call" | custom-call | flops 11000000512 | bytes 10000000 | tf_op jit(solution)/shard_map/second_norm/pallas_call | solution.py:567
  68.3 17.8 %feed_back.1 = (f32[1024,768]{1,0:T(8,128)}, f32[384,768]{1,0:T(8,128)}, f32[384,768]{1,0:T(8,128)}, f32[384,768]{1,0:T(8,128)}, f32[384,768]{1,0:T(8,128)}, /*index=5*/f32[8,1536]{1,0:T(8,128)}) custom-call(s32[1,2]{1,0:T(1,128)} %add_bitcast_fusion.bits_ref.starts_ref, bf16[1024,768]{1,0:T(8,128)(2,1)} %get-tuple-element.153.back_down_ref, ...), custom_call_target="tpu_custom_call" | custom-call | flops 14300000256 | bytes 13000000 | tf_op jit(solution)/shard_map/feed_back/pallas_call | solution.py:601
  92.2 8.1 first_norm_back.1
  101.7 15.6 %collective-permute-done.4 = f32[384,768]{1,0:T(8,128)} collective-permute-done((f32[384,768]{1,0:T(8,128)}, f32[384,768]{1,0:T(8,128)}, u32[]{:S(2)}, u32[]{:S(2)}) %collective-permute-start.4) | collective-permute-done | bytes 1179680 | tf_op jit(solution)/shard_map/ppermute | solution.py:714
  120.6 28.0 %attend_back.1 = (f32[384,768]{1,0:T(8,128)}, f32[384,768]{1,0:T(8,128)}, f32[400,768]{1,0:T(8,128)}, f32[400,768]{1,0:T(8,128)}, f32[1024,768]{1,0:T(8,128)}) custom-call(s32[1,4]{1,0:T(1,128)} %lengths_ref.3, s32[1,2]{1,0:T(1,128)} %add_bitcast_fusion.bits_ref.starts_ref, bf16[1024,768]{1,0:T(8,128)(2,1)} %get-tuple-element.167.back_attn_ref, ...), custom_call_target="tpu_custom_call" | custom-call | flops 29699999744 | bytes 27000000 | tf_op jit(solution)/shard_map/attend_back/pallas_call | solution.py:492
  154.2 24.9 %collective-permute-done.9 = f32[384,768]{1,0:T(8,128)S(1)} collective-permute-done((f32[384,768]{1,0:T(8,128)}, f32[384,768]{1,0:T(8,128)S(1)}, u32[]{:S(2)}, u32[]{:S(2)}) %collective-permute-start.9) | collective-permute-done | bytes 1179680 | tf_op jit(solution)/shard_map/ppermute | solution.py:714
  181.2 10.2 %collective-permute-done.8 = f32[192,768]{1,0:T(8,128)S(1)} collective-permute-done((f32[192,768]{1,0:T(8,128)}, f32[192,768]{1,0:T(8,128)S(1)}, u32[]{:S(2)}, u32[]{:S(2)}) %collective-permute-start.8) | collective-permute-done | bytes 589856 | tf_op jit(solution)/shard_map/ppermute | solution.py:714
  213.9 7.8 collective-permute-done.16
  221.7 4.3 collective-permute-start.22
  236.9 6.1 collective-permute-start.18
  254.1 5.1 collective-permute-start.30
  268.7 6.2 collective-permute-start.23
  277.3 37.5 %join.6.refs_0_ = f32[384,768]{1,0:T(8,128)} custom-call(s32[1,2]{1,0:T(1,128)} %add_bitcast_fusion.bits_ref.starts_ref, f32[192,768]{1,0:T(8,128)} %copy-done.12, f32[192,768]{1,0:T(8,128)} %copy-done.24), custom_call_target="tpu_custom_call" | custom-call | flops 2200000000 | bytes 2000000 | tf_op jit(solution)/shard_map/join/pallas_call | solution.py:677
  319.2 37.5 %join.7.refs_2_ = f32[384,768]{1,0:T(8,128)} custom-call(s32[1,2]{1,0:T(1,128)} %add_bitcast_fusion.bits_ref.starts_ref, f32[192,768]{1,0:T(8,128)} %broadcast_select_fusion.4.refs_0_, f32[192,768]{1,0:T(8,128)} %collective-permute-done.26.refs_1_), custom_call_target="tpu_custom_call" | custom-call | flops 2200000000 | bytes 2000000 | tf_op jit(solution)/shard_map/join/pallas_call | solution.py:677
  368.4 13.0 %collective-permute-done.36 = f32[200,768]{1,0:T(8,128)S(1)} collective-permute-done((f32[200,768]{1,0:T(8,128)S(1)}, f32[200,768]{1,0:T(8,128)S(1)}, u32[]{:S(2)}, u32[]{:S(2)}) %collective-permute-start.36) | collective-permute-done | bytes 614432 | tf_op jit(solution)/shard_map/ppermute | solution.py:780
  387.8 144.7 %place.3 = f32[1536,768]{1,0:T(8,128)} custom-call(s32[1,2]{1,0:T(1,128)} %add_bitcast_fusion.bits_ref.starts_ref, f32[384,768]{1,0:T(8,128)} %join.6.refs_0_, f32[384,768]{1,0:T(8,128)} %collective-permute-done.35.refs_1_, f32[384,768]{1,0:T(8,128)} %join.7.refs_2_, f32[384,768]{1,0:T(8,128)} %collective-permute-done.37.refs_3_), custom_call_target="tpu_custom_call" | custom-call | flops 2200000000 | bytes 2000000 | tf_op jit(solution)/shard_map/place/pallas_call | solution.py:677
  533.7 37.5 %join.8.refs_2_ = f32[384,768]{1,0:T(8,128)} custom-call(s32[1,2]{1,0:T(1,128)} %add_bitcast_fusion.bits_ref.starts_ref, f32[192,768]{1,0:T(8,128)} %broadcast_select_fusion.3.refs_0_, f32[192,768]{1,0:T(8,128)} %collective-permute-done.41.refs_1_), custom_call_target="tpu_custom_call" | custom-call | flops 2200000000 | bytes 2000000 | tf_op jit(solution)/shard_map/join/pallas_call | solution.py:677
  573.1 37.5 %join.9.refs_0_ = f32[384,768]{1,0:T(8,128)} custom-call(s32[1,2]{1,0:T(1,128)} %add_bitcast_fusion.bits_ref.starts_ref, f32[192,768]{1,0:T(8,128)} %broadcast_select_fusion.2.refs_0_, f32[192,768]{1,0:T(8,128)} %collective-permute-done.40.refs_1_), custom_call_target="tpu_custom_call" | custom-call | flops 2200000000 | bytes 2000000 | tf_op jit(solution)/shard_map/join/pallas_call | solution.py:677
  611.4 39.0 %join.10.refs_2_ = f32[400,768]{1,0:T(8,128)} custom-call(s32[1,2]{1,0:T(1,128)} %add_bitcast_fusion.bits_ref.starts_ref, f32[200,768]{1,0:T(8,128)} %copy-done.11, f32[200,768]{1,0:T(8,128)} %collective-permute-done.39.refs_1_), custom_call_target="tpu_custom_call" | custom-call | flops 2200000000 | bytes 2000000 | tf_op jit(solution)/shard_map/join/pallas_call | solution.py:677
  650.6 37.5 %join.11.refs_0_ = f32[384,768]{1,0:T(8,128)} custom-call(s32[1,2]{1,0:T(1,128)} %add_bitcast_fusion.bits_ref.starts_ref, f32[192,768]{1,0:T(8,128)} %broadcast_select_fusion.1.refs_0_, f32[192,768]{1,0:T(8,128)} %collective-permute-done.38.refs_1_), custom_call_target="tpu_custom_call" | custom-call | flops 2200000000 | bytes 2000000 | tf_op jit(solution)/shard_map/join/pallas_call | solution.py:677
  691.7 144.7 %place.4 = f32[768,1536]{1,0:T(8,128)} custom-call(s32[1,2]{1,0:T(1,128)} %add_bitcast_fusion.bits_ref.starts_ref, f32[384,768]{1,0:T(8,128)} %join.9.refs_0_, f32[384,768]{1,0:T(8,128)} %copy-done.5, f32[384,768]{1,0:T(8,128)} %join.8.refs_2_, f32[384,768]{1,0:T(8,128)} %copy-done.4), custom_call_target="tpu_custom_call" | custom-call | flops 2200000000 | bytes 2000000 | tf_op jit(solution)/shard_map/place/pallas_call | solution.py:677
  837.5 147.8 %place.5 = (f32[768,384]{1,0:T(8,128)}, f32[768,384]{1,0:T(8,128)}, f32[768,384]{1,0:T(8,128)}, f32[384,768]{1,0:T(8,128)}, f32[32,768]{1,0:T(8,128)}) custom-call(s32[1,2]{1,0:T(1,128)} %add_bitcast_fusion.bits_ref.starts_ref, f32[384,768]{1,0:T(8,128)} %join.11.refs_0_, f32[384,768]{1,0:T(8,128)} %copy-done.23, f32[400,768]{1,0:T(8,128)} %join.10.refs_2_, ...), custom_call_target="tpu_custom_call" | custom-call | flops 2200000000 | bytes 2000000 | tf_op jit(solution)/shard_map/place/pallas_call | solution.py:677
  (185 shorter events, 127.4 us)
Async XLA Ops:
  86.5 30.7 %collective-permute-start.4 = (f32[384,768]{1,0:T(8,128)}, f32[384,768]{1,0:T(8,128)}, u32[]{:S(2)}, u32[]{:S(2)}) collective-permute-start(f32[384,768]{1,0:T(8,128)} %get-tuple-element.162), channel_id=1, source_target_pairs={{0,4},{2,6},{4,0},{6,2},{8,12},{10,14},{12,8},{14,10},{16,20},{18,... | collective-permute-start | bytes 3538952 | tf_op jit(solution)/shard_map/ppermute | solution.py:714
  148.6 50.0 %collective-permute-start.5 = (f32[1024,768]{1,0:T(8,128)}, f32[1024,768]{1,0:T(8,128)S(1)}, u32[]{:S(2)}, u32[]{:S(2)}) collective-permute-start(f32[1024,768]{1,0:T(8,128)} %get-tuple-element.191), channel_id=1, source_target_pairs={{0,1},{1,0},{2,3},{3,2},{4,5},{5,4},{6,7},{7,6},{8,9},{9,8},{10,11... | collective-permute-start | bytes 9437192 | tf_op jit(solution)/shard_map/ppermute | solution.py:696
  148.6 30.5 %collective-permute-start.9 = (f32[384,768]{1,0:T(8,128)}, f32[384,768]{1,0:T(8,128)S(1)}, u32[]{:S(2)}, u32[]{:S(2)}) collective-permute-start(f32[384,768]{1,0:T(8,128)} %get-tuple-element.180), channel_id=1, source_target_pairs={{0,4},{2,6},{4,0},{6,2},{8,12},{10,14},{12,8},{14,10},{16,20},{18,... | collective-permute-start | bytes 3538952 | tf_op jit(solution)/shard_map/ppermute | solution.py:714
  152.0 41.9 %collective-permute-start.6 = (f32[384,768]{1,0:T(8,128)}, f32[384,768]{1,0:T(8,128)S(1)}, u32[]{:S(2)}, u32[]{:S(2)}) collective-permute-start(f32[384,768]{1,0:T(8,128)} %get-tuple-element.178), channel_id=1, source_target_pairs={{0,2},{2,0},{4,6},{6,4},{8,10},{10,8},{12,14},{14,12},{16,18},{18,... | collective-permute-start | bytes 3538952 | tf_op jit(solution)/shard_map/ppermute | solution.py:714
  152.1 39.3 %collective-permute-start.8 = (f32[192,768]{1,0:T(8,128)}, f32[192,768]{1,0:T(8,128)S(1)}, u32[]{:S(2)}, u32[]{:S(2)}) collective-permute-start(f32[192,768]{1,0:T(8,128)} %get-tuple-element.300), channel_id=1, source_target_pairs={{0,4},{2,6},{4,0},{6,2},{8,12},{10,14},{12,8},{14,10},{16,20},{18,... | collective-permute-start | bytes 1769480 | tf_op jit(solution)/shard_map/ppermute | solution.py:714
  154.1 39.6 %collective-permute-start.7 = (f32[192,768]{1,0:T(8,128)}, f32[192,768]{1,0:T(8,128)S(1)}, u32[]{:S(2)}, u32[]{:S(2)}) collective-permute-start(f32[192,768]{1,0:T(8,128)} %get-tuple-element.303), channel_id=1, source_target_pairs={{0,2},{2,0},{4,6},{6,4},{8,10},{10,8},{12,14},{14,12},{16,18},{18,... | collective-permute-start | bytes 1769480 | tf_op jit(solution)/shard_map/ppermute | solution.py:714
  191.5 30.2 %collective-permute-start.16 = (f32[400,768]{1,0:T(8,128)}, f32[400,768]{1,0:T(8,128)}, u32[]{:S(2)}, u32[]{:S(2)}) collective-permute-start(f32[400,768]{1,0:T(8,128)} %get-tuple-element.202), channel_id=1, source_target_pairs={{0,4},{2,6},{4,0},{6,2},{8,12},{10,14},{12,8},{14,10},{16,20},{18,... | collective-permute-start | bytes 3686408 | tf_op jit(solution)/shard_map/ppermute | solution.py:714
  193.7 43.2 %collective-permute-start.10 = (f32[384,768]{1,0:T(8,128)}, f32[384,768]{1,0:T(8,128)}, u32[]{:S(2)}, u32[]{:S(2)}) collective-permute-start(f32[384,768]{1,0:T(8,128)} %get-tuple-element.195), channel_id=1, source_target_pairs={{0,2},{2,0},{4,6},{6,4},{8,10},{10,8},{12,14},{14,12},{16,18},{18,... | collective-permute-start | bytes 3538952 | tf_op jit(solution)/shard_map/ppermute | solution.py:714
  198.6 30.0 %collective-permute-start.15 = (f32[192,768]{1,0:T(8,128)S(1)}, f32[192,768]{1,0:T(8,128)}, u32[]{:S(2)}, u32[]{:S(2)}) collective-permute-start(f32[192,768]{1,0:T(8,128)S(1)} %add_add_fusion.4), channel_id=1, source_target_pairs={{0,8},{24,16},{2,10},{26,18},{4,12},{28,20},{6,14},{30,22},{1,9},{... | collective-permute-start | bytes 1769480 | tf_op jit(solution)/shard_map/ppermute | solution.py:772
  261.8 53.0 %collective-permute-start.28 = (f32[192,768]{1,0:T(8,128)S(1)}, f32[192,768]{1,0:T(8,128)}, u32[]{:S(2)}, u32[]{:S(2)}) collective-permute-start(f32[192,768]{1,0:T(8,128)S(1)} %add.164), channel_id=1, source_target_pairs={{8,16},{16,8},{10,18},{18,10},{12,20},{20,12},{14,22},{22,14},{9,1... | collective-permute-start | bytes 1769480 | tf_op jit(solution)/shard_map/ppermute | solution.py:777
  264.5 52.8 %collective-permute-start.27 = (f32[192,768]{1,0:T(8,128)S(1)}, f32[192,768]{1,0:T(8,128)}, u32[]{:S(2)}, u32[]{:S(2)}) collective-permute-start(f32[192,768]{1,0:T(8,128)S(1)} %add.167), channel_id=1, source_target_pairs={{8,0},{16,24},{10,2},{18,26},{12,4},{20,28},{14,6},{22,30},{9,1},{... | collective-permute-start | bytes 1769480 | tf_op jit(solution)/shard_map/ppermute | solution.py:780
  266.7 52.5 %collective-permute-start.26 = (f32[192,768]{1,0:T(8,128)}, f32[192,768]{1,0:T(8,128)}, u32[]{:S(2)}, u32[]{:S(2)}) collective-permute-start(f32[192,768]{1,0:T(8,128)} %broadcast_select_fusion.4.refs_0_), channel_id=1, source_target_pairs={{0,2},{2,0},{4,6},{6,4},{8,10},{10,8},{12,14},{14,12},{16,18},{18,... | collective-permute-start | bytes 1769480 | tf_op jit(solution)/shard_map/ppermute | solution.py:714
  268.7 90.5 %collective-permute-start.23 = (f32[192,768]{1,0:T(8,128)S(1)}, f32[192,768]{1,0:T(8,128)}, u32[]{:S(2)}, u32[]{:S(2)}) collective-permute-start(f32[192,768]{1,0:T(8,128)S(1)} %add_add_fusion.1), channel_id=1, source_target_pairs={{0,8},{24,16},{2,10},{26,18},{4,12},{28,20},{6,14},{30,22},{1,9},{... | collective-permute-start | bytes 1769480 | tf_op jit(solution)/shard_map/ppermute | solution.py:772
  275.8 85.3 %collective-permute-start.33 = (f32[200,768]{1,0:T(8,128)S(1)}, f32[200,768]{1,0:T(8,128)}, u32[]{:S(2)}, u32[]{:S(2)}) collective-permute-start(f32[200,768]{1,0:T(8,128)S(1)} %add.168), channel_id=1, source_target_pairs={{8,16},{16,8},{10,18},{18,10},{12,20},{20,12},{14,22},{22,14},{9,1... | collective-permute-start | bytes 1843208 | tf_op jit(solution)/shard_map/ppermute | solution.py:777
  316.0 47.6 %collective-permute-start.32 = (f32[192,768]{1,0:T(8,128)S(1)}, f32[192,768]{1,0:T(8,128)}, u32[]{:S(2)}, u32[]{:S(2)}) collective-permute-start(f32[192,768]{1,0:T(8,128)S(1)} %add.169), channel_id=1, source_target_pairs={{8,0},{16,24},{10,2},{18,26},{12,4},{20,28},{14,6},{22,30},{9,1},{... | collective-permute-start | bytes 1769480 | tf_op jit(solution)/shard_map/ppermute | solution.py:780
  365.6 167.0 %collective-permute-start.34 = (f32[192,768]{1,0:T(8,128)S(1)}, f32[192,768]{1,0:T(8,128)S(1)}, u32[]{:S(2)}, u32[]{:S(2)}) collective-permute-start(f32[192,768]{1,0:T(8,128)S(1)} %add.172), channel_id=1, source_target_pairs={{8,0},{16,24},{10,2},{18,26},{12,4},{20,28},{14,6},{22,30},{9,1},{... | collective-permute-start | bytes 1769480 | tf_op jit(solution)/shard_map/ppermute | solution.py:780
  366.9 166.8 %collective-permute-start.41 = (f32[192,768]{1,0:T(8,128)}, f32[192,768]{1,0:T(8,128)}, u32[]{:S(2)}, u32[]{:S(2)}) collective-permute-start(f32[192,768]{1,0:T(8,128)} %broadcast_select_fusion.3.refs_0_), channel_id=1, source_target_pairs={{0,2},{2,0},{4,6},{6,4},{8,10},{10,8},{12,14},{14,12},{16,18},{18,... | collective-permute-start | bytes 1769480 | tf_op jit(solution)/shard_map/ppermute | solution.py:714
  381.4 191.8 %collective-permute-start.40 = (f32[192,768]{1,0:T(8,128)}, f32[192,768]{1,0:T(8,128)}, u32[]{:S(2)}, u32[]{:S(2)}) collective-permute-start(f32[192,768]{1,0:T(8,128)} %broadcast_select_fusion.2.refs_0_), channel_id=1, source_target_pairs={{0,4},{2,6},{4,0},{6,2},{8,12},{10,14},{12,8},{14,10},{16,20},{18,... | collective-permute-start | bytes 1769480 | tf_op jit(solution)/shard_map/ppermute | solution.py:714
  384.4 226.9 %collective-permute-start.39 = (f32[200,768]{1,0:T(8,128)S(1)}, f32[200,768]{1,0:T(8,128)}, u32[]{:S(2)}, u32[]{:S(2)}) collective-permute-start(f32[200,768]{1,0:T(8,128)S(1)} %broadcast_select_fusion.refs_0_), channel_id=1, source_target_pairs={{0,2},{2,0},{4,6},{6,4},{8,10},{10,8},{12,14},{14,12},{16,18},{18,... | collective-permute-start | bytes 1843208 | tf_op jit(solution)/shard_map/ppermute | solution.py:714
  533.5 117.1 %collective-permute-start.38 = (f32[192,768]{1,0:T(8,128)}, f32[192,768]{1,0:T(8,128)}, u32[]{:S(2)}, u32[]{:S(2)}) collective-permute-start(f32[192,768]{1,0:T(8,128)} %broadcast_select_fusion.1.refs_0_), channel_id=1, source_target_pairs={{0,4},{2,6},{4,0},{6,2},{8,12},{10,14},{12,8},{14,10},{16,20},{18,... | collective-permute-start | bytes 1769480 | tf_op jit(solution)/shard_map/ppermute | solution.py:714
  571.3 118.4 %collective-permute-start.44 = (f32[384,768]{1,0:T(8,128)}, f32[384,768]{1,0:T(8,128)S(1)}, u32[]{:S(2)}, u32[]{:S(2)}) collective-permute-start(f32[384,768]{1,0:T(8,128)} %join.8.refs_2_), channel_id=1, source_target_pairs={{0,4},{2,6},{4,0},{6,2},{8,12},{10,14},{12,8},{14,10},{16,20},{18,... | collective-permute-start | bytes 3538952 | tf_op jit(solution)/shard_map/ppermute | solution.py:714
  610.6 79.0 %collective-permute-start.43 = (f32[384,768]{1,0:T(8,128)}, f32[384,768]{1,0:T(8,128)S(1)}, u32[]{:S(2)}, u32[]{:S(2)}) collective-permute-start(f32[384,768]{1,0:T(8,128)} %join.9.refs_0_), channel_id=1, source_target_pairs={{0,2},{2,0},{4,6},{6,4},{8,10},{10,8},{12,14},{14,12},{16,18},{18,... | collective-permute-start | bytes 3538952 | tf_op jit(solution)/shard_map/ppermute | solution.py:714
  650.4 186.1 %collective-permute-start.45 = (f32[400,768]{1,0:T(8,128)}, f32[400,768]{1,0:T(8,128)}, u32[]{:S(2)}, u32[]{:S(2)}) collective-permute-start(f32[400,768]{1,0:T(8,128)} %join.10.refs_2_), channel_id=1, source_target_pairs={{0,4},{2,6},{4,0},{6,2},{8,12},{10,14},{12,8},{14,10},{16,20},{18,... | collective-permute-start | bytes 3686408 | tf_op jit(solution)/shard_map/ppermute | solution.py:714
  688.1 148.3 %collective-permute-start.42 = (f32[384,768]{1,0:T(8,128)}, f32[384,768]{1,0:T(8,128)S(1)}, u32[]{:S(2)}, u32[]{:S(2)}) collective-permute-start(f32[384,768]{1,0:T(8,128)} %join.11.refs_0_), channel_id=1, source_target_pairs={{0,2},{2,0},{4,6},{6,4},{8,10},{10,8},{12,14},{14,12},{16,18},{18,... | collective-permute-start | bytes 3538952 | tf_op jit(solution)/shard_map/ppermute | solution.py:714
  (47 other events, 844.1 us)

commit v4 on v3

--- a/solution.py
+++ b/solution.py
@@ -109,7 +109,8 @@
     values_ref,
     context_ref,
     total_ref,
-    attn_out_ref,
+    attn_low_ref,
+    attn_high_ref,
     turned_ref,
 ):
     rows = tokens_ref.shape[0]
@@ -140,7 +141,9 @@
             context_ref[pl.ds(first_row, LANES), lanes] = merge_heads(turned).astype(jnp.bfloat16)
 
     over_query_blocks(ends, rows, widths, body)
-    attn_out_ref[...] = contract(context_ref[...], out_weight_ref[...], 1, 0)
+    half = rows // 2
+    attn_low_ref[...] = contract(context_ref[:half], out_weight_ref[...], 1, 0)
+    attn_high_ref[...] = contract(context_ref[half:], out_weight_ref[...], 1, 0)
 
 
 def attend_back_kernel(
@@ -148,7 +151,8 @@
     seqs,
     lengths_ref,
     bits_ref,
-    back_attn_ref,
+    back_low_ref,
+    back_high_ref,
     out_weight_ref,
     queries_ref,
     keys_ref,
@@ -164,7 +168,8 @@
     first_kept_ref,
     second_sent_ref,
     second_kept_ref,
-    partial_ref,
+    partial_low_ref,
+    partial_high_ref,
     first_pack_ref,
     second_pack_ref,
     back_context_ref,
@@ -176,9 +181,11 @@
     rows = tokens_ref.shape[0]
     width_here = q_weight_ref.shape[1]
     pairs = width_here // LANES
-    back_context_ref[...] = contract(back_attn_ref[...], out_weight_ref[...], 1, 1).astype(
-        jnp.bfloat16
-    )
+    half_rows = rows // 2
+    for at, back_ref in enumerate((back_low_ref, back_high_ref)):
+        back_context_ref[at * half_rows : (at + 1) * half_rows] = contract(
+            back_ref[...], out_weight_ref[...], 1, 1
+        ).astype(jnp.bfloat16)
     turned_ref[...] = keys_ref[...].astype(jnp.float32).T.astype(jnp.bfloat16)
     back_keys_ref[...] = jnp.zeros_like(back_keys_ref)
     back_values_ref[...] = jnp.zeros_like(back_values_ref)
@@ -216,7 +223,9 @@
     first_pack_ref[:, width_here:] = contract(tokens, back_keys, 0, 0)
     put_halves(first_sent_ref, first_kept_ref, first_pack_ref, bits_ref[0, 0])
     grad_values = contract(tokens, back_values, 0, 0)
-    grad_out = contract(context_ref[...], back_attn_ref[...], 0, 0)
+    grad_out = contract(context_ref[:half_rows], back_low_ref[...], 0, 0) + contract(
+        context_ref[half_rows:], back_high_ref[...], 0, 0
+    )
     out_half, value_half, small_half = width_here // 2, model // 4, small_ref.shape[0] // 2
     top = 0
     for at in range(2):
@@ -240,11 +249,13 @@
             )
         top += small_half
     put_halves(second_sent_ref, second_kept_ref, second_pack_ref, bits_ref[0, 1])
-    partial_ref[...] = (
-        contract(back_queries, q_weight_ref[...], 1, 1)
-        + contract(back_keys, k_weight_ref[...], 1, 1)
-        + contract(back_values, v_weight_ref[...], 1, 1)
-    )
+    for at, out_ref in enumerate((partial_low_ref, partial_high_ref)):
+        part = slice(at * half_rows, (at + 1) * half_rows)
+        out_ref[...] = (
+            contract(back_queries[part], q_weight_ref[...], 1, 1)
+            + contract(back_keys[part], k_weight_ref[...], 1, 1)
+            + contract(back_values[part], v_weight_ref[...], 1, 1)
+        )
 
 
 def row_mean(values):
@@ -262,166 +273,204 @@
     return rate * (scaled - row_mean(scaled) - unit * row_mean(scaled * unit))
 
 
-def add_sums(sums_ref, members):
-    @pl.when(pl.program_id(0) == 0)
-    def _():
-        sums_ref[...] = jnp.zeros_like(sums_ref)
-
-    for at, member in enumerate(members):
-        sums_ref[at : at + 1, :] += jnp.sum(member, axis=0, keepdims=True)
-
-
-def feed_kernel(
-    tokens_ref,
-    own_ref,
-    other_ref,
-    out_bias_ref,
-    gain_ref,
-    shift_ref,
-    up_weight_ref,
-    up_bias_ref,
-    down_weight_ref,
-    first_sum_ref,
-    first_low_ref,
-    inner_ref,
-    active_ref,
-    partial_ref,
-):
-    first_sum = (
-        tokens_ref[...].astype(jnp.float32) + (own_ref[...] + other_ref[...]) + out_bias_ref[...]
-    )
-    first_sum_ref[...] = first_sum
-    unit, unused = standardize(first_sum)
-    first_low = (unit * gain_ref[...] + shift_ref[...]).astype(jnp.bfloat16)
-    first_low_ref[...] = first_low
-    inner = contract(first_low, up_weight_ref[...], 1, 0) + up_bias_ref[...]
-    inner_ref[...] = inner
-    active = (inner * (0.5 * (1.0 + lax.erf(inner * 0.7071067811865476)))).astype(jnp.bfloat16)
-    active_ref[...] = active
-    partial_ref[...] = contract(active, down_weight_ref[...], 1, 0)
-
-
-def second_norm_kernel(
+def column_sum(member):
+    return jnp.sum(member, axis=0, keepdims=True)
+
+
+def row_blocks(rows):
+    return [slice(at, at + ROW_BLOCK) for at in range(0, rows, ROW_BLOCK)]
+
+
+def feed_kernel(first_row, *refs):
+    (
+        tokens_ref,
+        own_ref,
+        *other_refs,
+        out_bias_ref,
+        gain_ref,
+        shift_ref,
+        up_weight_ref,
+        up_bias_ref,
+        down_weight_ref,
+        first_sum_ref,
+        first_low_ref,
+        active_ref,
+        partial_ref,
+    ) = refs
+    for at, other_ref in zip(row_blocks(own_ref.shape[0]), other_refs, strict=True):
+        tokens = tokens_ref[first_row + at.start : first_row + at.stop]
+        first_sum = (
+            tokens.astype(jnp.float32) + (own_ref[at] + other_ref[...]) + out_bias_ref[...]
+        )
+        first_sum_ref[at] = first_sum
+        unit, unused = standardize(first_sum)
+        first_low = (unit * gain_ref[...] + shift_ref[...]).astype(jnp.bfloat16)
+        first_low_ref[at] = first_low
+        inner = contract(first_low, up_weight_ref[...], 1, 0) + up_bias_ref[...]
+        active = (inner * (0.5 * (1.0 + lax.erf(inner * 0.7071067811865476)))).astype(
+            jnp.bfloat16
+        )
+        active_ref[at] = active
+        partial_ref[at] = contract(active, down_weight_ref[...], 1, 0)
+
+
+def second_norm_kernel(first_row, *refs):
+    (
+        first_sum_ref,
+        own_ref,
+        *other_refs,
+        cotangent_ref,
+        first_gain_ref,
+        first_shift_ref,
+        down_bias_ref,
+        gain_ref,
+        shift_ref,
+        layer_out_ref,
+        back_second_ref,
+        back_down_ref,
+        sums_ref,
+    ) = refs
+    bias_sum, gain_sum, shift_sum = 0.0, 0.0, 0.0
+    for at, other_ref in zip(row_blocks(own_ref.shape[0]), other_refs, strict=True):
+        unit, unused = standardize(first_sum_ref[at])
+        first = unit * first_gain_ref[...] + first_shift_ref[...]
+        second_sum = first + (own_ref[at] + other_ref[...]) + down_bias_ref[...]
+        unit, rate = standardize(second_sum)
+        layer_out_ref[at] = (unit * gain_ref[...] + shift_ref[...]).astype(jnp.bfloat16)
+        upstream = cotangent_ref[first_row + at.start : first_row + at.stop].astype(jnp.float32)
+        back_second = norm_back(upstream, unit, rate, gain_ref[...])
+        back_second_ref[at] = back_second
+        back_down_ref[at] = back_second.astype(jnp.bfloat16)
+        bias_sum += column_sum(back_second)
+        gain_sum += column_sum(upstream * unit)
+        shift_sum += column_sum(upstream)
+    sums_ref[...] = jnp.zeros_like(sums_ref)
+    sums_ref[0:1, :] = bias_sum
+    sums_ref[1:2, :] = gain_sum
+    sums_ref[2:3, :] = shift_sum
+
+
+def grad_down_kernel(
     bits_ref,
-    first_sum_ref,
-    own_ref,
-    other_ref,
-    cotangent_ref,
-    active_ref,
-    first_gain_ref,
-    first_shift_ref,
-    down_bias_ref,
-    gain_ref,
-    shift_ref,
-    layer_out_ref,
-    back_second_ref,
-    back_down_ref,
+    active_low_ref,
+    active_high_ref,
+    back_low_ref,
+    back_high_ref,
     low_sent_ref,
     low_kept_ref,
     high_sent_ref,
     high_kept_ref,
+):
+    rows = low_sent_ref.shape[0]
+    for at, (sent_ref, kept_ref) in enumerate(
+        ((low_sent_ref, low_kept_ref), (high_sent_ref, high_kept_ref))
+    ):
+        mine = bits_ref[0, at]
+        for out_ref, place in ((sent_ref, 1 - mine), (kept_ref, mine)):
+            units = pl.ds(pl.multiple_of((2 * at + place) * rows, LANES), rows)
+            out_ref[...] = contract(active_low_ref[:, units], back_low_ref[...], 0, 0) + contract(
+                active_high_ref[:, units], back_high_ref[...], 0, 0
+            )
+
+
+def feed_back_kernel(
+    back_down_ref,
+    first_low_ref,
+    up_weight_ref,
+    up_bias_ref,
+    down_weight_ref,
+    partial_ref,
+    back_inner_ref,
     sums_ref,
-    grad_low_ref,
-    grad_high_ref,
 ):
-    unit, unused = standardize(first_sum_ref[...])
-    first = unit * first_gain_ref[...] + first_shift_ref[...]
-    second_sum = first + (own_ref[...] + other_ref[...]) + down_bias_ref[...]
-    unit, rate = standardize(second_sum)
-    layer_out_ref[...] = (unit * gain_ref[...] + shift_ref[...]).astype(jnp.bfloat16)
-    upstream = cotangent_ref[...].astype(jnp.float32)
-    back_second = norm_back(upstream, unit, rate, gain_ref[...])
-    back_second_ref[...] = back_second
-    back_down = back_second.astype(jnp.bfloat16)
-    back_down_ref[...] = back_down
-    half = grad_low_ref.shape[0]
-
-    @pl.when(pl.program_id(0) == 0)
-    def _():
-        grad_low_ref[...] = jnp.zeros_like(grad_low_ref)
-        grad_high_ref[...] = jnp.zeros_like(grad_high_ref)
-
-    grad_low_ref[...] += contract(active_ref[:, :half], back_down, 0, 0)
-    grad_high_ref[...] += contract(active_ref[:, half:], back_down, 0, 0)
-    add_sums(sums_ref, (back_second, upstream * unit, upstream))
-
-    @pl.when(pl.program_id(0) == pl.num_programs(0) - 1)
-    def _():
-        put_halves(low_sent_ref, low_kept_ref, grad_low_ref, bits_ref[0, 0])
-        put_halves(high_sent_ref, high_kept_ref, grad_high_ref, bits_ref[0, 1])
-
-
-def feed_back_kernel(
+    total = 0.0
+    for at in row_blocks(back_down_ref.shape[0]):
+        inner = contract(first_low_ref[at], up_weight_ref[...], 1, 0) + up_bias_ref[...]
+        slope = 0.5 * (1.0 + lax.erf(inner * 0.7071067811865476)) + inner * (
+            0.3989422804014327 * jnp.exp(-0.5 * inner * inner)
+        )
+        back_active = contract(back_down_ref[at], down_weight_ref[...], 1, 1)
+        back_inner = (back_active * slope).astype(jnp.bfloat16)
+        back_inner_ref[at] = back_inner
+        partial_ref[at] = contract(back_inner, up_weight_ref[...], 1, 1)
+        total += column_sum(back_inner.astype(jnp.float32))
+    sums_ref[...] = jnp.zeros_like(sums_ref)
+    sums_ref[0:1, :] = total
+
+
+def grad_up_kernel(
     bits_ref,
-    back_down_ref,
-    inner_ref,
     first_low_ref,
-    down_weight_ref,
-    up_weight_ref,
-    partial_ref,
+    first_high_ref,
+    back_low_ref,
+    back_high_ref,
     low_sent_ref,
     low_kept_ref,
     high_sent_ref,
     high_kept_ref,
-    sums_ref,
-    grad_low_ref,
-    grad_high_ref,
 ):
-    inner = inner_ref[...]
-    slope = 0.5 * (1.0 + lax.erf(inner * 0.7071067811865476)) + inner * (
-        0.3989422804014327 * jnp.exp(-0.5 * inner * inner)
-    )
-    back_active = contract(back_down_ref[...], down_weight_ref[...], 1, 1)
-    back_inner = (back_active * slope).astype(jnp.bfloat16)
-    partial_ref[...] = contract(back_inner, up_weight_ref[...], 1, 1)
-    half = grad_low_ref.shape[1]
-
-    @pl.when(pl.program_id(0) == 0)
-    def _():
-        grad_low_ref[...] = jnp.zeros_like(grad_low_ref)
-        grad_high_ref[...] = jnp.zeros_like(grad_high_ref)
-
-    first_low = first_low_ref[...]
-    grad_low_ref[...] += contract(first_low, back_inner[:, :half], 0, 0)
-    grad_high_ref[...] += contract(first_low, back_inner[:, half:], 0, 0)
-    add_sums(sums_ref, (back_inner.astype(jnp.float32),))
-
-    @pl.when(pl.program_id(0) == pl.num_programs(0) - 1)
-    def _():
-        put_halves(low_sent_ref, low_kept_ref, grad_low_ref, bits_ref[0, 0])
-        put_halves(high_sent_ref, high_kept_ref, grad_high_ref, bits_ref[0, 1])
-
-
-def first_norm_kernel(
-    first_sum_ref,
-    own_ref,
-    other_ref,
-    back_second_ref,
-    gain_ref,
-    back_first_sum_ref,
-    back_attn_ref,
-    sums_ref,
-):
-    unit, rate = standardize(first_sum_ref[...])
-    upstream = (own_ref[...] + other_ref[...]) + back_second_ref[...]
-    back_first_sum = norm_back(upstream, unit, rate, gain_ref[...])
-    back_first_sum_ref[...] = back_first_sum
-    back_attn_ref[...] = back_first_sum.astype(jnp.bfloat16)
-    add_sums(sums_ref, (back_first_sum, upstream * unit, upstream))
+    rows, columns = low_sent_ref.shape
+    for at, (sent_ref, kept_ref) in enumerate(
+        ((low_sent_ref, low_kept_ref), (high_sent_ref, high_kept_ref))
+    ):
+        mine = bits_ref[0, at]
+        units = slice(at * columns, (at + 1) * columns)
+        for out_ref, place in ((sent_ref, 1 - mine), (kept_ref, mine)):
+            features = pl.ds(pl.multiple_of(place * rows, LANES), rows)
+            out_ref[...] = contract(
+                first_low_ref[:, features], back_low_ref[:, units], 0, 0
+            ) + contract(first_high_ref[:, features], back_high_ref[:, units], 0, 0)
+
+
+def first_norm_kernel(*refs):
+    (
+        first_sum_ref,
+        own_ref,
+        *other_refs,
+        back_second_ref,
+        gain_ref,
+        back_first_sum_ref,
+        back_attn_ref,
+        sums_ref,
+    ) = refs
+    bias_sum, gain_sum, shift_sum = 0.0, 0.0, 0.0
+    for at, other_ref in zip(row_blocks(own_ref.shape[0]), other_refs, strict=True):
+        unit, rate = standardize(first_sum_ref[at])
+        upstream = (own_ref[at] + other_ref[...]) + back_second_ref[at]
+        back_first_sum = norm_back(upstream, unit, rate, gain_ref[...])
+        back_first_sum_ref[at] = back_first_sum
+        back_attn_ref[at] = back_first_sum.astype(jnp.bfloat16)
+        bias_sum += column_sum(back_first_sum)
+        gain_sum += column_sum(upstream * unit)
+        shift_sum += column_sum(upstream)
+    sums_ref[...] = jnp.zeros_like(sums_ref)
+    sums_ref[0:1, :] = bias_sum
+    sums_ref[1:2, :] = gain_sum
+    sums_ref[2:3, :] = shift_sum
+
+
+def input_kernel(*refs):
+    *sources, grad_ref = refs
+    rows = grad_ref.shape[0] // 2
+    blocks = row_blocks(rows)
+    for half in range(2):
+        own_ref, *other_refs, first_ref = sources[half * len(sources) // 2 :][: len(sources) // 2]
+        for at, other_ref in zip(blocks, other_refs, strict=True):
+            grad_ref[half * rows + at.start : half * rows + at.stop] = (
+                (own_ref[at] + other_ref[...]) + first_ref[at]
+            ).astype(jnp.bfloat16)
+
+
+def joined_kernel(low_ref, high_ref, out_ref):
+    rows = low_ref.shape[0]
+    out_ref[:rows] = low_ref[...]
+    out_ref[rows:] = high_ref[...]
 
 
 def struct(shape, dtype):
     return jax.ShapeDtypeStruct(shape, dtype)
 
 
-def by_rows(columns):
-    return pl.BlockSpec((ROW_BLOCK, columns), lambda step: (step, 0))
-
-
-def held(shape):
-    return pl.BlockSpec(shape, lambda *step: (0, 0), pipeline_mode=pl.Buffered(1))
-
-
 def in_smem():
     return pl.BlockSpec(memory_space=pltpu.SMEM)
 
@@ -430,224 +479,64 @@
     return pl.BlockSpec(memory_space=pltpu.VMEM)
 
 
-def params(mebibytes):
-    return pltpu.CompilerParams(vmem_limit_bytes=mebibytes * MIB)
-
-
-def lasting(microseconds):
-    return pl.CostEstimate(
-        flops=int(microseconds * 1.1e9),
-        transcendentals=0,
-        bytes_accessed=int(microseconds * 1e6),
-    )
-
-
 def key_widths(rows):
     return tuple(width for width in (640,) if width < rows) + (rows,)
 
 
-def attend(lengths, tokens, q_weight, k_weight, v_weight, q_bias, v_bias, out_weight):
+def call(body, outs, scalars, operands, name, mebibytes=16, scratch=()):
+    return pl.pallas_call(
+        body,
+        out_shape=tuple(struct(*out) for out in outs),
+        in_specs=[in_smem()] * len(scalars) + [in_vmem()] * len(operands),
+        out_specs=(in_vmem(),) * len(outs),
+        scratch_shapes=[pltpu.VMEM(*shape) for shape in scratch],
+        compiler_params=pltpu.CompilerParams(vmem_limit_bytes=mebibytes * MIB),
+        name=name,
+    )(*scalars, *operands)
+
+
+low, exact = jnp.bfloat16, jnp.float32
+
+
+def attend(lengths, tokens, *others):
     rows, model = tokens.shape
-    width = q_weight.shape[1]
+    width = others[0].shape[1]
     totals = rows // LANES * (width // LANES)
-    low = struct((rows, width), jnp.bfloat16)
-    return pl.pallas_call(
+    half = (rows // 2, model)
+    return call(
         functools.partial(attend_kernel, key_widths(rows), lengths.shape[1]),
-        out_shape=(
-            low,
-            low,
-            low,
-            low,
-            struct((totals, 2 * LANES), jnp.float32),
-            struct((rows, model), jnp.float32),
-        ),
-        in_specs=[in_smem()] + [in_vmem()] * 7,
-        out_specs=(in_vmem(),) * 6,
-        scratch_shapes=[pltpu.VMEM((width, rows), jnp.bfloat16)],
-        compiler_params=params(60),
-        cost_estimate=lasting(20),
-        name="attend",
-    )(lengths, tokens, q_weight, k_weight, v_weight, q_bias, v_bias, out_weight)
-
-
-def attend_back(
-    lengths,
-    bits,
-    back_attn,
-    out_weight,
-    queries,
-    keys,
-    values,
-    totals,
-    tokens,
-    context,
-    q_weight,
-    k_weight,
-    v_weight,
-    small,
-):
-    rows, model = tokens.shape
-    width = q_weight.shape[1]
-    pack_rows = width + model // 2 + small.shape[0]
-    return pl.pallas_call(
+        [((rows, width), low)] * 4
+        + [((totals, 2 * LANES), exact), (half, exact), (half, exact)],
+        (lengths,),
+        (tokens, *others),
+        "attend",
+        20,
+        [((width, rows), low)],
+    )
+
+
+def attend_back(lengths, bits, operands, rows, model, width, small_rows):
+    pack_rows = width + model // 2 + small_rows
+    half = (rows // 2, model)
+    return call(
         functools.partial(attend_back_kernel, key_widths(rows), lengths.shape[1]),
-        out_shape=(
-            struct((model // 2, 2 * width), jnp.float32),
-            struct((model // 2, 2 * width), jnp.float32),
-            struct((pack_rows // 2, model), jnp.float32),
-            struct((pack_rows // 2, model), jnp.float32),
-            struct((rows, model), jnp.float32),
-        ),
-        in_specs=[in_smem()] * 2 + [in_vmem()] * 12,
-        out_specs=(in_vmem(),) * 5,
-        scratch_shapes=[
-            pltpu.VMEM((model, 2 * width), jnp.float32),
-            pltpu.VMEM((pack_rows, model), jnp.float32),
-            pltpu.VMEM((rows, width), jnp.bfloat16),
-            pltpu.VMEM((width, rows), jnp.bfloat16),
-            pltpu.VMEM((rows, width), jnp.bfloat16),
-            pltpu.VMEM((rows, width), jnp.float32),
-            pltpu.VMEM((rows, width), jnp.float32),
+        [((model // 2, 2 * width), exact)] * 2
+        + [((pack_rows // 2, model), exact)] * 2
+        + [(half, exact)] * 2,
+        (lengths, bits),
+        operands,
+        "attend_back",
+        28,
+        [
+            ((model, 2 * width), exact),
+            ((pack_rows, model), exact),
+            ((rows, width), low),
+            ((width, rows), low),
+            ((rows, width), low),
+            ((rows, width), exact),
+            ((rows, width), exact),
         ],
-        compiler_params=params(60),
-        cost_estimate=lasting(27),
-        name="attend_back",
-    )(
-        lengths,
-        bits,
-        back_attn,
-        out_weight,
-        queries,
-        keys,
-        values,
-        totals,
-        tokens,
-        context,
-        q_weight,
-        k_weight,
-        v_weight,
-        small,
-    )
-
-
-def feed(tokens, own, other, out_bias, gain, shift, up_weight, up_bias, down_weight):
-    rows, model = tokens.shape
-    hidden = up_weight.shape[1]
-    return pl.pallas_call(
-        feed_kernel,
-        grid=(rows // ROW_BLOCK,),
-        out_shape=(
-            struct((rows, model), jnp.float32),
-            struct((rows, model), jnp.bfloat16),
-            struct((rows, hidden), jnp.float32),
-            struct((rows, hidden), jnp.bfloat16),
-            struct((rows, model), jnp.float32),
-        ),
-        in_specs=[by_rows(model)] * 3
-        + [held((1, model))] * 3
-        + [held((model, hidden)), held((1, hidden)), held((hidden, model))],
-        out_specs=(
-            by_rows(model),
-            by_rows(model),
-            by_rows(hidden),
-            by_rows(hidden),
-            by_rows(model),
-        ),
-        compiler_params=params(60),
-        cost_estimate=lasting(10),
-        name="feed",
-    )(tokens, own, other, out_bias, gain, shift, up_weight, up_bias, down_weight)
-
-
-def second_norm(
-    bits, first_sum, own, other, cotangent, active, first_gain, first_shift, down_bias, gain, shift
-):
-    rows, model = first_sum.shape
-    hidden = active.shape[1]
-    return pl.pallas_call(
-        second_norm_kernel,
-        grid=(rows // ROW_BLOCK,),
-        out_shape=(
-            struct((rows, model), jnp.bfloat16),
-            struct((rows, model), jnp.float32),
-            struct((rows, model), jnp.bfloat16),
-            struct((hidden // 4, model), jnp.float32),
-            struct((hidden // 4, model), jnp.float32),
-            struct((hidden // 4, model), jnp.float32),
-            struct((hidden // 4, model), jnp.float32),
-            struct((8, model), jnp.float32),
-        ),
-        in_specs=[in_smem()] + [by_rows(model)] * 4 + [by_rows(hidden)] + [held((1, model))] * 5,
-        out_specs=(
-            by_rows(model),
-            by_rows(model),
-            by_rows(model),
-            held((hidden // 4, model)),
-            held((hidden // 4, model)),
-            held((hidden // 4, model)),
-            held((hidden // 4, model)),
-            held((8, model)),
-        ),
-        scratch_shapes=[pltpu.VMEM((hidden // 2, model), jnp.float32)] * 2,
-        cost_estimate=lasting(10),
-        compiler_params=params(60),
-        name="second_norm",
-    )(bits, first_sum, own, other, cotangent, active, first_gain, first_shift, down_bias, gain, shift)
-
-
-def feed_back(bits, back_down, inner, first_low, down_weight, up_weight):
-    rows, model = back_down.shape
-    hidden = inner.shape[1]
-    return pl.pallas_call(
-        feed_back_kernel,
-        grid=(rows // ROW_BLOCK,),
-        out_shape=(
-            struct((rows, model), jnp.float32),
-            struct((model // 2, hidden // 2), jnp.float32),
-            struct((model // 2, hidden // 2), jnp.float32),
-            struct((model // 2, hidden // 2), jnp.float32),
-            struct((model // 2, hidden // 2), jnp.float32),
-            struct((8, hidden), jnp.float32),
-        ),
-        in_specs=[
-            in_smem(),
-            by_rows(model),
-            by_rows(hidden),
-            by_rows(model),
-            held((hidden, model)),
-            held((model, hidden)),
-        ],
-        out_specs=(
-            by_rows(model),
-            held((model // 2, hidden // 2)),
-            held((model // 2, hidden // 2)),
-            held((model // 2, hidden // 2)),
-            held((model // 2, hidden // 2)),
-            held((8, hidden)),
-        ),
-        scratch_shapes=[pltpu.VMEM((model, hidden // 2), jnp.float32)] * 2,
-        cost_estimate=lasting(13),
-        compiler_params=params(60),
-        name="feed_back",
-    )(bits, back_down, inner, first_low, down_weight, up_weight)
-
-
-def first_norm_back(first_sum, own, other, back_second, gain):
-    rows, model = first_sum.shape
-    return pl.pallas_call(
-        first_norm_kernel,
-        grid=(rows // ROW_BLOCK,),
-        out_shape=(
-            struct((rows, model), jnp.float32),
-            struct((rows, model), jnp.bfloat16),
-            struct((8, model), jnp.float32),
-        ),
-        in_specs=[by_rows(model)] * 4 + [held((1, model))],
-        out_specs=(by_rows(model), by_rows(model), held((8, model))),
-        cost_estimate=lasting(5),
-        compiler_params=params(60),
-        name="first_norm_back",
-    )(first_sum, own, other, back_second, gain)
+    )
 
 
 def place_kernel(moves, starts_ref, *refs):
@@ -677,10 +566,10 @@
     return pl.pallas_call(
         functools.partial(place_kernel, moves),
         out_shape=tuple(struct(shape, jnp.float32) for shape in shapes),
-        in_specs=[in_smem()] + [anywhere] * len(operands),
+        in_specs=[in_smem()] + [in_vmem()] * len(operands),
         out_specs=(anywhere,) * len(shapes),
         scratch_shapes=[pltpu.SemaphoreType.DMA((len(moves),))],
-        cost_estimate=lasting(2),
+        compiler_params=pltpu.CompilerParams(vmem_limit_bytes=8 * MIB),
         name=name,
     )(starts, *operands)
 
@@ -832,35 +721,47 @@
     width = q_weight.shape[1]
     hidden = up_weight.shape[1]
     row = lambda vector: vector.reshape(1, -1)
-    queries, keys, values, context, totals, attn_part = attend(
+    rows = tokens_in.shape[0]
+    half_rows = rows // 2
+    half_shape = (half_rows, model)
+    queries, keys, values, context, totals, *attn_parts = attend(
         seq_lengths, tokens_in, q_weight, k_weight, v_weight, row(q_bias), row(v_bias), out_weight
     )
-    first_sum, first_low, inner, active, down_part = feed(
-        tokens_in,
-        attn_part,
-        swap_cores(attn_part, tensor_count),
-        row(out_bias),
-        row(first_gain),
-        row(first_shift),
-        up_weight,
-        row(up_bias),
-        down_weight,
-    )
-    layer_out, back_second, back_down, *down_halves, second_sums = second_norm(
-        bits,
-        first_sum,
-        down_part,
-        swap_cores(down_part, tensor_count),
-        cotangent,
-        active,
-        row(first_gain),
-        row(first_shift),
-        row(down_bias),
-        row(second_gain),
-        row(second_shift),
-    )
+    first_vectors = (row(out_bias), row(first_gain), row(first_shift))
     order = Sequence()
-    order.ran(back_down)
+
+    def exchanged(parts):
+        return [
+            (part,)
+            + tuple(swap_cores(part[at], tensor_count) for at in row_blocks(part.shape[0]))
+            for part in parts
+        ]
+
+    fed = []
+    for at, pair in enumerate(exchanged(attn_parts)):
+        fed.append(
+            call(
+                functools.partial(feed_kernel, at * half_rows),
+                [(half_shape, exact), (half_shape, low), ((half_rows, hidden), low), (half_shape, exact)],
+                (),
+                (tokens_in, *pair, *first_vectors, up_weight, row(up_bias), down_weight),
+                "feed",
+            )
+        )
+    first_sums, first_lows, actives, down_parts = zip(*fed, strict=True)
+    second_vectors = [row(member) for member in (first_gain, first_shift, down_bias, second_gain, second_shift)]
+    normed = []
+    for at, pair in enumerate(exchanged(down_parts)):
+        normed.append(
+            call(
+                functools.partial(second_norm_kernel, at * half_rows),
+                [(half_shape, low), (half_shape, exact), (half_shape, low), ((8, model), exact)],
+                (),
+                (first_sums[at], *pair, cotangent, *second_vectors),
+                "second_norm",
+            )
+        )
+    outs, back_seconds, back_downs, second_sums = zip(*normed, strict=True)
     chunks = {}
 
     def begin(name, halves):
@@ -873,52 +774,91 @@
             inputs = chunk.inputs()
             order.ran(chunk.advance(order.after(inputs) if chunk.step else inputs))
 
+    down_halves = call(
+        grad_down_kernel,
+        [((hidden // 4, model), exact)] * 4,
+        (bits,),
+        (*actives, *back_downs),
+        "grad_down",
+    )
+    order.ran(down_halves[0])
     begin("D", down_halves)
     run("D1", "D0")
-    [back_down] = order.after((back_down,))
-    back_part, *up_halves, up_sums = feed_back(
-        bits, back_down, inner, first_low, down_weight, up_weight
-    )
-    order.ran(back_part)
+    fed_back = []
+    for at in range(2):
+        [back_down] = order.after((back_downs[at],))
+        fed_back.append(
+            call(
+                feed_back_kernel,
+                [(half_shape, exact), ((half_rows, hidden), low), ((8, hidden), exact)],
+                (),
+                (back_down, first_lows[at], up_weight, row(up_bias), down_weight),
+                "feed_back",
+            )
+        )
+        order.ran(fed_back[-1][1])
+    back_parts, back_inners, up_sums = zip(*fed_back, strict=True)
+    back_inner = order.after((back_inners[0],))
+    up_halves = call(
+        grad_up_kernel,
+        [((model // 2, hidden // 2), exact)] * 4,
+        (bits,),
+        (*first_lows, *back_inner, back_inners[1]),
+        "grad_up",
+    )
+    order.ran(up_halves[0])
     begin("U", up_halves)
     run("U1", "U0")
-    back_first_sum, back_attn, first_sums = first_norm_back(
-        first_sum, back_part, swap_cores(back_part, tensor_count), back_second, row(first_gain)
-    )
-    order.ran(back_attn)
-    run("D1", "D0")
+    normed_back = []
+    for at, pair in enumerate(exchanged(back_parts)):
+        pair = order.after(pair)
+        normed_back.append(
+            call(
+                first_norm_kernel,
+                [(half_shape, exact), (half_shape, low), ((8, model), exact)],
+                (),
+                (first_sums[at], *pair, back_seconds[at], row(first_gain)),
+                "first_norm_back",
+            )
+        )
+        order.ran(normed_back[-1][1])
+        if at == 0:
+            run("D1", "D0")
+    back_first_sums, back_attns, norm_sums = zip(*normed_back, strict=True)
     small = jnp.concatenate(
         [
             jnp.zeros((1, model), jnp.float32),
-            up_sums[0].reshape(-1, model),
-            first_sums[:3],
-            second_sums[:3],
+            (up_sums[0] + up_sums[1])[0].reshape(-1, model),
+            (norm_sums[0] + norm_sums[1])[:3],
+            (second_sums[0] + second_sums[1])[:3],
         ]
     )
     small = jnp.pad(small, ((0, -small.shape[0] % 32), (0, 0)))
-    [back_attn] = order.after((back_attn,))
-    *attn_halves, input_part = attend_back(
+    back_attn = order.after(back_attns)
+    *attn_halves, low_part, high_part = attend_back(
         seq_lengths,
         bits,
-        back_attn,
-        out_weight,
-        queries,
-        keys,
-        values,
-        totals,
-        tokens_in,
-        context,
-        q_weight,
-        k_weight,
-        v_weight,
-        small,
-    )
-    order.ran(input_part)
+        (*back_attn, out_weight, queries, keys, values, totals, tokens_in, context)
+        + (q_weight, k_weight, v_weight, small),
+        rows,
+        model,
+        width,
+        small.shape[0],
+    )
+    order.ran(low_part)
     begin("A", attn_halves)
     run("A1", "U1", "D0", "D1", "U0", "A0")
-    input_part, input_other = order.after((input_part, swap_cores(input_part, tensor_count)))
-    grad_input = ((input_part + input_other) + back_first_sum).astype(jnp.bfloat16)
+    pairs = exchanged((low_part, high_part))
+    first = order.after(pairs[0])
+    [grad_input] = call(
+        input_kernel,
+        [((rows, model), low)],
+        (),
+        (*first, back_first_sums[0], *pairs[1], back_first_sums[1]),
+        "grad_input",
+    )
     order.ran(grad_input)
+    [layer_out] = call(joined_kernel, [((rows, model), low)], (), outs, "layer_out")
     run("U1", "D0", "A1", "D1", "D0", "U0", "A0", "U1", "D1", "D0", "A1", "U0", "A0", "U1", "D1")
     run("A1", "D0", "U0", "U1", "D1", "A0", "A1", "U0", "A0", "A1")
 

time: 991 us -> 362 us (0.37)
  Pallas kernels: 768 us -> 96.2 us
  waiting for transfers between devices: 91.1 us -> 132 us
  local copies, waits for them, and re-layouts: 20.3 us -> 36.5 us
  other arithmetic: 35.7 us -> 22.2 us
    pallas_call x9, Pallas kernels: 664 us -> 13.3 us  [place_blocks(): pl.pallas_call(functools.partial(place_kernel, moves), out_shape=tuple((s...]
    ppermute x24, waiting for transfers between devices: 67.1 us -> 95.4 us  [swap(): lax.ppermute(value, 'dp', [(i, i ^ 1 << bit) for i in range(self.count)])]
    pallas_call x6 -> x14, Pallas kernels: 104 us -> 82.9 us  [call(): pl.pallas_call(body, out_shape=tuple((struct(*out) for out in outs)), in_...]
    unnamed x50 -> x150, local copies, waits for them, and re-layouts: 7.28 us -> 27.9 us
    ppermute x6, waiting for transfers between devices: 13 us -> 32.3 us  [advance(): self.arriving = lax.ppermute(value, 'dp', ring.outward)]
  transfers between devices with their start and end apart: 46 -> 58, of which waited for: 14 -> 19; matrix products, arithmetic and copies ran while one was open for 4% -> 7% of each run, Pallas kernels for 53% -> 17%
where the time goes in v4:
time: 362 us; the launch traced here: 358 us
  waiting for transfers between devices  132 us (36%)
  Pallas kernels  96.2 us (27%)
  starting transfers between devices  68.7 us (19%)
  local copies, waits for them, and re-layouts  36.5 us (10%)
  other arithmetic  22.2 us (6%)
    ppermute x24, waiting for transfers between devices, swap(): lax.ppermute(value, 'dp', [(i, i ^ 1 << bit) for i in range(self.count)])  95.4 us
    pallas_call x14, Pallas kernels, call(): pl.pallas_call(body, out_shape=tuple((struct(*out) for out in outs)), in_...  82.9 us
    ppermute x6, waiting for transfers between devices, advance(): self.arriving = lax.ppermute(value, 'dp', ring.outward)  32.3 us
    ppermute x24, starting transfers between devices, swap(): lax.ppermute(value, 'dp', [(i, i ^ 1 << bit) for i in range(self.count)])  29.9 us
    unnamed x150, local copies, waits for them, and re-layouts  27.9 us
    ppermute x6, starting transfers between devices, advance(): self.arriving = lax.ppermute(value, 'dp', ring.inward)  21.3 us
    pallas_call x9, Pallas kernels, place_blocks(): pl.pallas_call(functools.partial(place_kernel, moves), out_shape=tuple((s...  13.3 us
    add x12, other arithmetic, advance(): value = value + arrived  8.35 us
  transfers between devices with their start and end apart: 58, of which 19 were waited for; matrix products, arithmetic and copies ran while one was open for 7% of the time, Pallas kernels for 17%

profile of v4, /device:TPU:0, one launch (start us, length us, event | category | flops | bytes accessed | tf_op | source)
XLA Modules:
  0.0 357.7 jit_solution(3711609347865721394)
XLA Ops:
  8.3 20.4 %attend.1 = (bf16[1024,384]{1,0:T(8,128)(2,1)S(1)}, bf16[1024,384]{1,0:T(8,128)(2,1)S(1)}, bf16[1024,384]{1,0:T(8,128)(2,1)S(1)}, bf16[1024,384]{1,0:T(8,128)(2,...) custom-call(s32[1,4]{1,0:T(1,128)S(1)} %copy-done.63, ...), custom_call_target="tpu_custom_call" | custom-call | tf_op jit(solution)/shard_map/attend/pallas_call | solution.py:487
  53.2 3.6 second_norm.3
  58.9 3.6 second_norm.2
  63.6 4.4 %grad_down.1 = (f32[384,768]{1,0:T(8,128)}, f32[384,768]{1,0:T(8,128)S(1)}, f32[384,768]{1,0:T(8,128)}, f32[384,768]{1,0:T(8,128)S(1)}) custom-call(s32[1,2]{1,0:T(1,128)S(1)} %add_bitcast_fusion.bits_ref.starts_ref, bf16[512,1536]{1,0:T(8,128)(2,1)S(1)} %copy-done.38, bf16[512,1536]{1,0:T(8,128)(2,1)S(1)} %copy-done.34, ...), custom_call_target="tpu_custom_call" | custom-call | tf_op jit(solution)/shard_map/grad_down/pallas_call | solution.py:487
  69.0 4.3 %feed_back.2 = (f32[512,768]{1,0:T(8,128)S(1)}, bf16[512,1536]{1,0:T(8,128)(2,1)S(1)}, f32[8,1536]{1,0:T(8,128)S(1)}) custom-call(bf16[512,768]{1,0:T(8,128)(2,1)S(1)} %get-tuple-element.188.back_low_ref.back_down_ref, bf16[512,768]{1,0:T(8,128)(2,1)S(1)} %copy-done.23, bf16[768,1536]{1,0:T(8,128)(2,1)S(1)} %copy-done, ...), custom_call_target="tpu_custom_call" | custom-call | tf_op jit(solution)/shard_map/feed_back/pallas_call | solution.py:487
  75.7 4.0 %collective-permute-start.13 = (f32[384,768]{1,0:T(8,128)}, f32[384,768]{1,0:T(8,128)}, u32[]{:S(2)}, u32[]{:S(2)}) collective-permute-start(f32[384,768]{1,0:T(8,128)} %get-tuple-element.205), channel_id=1, source_target_pairs={{0,4},{2,6},{4,0},{6,2},{8,12},{10,14},{12,8},{14,10},{16,20},{18,... | collective-permute-start | bytes 3538952 | tf_op jit(solution)/shard_map/ppermute | solution.py:603
  81.2 4.3 %feed_back.3 = (f32[512,768]{1,0:T(8,128)S(1)}, bf16[512,1536]{1,0:T(8,128)(2,1)S(1)}, f32[8,1536]{1,0:T(8,128)S(1)}) custom-call(bf16[512,768]{1,0:T(8,128)(2,1)S(1)} %get-tuple-element.193.back_high_ref.back_down_ref, bf16[512,768]{1,0:T(8,128)(2,1)S(1)} %get-tuple-element.191.first_low_ref.first_high_ref, bf16[768,1536]{1,0:T(8,128)(2,1)S(1)} %copy-done, ...), custom_call_target="tpu_custom_call" | custom-call | tf_op jit(solution)/shard_map/feed_back/pallas_call | solution.py:487
  90.8 3.4 grad_up.1
  98.5 8.0 %collective-permute-done.13 = f32[384,768]{1,0:T(8,128)} collective-permute-done((f32[384,768]{1,0:T(8,128)}, f32[384,768]{1,0:T(8,128)}, u32[]{:S(2)}, u32[]{:S(2)}) %collective-permute-start.13) | collective-permute-done | bytes 1179680 | tf_op jit(solution)/shard_map/ppermute | solution.py:603
  115.6 24.2 %attend_back.1 = (f32[384,768]{1,0:T(8,128)}, f32[384,768]{1,0:T(8,128)S(1)}, f32[400,768]{1,0:T(8,128)}, f32[400,768]{1,0:T(8,128)S(1)}, f32[512,768]{1,0:T(8,128)S(1)}, /*index=5*/f32[512,768]{1,0:T(8,128)S(1)}) custom-call(s32[1,4]{1,0:T(1,128)S(1)} %copy-done.64, s32[1,2]{1,0:T(1,128)S(1)} %add_bitcast_fusion.bits_ref.starts_ref, ...), custom_call_target="tpu_custom_call" | custom-call | tf_op jit(solution)/shard_map/attend_back/pallas_call | solution.py:487
  144.2 11.7 %collective-permute-done.18 = f32[192,768]{1,0:T(8,128)S(1)} collective-permute-done((f32[192,768]{1,0:T(8,128)S(1)}, f32[192,768]{1,0:T(8,128)S(1)}, u32[]{:S(2)}, u32[]{:S(2)}) %collective-permute-start.18) | collective-permute-done | bytes 589856 | tf_op jit(solution)/shard_map/ppermute | solution.py:603
  159.5 3.5 collective-permute-start.24
  179.6 9.6 %collective-permute-done.28 = f32[400,768]{1,0:T(8,128)} collective-permute-done((f32[400,768]{1,0:T(8,128)}, f32[400,768]{1,0:T(8,128)}, u32[]{:S(2)}, u32[]{:S(2)}) %collective-permute-start.28) | collective-permute-done | bytes 1228832 | tf_op jit(solution)/shard_map/ppermute | solution.py:603
  189.2 3.2 collective-permute-start.34
  205.1 5.3 %collective-permute-start.30 = (f32[192,768]{1,0:T(8,128)S(1)}, f32[192,768]{1,0:T(8,128)S(1)}, u32[]{:S(2)}, u32[]{:S(2)}) collective-permute-start(f32[192,768]{1,0:T(8,128)S(1)} %add_add_fusion.2), channel_id=1, source_target_pairs={{0,8},{24,16},{2,10},{26,18},{4,12},{28,20},{6,14},{30,22},{1,9},{... | collective-permute-start | bytes 1769480 | tf_op jit(solution)/shard_map/ppermute | solution.py:661
  219.7 4.6 %collective-permute-start.42 = (f32[200,768]{1,0:T(8,128)S(1)}, f32[200,768]{1,0:T(8,128)S(1)}, u32[]{:S(2)}, u32[]{:S(2)}) collective-permute-start(f32[200,768]{1,0:T(8,128)S(1)} %add_add_fusion), channel_id=1, source_target_pairs={{0,8},{24,16},{2,10},{26,18},{4,12},{28,20},{6,14},{30,22},{1,9},{... | collective-permute-start | bytes 1843208 | tf_op jit(solution)/shard_map/ppermute | solution.py:661
  227.8 7.5 %collective-permute-done.36 = f32[192,768]{1,0:T(8,128)S(1)} collective-permute-done((f32[192,768]{1,0:T(8,128)S(1)}, f32[192,768]{1,0:T(8,128)S(1)}, u32[]{:S(2)}, u32[]{:S(2)}) %collective-permute-start.36) | collective-permute-done | bytes 589856 | tf_op jit(solution)/shard_map/ppermute | solution.py:669
  245.7 5.4 %collective-permute-done.38.refs_1_ = f32[192,768]{1,0:T(8,128)S(1)} collective-permute-done((f32[192,768]{1,0:T(8,128)S(1)}, f32[192,768]{1,0:T(8,128)S(1)}, u32[]{:S(2)}, u32[]{:S(2)}) %collective-permute-start.38) | collective-permute-done | bytes 589856 | tf_op jit(solution)/shard_map/ppermute | solution.py:603
  254.2 8.3 %collective-permute-done.44 = f32[192,768]{1,0:T(8,128)S(1)} collective-permute-done((f32[192,768]{1,0:T(8,128)S(1)}, f32[192,768]{1,0:T(8,128)S(1)}, u32[]{:S(2)}, u32[]{:S(2)}) %collective-permute-start.44) | collective-permute-done | bytes 589856 | tf_op jit(solution)/shard_map/ppermute | solution.py:669
  265.3 10.4 %collective-permute-done.48 = f32[200,768]{1,0:T(8,128)S(1)} collective-permute-done((f32[200,768]{1,0:T(8,128)S(1)}, f32[200,768]{1,0:T(8,128)S(1)}, u32[]{:S(2)}, u32[]{:S(2)}) %collective-permute-start.48) | collective-permute-done | bytes 614432 | tf_op jit(solution)/shard_map/ppermute | solution.py:669
  279.9 4.0 %collective-permute-done.46 = f32[192,768]{1,0:T(8,128)S(1)} collective-permute-done((f32[192,768]{1,0:T(8,128)S(1)}, f32[192,768]{1,0:T(8,128)S(1)}, u32[]{:S(2)}, u32[]{:S(2)}) %collective-permute-start.46) | collective-permute-done | bytes 589856 | tf_op jit(solution)/shard_map/ppermute | solution.py:669
  284.4 4.6 %collective-permute-done.53.refs_1_ = f32[192,768]{1,0:T(8,128)S(1)} collective-permute-done((f32[192,768]{1,0:T(8,128)S(1)}, f32[192,768]{1,0:T(8,128)S(1)}, u32[]{:S(2)}, u32[]{:S(2)}) %collective-permute-start.53) | collective-permute-done | bytes 589856 | tf_op jit(solution)/shard_map/ppermute | solution.py:603
  290.7 6.3 %collective-permute-done.51.refs_1_ = f32[200,768]{1,0:T(8,128)S(1)} collective-permute-done((f32[200,768]{1,0:T(8,128)S(1)}, f32[200,768]{1,0:T(8,128)S(1)}, u32[]{:S(2)}, u32[]{:S(2)}) %collective-permute-start.51) | collective-permute-done | bytes 614432 | tf_op jit(solution)/shard_map/ppermute | solution.py:603
  304.8 45.0 %collective-permute-done.56.refs_3_ = f32[384,768]{1,0:T(8,128)S(1)} collective-permute-done((f32[384,768]{1,0:T(8,128)S(1)}, f32[384,768]{1,0:T(8,128)S(1)}, u32[]{:S(2)}, u32[]{:S(2)}) %collective-permute-start.56) | collective-permute-done | bytes 1179680 | tf_op jit(solution)/shard_map/ppermute | solution.py:603
  (324 shorter events, 146.1 us)
Async XLA Ops:
  75.7 30.8 %collective-permute-start.13 = (f32[384,768]{1,0:T(8,128)}, f32[384,768]{1,0:T(8,128)}, u32[]{:S(2)}, u32[]{:S(2)}) collective-permute-start(f32[384,768]{1,0:T(8,128)} %get-tuple-element.205), channel_id=1, source_target_pairs={{0,4},{2,6},{4,0},{6,2},{8,12},{10,14},{12,8},{14,10},{16,20},{18,... | collective-permute-start | bytes 3538952 | tf_op jit(solution)/shard_map/ppermute | solution.py:603
  79.7 30.2 %collective-permute-start.12 = (f32[384,768]{1,0:T(8,128)}, f32[384,768]{1,0:T(8,128)}, u32[]{:S(2)}, u32[]{:S(2)}) collective-permute-start(f32[384,768]{1,0:T(8,128)} %get-tuple-element.187), channel_id=1, source_target_pairs={{0,2},{2,0},{4,6},{6,4},{8,10},{10,8},{12,14},{14,12},{16,18},{18,... | collective-permute-start | bytes 3538952 | tf_op jit(solution)/shard_map/ppermute | solution.py:603
  87.9 23.6 %collective-permute-start.10 = (f32[256,768]{1,0:T(8,128)}, f32[256,768]{1,0:T(8,128)}, u32[]{:S(2)}, u32[]{:S(2)}) collective-permute-start(f32[256,768]{1,0:T(8,128)} %get-tuple-element.346), channel_id=1, source_target_pairs={{0,1},{1,0},{2,3},{3,2},{4,5},{5,4},{6,7},{7,6},{8,9},{9,8},{10,11... | collective-permute-start | bytes 2359304 | tf_op jit(solution)/shard_map/ppermute | solution.py:585
  89.3 22.2 %collective-permute-start.11 = (f32[256,768]{1,0:T(8,128)}, f32[256,768]{1,0:T(8,128)}, u32[]{:S(2)}, u32[]{:S(2)}) collective-permute-start(f32[256,768]{1,0:T(8,128)} %get-tuple-element.345), channel_id=1, source_target_pairs={{0,1},{1,0},{2,3},{3,2},{4,5},{5,4},{6,7},{7,6},{8,9},{9,8},{10,11... | collective-permute-start | bytes 2359304 | tf_op jit(solution)/shard_map/ppermute | solution.py:585
  94.3 49.3 %collective-permute-start.16 = (f32[384,768]{1,0:T(8,128)S(1)}, f32[384,768]{1,0:T(8,128)S(1)}, u32[]{:S(2)}, u32[]{:S(2)}) collective-permute-start(f32[384,768]{1,0:T(8,128)S(1)} %get-tuple-element.196), channel_id=1, source_target_pairs={{0,2},{2,0},{4,6},{6,4},{8,10},{10,8},{12,14},{14,12},{16,18},{18,... | collective-permute-start | bytes 3538952 | tf_op jit(solution)/shard_map/ppermute | solution.py:603
  106.5 37.0 %collective-permute-start.19 = (f32[384,768]{1,0:T(8,128)S(1)}, f32[384,768]{1,0:T(8,128)S(1)}, u32[]{:S(2)}, u32[]{:S(2)}) collective-permute-start(f32[384,768]{1,0:T(8,128)S(1)} %get-tuple-element.231), channel_id=1, source_target_pairs={{0,4},{2,6},{4,0},{6,2},{8,12},{10,14},{12,8},{14,10},{16,20},{18,... | collective-permute-start | bytes 3538952 | tf_op jit(solution)/shard_map/ppermute | solution.py:603
  143.6 21.7 %collective-permute-start.20 = (f32[256,768]{1,0:T(8,128)S(1)}, f32[256,768]{1,0:T(8,128)S(1)}, u32[]{:S(2)}, u32[]{:S(2)}) collective-permute-start(f32[256,768]{1,0:T(8,128)S(1)} %get-tuple-element.342), channel_id=1, source_target_pairs={{0,1},{1,0},{2,3},{3,2},{4,5},{5,4},{6,7},{7,6},{8,9},{9,8},{10,11... | collective-permute-start | bytes 2359304 | tf_op jit(solution)/shard_map/ppermute | solution.py:585
  158.9 30.3 %collective-permute-start.28 = (f32[400,768]{1,0:T(8,128)}, f32[400,768]{1,0:T(8,128)}, u32[]{:S(2)}, u32[]{:S(2)}) collective-permute-start(f32[400,768]{1,0:T(8,128)} %get-tuple-element.256), channel_id=1, source_target_pairs={{0,4},{2,6},{4,0},{6,2},{8,12},{10,14},{12,8},{14,10},{16,20},{18,... | collective-permute-start | bytes 3686408 | tf_op jit(solution)/shard_map/ppermute | solution.py:603
  165.3 39.8 %collective-permute-start.22 = (f32[384,768]{1,0:T(8,128)}, f32[384,768]{1,0:T(8,128)}, u32[]{:S(2)}, u32[]{:S(2)}) collective-permute-start(f32[384,768]{1,0:T(8,128)} %get-tuple-element.249), channel_id=1, source_target_pairs={{0,2},{2,0},{4,6},{6,4},{8,10},{10,8},{12,14},{14,12},{16,18},{18,... | collective-permute-start | bytes 3538952 | tf_op jit(solution)/shard_map/ppermute | solution.py:603
  167.0 27.9 %collective-permute-start.27 = (f32[192,768]{1,0:T(8,128)}, f32[192,768]{1,0:T(8,128)}, u32[]{:S(2)}, u32[]{:S(2)}) collective-permute-start(f32[192,768]{1,0:T(8,128)} %add_add_fusion.4), channel_id=1, source_target_pairs={{0,8},{24,16},{2,10},{26,18},{4,12},{28,20},{6,14},{30,22},{1,9},{... | collective-permute-start | bytes 1769480 | tf_op jit(solution)/shard_map/ppermute | solution.py:661
  177.7 21.0 %collective-permute-start.26 = (f32[192,768]{1,0:T(8,128)}, f32[192,768]{1,0:T(8,128)}, u32[]{:S(2)}, u32[]{:S(2)}) collective-permute-start(f32[192,768]{1,0:T(8,128)} %add.155), channel_id=1, source_target_pairs={{8,16},{16,8},{10,18},{18,10},{12,20},{20,12},{14,22},{22,14},{9,1... | collective-permute-start | bytes 1769480 | tf_op jit(solution)/shard_map/ppermute | solution.py:666
  179.2 22.9 %collective-permute-start.23 = (f32[192,768]{1,0:T(8,128)}, f32[192,768]{1,0:T(8,128)}, u32[]{:S(2)}, u32[]{:S(2)}) collective-permute-start(f32[192,768]{1,0:T(8,128)} %get-tuple-element.367), channel_id=1, source_target_pairs={{0,4},{2,6},{4,0},{6,2},{8,12},{10,14},{12,8},{14,10},{16,20},{18,... | collective-permute-start | bytes 1769480 | tf_op jit(solution)/shard_map/ppermute | solution.py:603
  189.2 22.7 %collective-permute-start.34 = (f32[192,768]{1,0:T(8,128)}, f32[192,768]{1,0:T(8,128)}, u32[]{:S(2)}, u32[]{:S(2)}) collective-permute-start(f32[192,768]{1,0:T(8,128)} %add_add_fusion.3), channel_id=1, source_target_pairs={{0,8},{24,16},{2,10},{26,18},{4,12},{28,20},{6,14},{30,22},{1,9},{... | collective-permute-start | bytes 1769480 | tf_op jit(solution)/shard_map/ppermute | solution.py:661
  205.1 19.2 %collective-permute-start.30 = (f32[192,768]{1,0:T(8,128)S(1)}, f32[192,768]{1,0:T(8,128)S(1)}, u32[]{:S(2)}, u32[]{:S(2)}) collective-permute-start(f32[192,768]{1,0:T(8,128)S(1)} %add_add_fusion.2), channel_id=1, source_target_pairs={{0,8},{24,16},{2,10},{26,18},{4,12},{28,20},{6,14},{30,22},{1,9},{... | collective-permute-start | bytes 1769480 | tf_op jit(solution)/shard_map/ppermute | solution.py:661
  240.8 36.3 %collective-permute-start.47 = (f32[384,768]{1,0:T(8,128)S(1)}, f32[384,768]{1,0:T(8,128)S(1)}, u32[]{:S(2)}, u32[]{:S(2)}) collective-permute-start(f32[384,768]{1,0:T(8,128)S(1)} %join.6.refs_0_), channel_id=1, source_target_pairs={{0,2},{2,0},{4,6},{6,4},{8,10},{10,8},{12,14},{14,12},{16,18},{18,... | collective-permute-start | bytes 3538952 | tf_op jit(solution)/shard_map/ppermute | solution.py:603
  251.9 23.8 %collective-permute-start.49 = (f32[384,768]{1,0:T(8,128)S(1)}, f32[384,768]{1,0:T(8,128)S(1)}, u32[]{:S(2)}, u32[]{:S(2)}) collective-permute-start(f32[384,768]{1,0:T(8,128)S(1)} %join.7.refs_2_), channel_id=1, source_target_pairs={{0,4},{2,6},{4,0},{6,2},{8,12},{10,14},{12,8},{14,10},{16,20},{18,... | collective-permute-start | bytes 3538952 | tf_op jit(solution)/shard_map/ppermute | solution.py:603
  252.9 22.7 %collective-permute-start.48 = (f32[200,768]{1,0:T(8,128)S(1)}, f32[200,768]{1,0:T(8,128)S(1)}, u32[]{:S(2)}, u32[]{:S(2)}) collective-permute-start(f32[200,768]{1,0:T(8,128)S(1)} %add.175), channel_id=1, source_target_pairs={{8,0},{16,24},{10,2},{18,26},{12,4},{20,28},{14,6},{22,30},{9,1},{... | collective-permute-start | bytes 1843208 | tf_op jit(solution)/shard_map/ppermute | solution.py:669
  262.7 21.2 %collective-permute-start.46 = (f32[192,768]{1,0:T(8,128)S(1)}, f32[192,768]{1,0:T(8,128)S(1)}, u32[]{:S(2)}, u32[]{:S(2)}) collective-permute-start(f32[192,768]{1,0:T(8,128)S(1)} %add.176), channel_id=1, source_target_pairs={{8,0},{16,24},{10,2},{18,26},{12,4},{20,28},{14,6},{22,30},{9,1},{... | collective-permute-start | bytes 1769480 | tf_op jit(solution)/shard_map/ppermute | solution.py:669
  264.0 25.1 %collective-permute-start.53 = (f32[192,768]{1,0:T(8,128)S(1)}, f32[192,768]{1,0:T(8,128)S(1)}, u32[]{:S(2)}, u32[]{:S(2)}) collective-permute-start(f32[192,768]{1,0:T(8,128)S(1)} %broadcast_select_fusion.3.refs_0_), channel_id=1, source_target_pairs={{0,2},{2,0},{4,6},{6,4},{8,10},{10,8},{12,14},{14,12},{16,18},{18,... | collective-permute-start | bytes 1769480 | tf_op jit(solution)/shard_map/ppermute | solution.py:603
  275.8 21.2 %collective-permute-start.51 = (f32[200,768]{1,0:T(8,128)S(1)}, f32[200,768]{1,0:T(8,128)S(1)}, u32[]{:S(2)}, u32[]{:S(2)}) collective-permute-start(f32[200,768]{1,0:T(8,128)S(1)} %broadcast_select_fusion.refs_0_), channel_id=1, source_target_pairs={{0,2},{2,0},{4,6},{6,4},{8,10},{10,8},{12,14},{14,12},{16,18},{18,... | collective-permute-start | bytes 1843208 | tf_op jit(solution)/shard_map/ppermute | solution.py:603
  297.9 54.7 %collective-permute-start.57 = (f32[400,768]{1,0:T(8,128)S(1)}, f32[400,768]{1,0:T(8,128)S(1)}, u32[]{:S(2)}, u32[]{:S(2)}) collective-permute-start(f32[400,768]{1,0:T(8,128)S(1)} %join.10.refs_2_), channel_id=1, source_target_pairs={{0,4},{2,6},{4,0},{6,2},{8,12},{10,14},{12,8},{14,10},{16,20},{18,... | collective-permute-start | bytes 3686408 | tf_op jit(solution)/shard_map/ppermute | solution.py:603
  298.0 51.8 %collective-permute-start.56 = (f32[384,768]{1,0:T(8,128)S(1)}, f32[384,768]{1,0:T(8,128)S(1)}, u32[]{:S(2)}, u32[]{:S(2)}) collective-permute-start(f32[384,768]{1,0:T(8,128)S(1)} %join.8.refs_2_), channel_id=1, source_target_pairs={{0,4},{2,6},{4,0},{6,2},{8,12},{10,14},{12,8},{14,10},{16,20},{18,... | collective-permute-start | bytes 3538952 | tf_op jit(solution)/shard_map/ppermute | solution.py:603
  300.0 49.8 %collective-permute-start.55 = (f32[384,768]{1,0:T(8,128)S(1)}, f32[384,768]{1,0:T(8,128)S(1)}, u32[]{:S(2)}, u32[]{:S(2)}) collective-permute-start(f32[384,768]{1,0:T(8,128)S(1)} %join.9.refs_0_), channel_id=1, source_target_pairs={{0,2},{2,0},{4,6},{6,4},{8,10},{10,8},{12,14},{14,12},{16,18},{18,... | collective-permute-start | bytes 3538952 | tf_op jit(solution)/shard_map/ppermute | solution.py:603
  302.2 50.3 %collective-permute-start.54 = (f32[384,768]{1,0:T(8,128)S(1)}, f32[384,768]{1,0:T(8,128)S(1)}, u32[]{:S(2)}, u32[]{:S(2)}) collective-permute-start(f32[384,768]{1,0:T(8,128)S(1)} %join.11.refs_0_), channel_id=1, source_target_pairs={{0,2},{2,0},{4,6},{6,4},{8,10},{10,8},{12,14},{14,12},{16,18},{18,... | collective-permute-start | bytes 3538952 | tf_op jit(solution)/shard_map/ppermute | solution.py:603
  (109 other events, 680.4 us)
